TPU v7x, 256 devices: a whole 4x4x8 slice. The times are simulated.
256 devices in a mesh: tensor: 32 (over z, x), adapter: 8 (over y, core).
Axes of the slice: x: 4, y: 4, z: 8, core: 2. Of those that a mesh axis runs over, the one named last changes fastest.
Arguments:
- tokens: bfloat16 [4096, 2880], P(('adapter', 'tensor')), may hold values from -6 to 6
- gain_attention: float32 [2880], replicated, may hold values from 0.1 to 1.9
- query_weight: bfloat16 [2880, 4096], P(None, 'tensor'), may hold values from -0.109375 to 0.109375
- keyval_weight: bfloat16 [2880, 2, 64, 8], P(None, None, 'tensor'), may hold values from -0.109375 to 0.109375
- output_weight: bfloat16 [4096, 2880], P('tensor'), may hold values from -0.09375 to 0.09375
- sink_logits: float32 [64], P('tensor'), may hold values from -1 to 2
- heads_down: bfloat16 [64, 48, 2880], P('adapter'), may hold values from -0.109375 to 0.109375
- query_up: bfloat16 [64, 16, 4096], P(None, None, 'tensor'), may hold values from -1.5 to 1.5
- keyval_up: bfloat16 [64, 2, 16, 64, 8], P(None, None, None, 'tensor'), may hold values from -1.5 to 1.5
- output_down: bfloat16 [64, 16, 4096], P(None, None, 'tensor'), may hold values from -0.09375 to 0.09375
- output_up: bfloat16 [64, 16, 2880], P('tensor'), may hold values from -1.5 to 1.5
- gain_mixture: float32 [2880], replicated, may hold values from 0.1 to 1.9
- gate_up_weight: bfloat16 [2880, 2, 11520], P(None, None, 'tensor'), may hold values from -0.109375 to 0.109375
- down_weight: bfloat16 [11520, 2880], P('tensor'), may hold values from -0.109375 to 0.109375
- mixture_down: bfloat16 [64, 16, 2880], P('adapter'), may hold values from -0.109375 to 0.109375
- mixture_up: bfloat16 [64, 16, 2880], P('tensor'), may hold values from -1.5 to 1.5
- lengths: int32 [8, 8], replicated, may hold values from 1 to 256, 512 in all within a row
- prompt_adapter: int32 [8, 8], replicated, may hold values from 0 to 63
- adapter_slot: int32 [64], replicated, may hold values from 0 to 63, each once
- expert_ids: int32 [4096, 4], P('adapter'), may hold values from 0 to 31, all different within a row; in each aligned block of 512 rows (0 to 511, 512 to 1023, ...) at most 128 rows name the same one
- expert_weights: float32 [4096, 4], P('adapter'), may hold values from 0.05 to 0.5
Outputs:
- layer_out: bfloat16 [4096, 2880], P(('adapter', 'tensor'))
Inputs may be any that keep to these rules, and one draw needn't show every extreme that they name: `expert_ids`: in each group of 512 tokens no expert is named by more than 128 tokens.
All inputs are finite; a program needn't handle non-finite values.
Results may differ from a plain program's by a relative error of at most 0.02.
Values may be sent and summed in bfloat16 or wider, within the bound.
A program may use at most 128 MiB of HBM per device.

v0:
```python
import math

import jax
import jax.numpy as jnp
from jax import lax
from jax.sharding import PartitionSpec as P

QH = 64
KVH = 8
HD = 64
FF = 2880
WINDOW = 128
TOP = 4
ROUTED = 32
R = 16


NORM_EPS = 1e-05
ROPE_BASE = 150000.0
SWIGLU_ALPHA = 1.702


def token_tables(length_row, adapter_row, first_row, row_count):
    prompt_ends = jnp.cumsum(length_row)
    prompt_starts = prompt_ends - length_row
    token_index = first_row + jnp.arange(row_count, dtype=jnp.int32)
    member = (token_index[:, None] >= prompt_starts[None, :]) & (
        token_index[:, None] < prompt_ends[None, :]
    )
    prompt_index = jnp.arange(length_row.shape[0], dtype=jnp.int32)
    segment = jnp.sum(jnp.where(member, prompt_index[None, :], 0), axis=1)
    prompt_begin = jnp.sum(jnp.where(member, prompt_starts[None, :], 0), axis=1)
    adapter = jnp.sum(jnp.where(member, adapter_row[None, :], 0), axis=1)
    return (segment, token_index - prompt_begin, adapter)


def settle(values):
    return lax.optimization_barrier(values.astype(jnp.bfloat16)).astype(jnp.float32)


def rms_scale(row_block, gain):
    wide = row_block.astype(jnp.float32)
    mean_square = jnp.mean(wide * wide, axis=-1, keepdims=True)
    return (wide * lax.rsqrt(mean_square + NORM_EPS) * gain).astype(jnp.bfloat16)


def rotate(head_rows, position):
    half_width = head_rows.shape[-1] // 2
    freqs = jnp.exp(-math.log(ROPE_BASE) * jnp.arange(half_width, dtype=jnp.float32) / half_width)
    angles = position.astype(jnp.float32)[:, None] * freqs[None, :]
    cosine = jnp.cos(angles)[:, None, :]
    sine_val = jnp.sin(angles)[:, None, :]
    first_half = head_rows[..., :half_width]
    second_half = head_rows[..., half_width:]
    return jnp.concatenate(
        [
            first_half * cosine - second_half * sine_val,
            second_half * cosine + first_half * sine_val,
        ],
        axis=-1,
    )


def spread_rank(onehot, rank_rows):
    return (onehot[:, :, None] * rank_rows[:, None, :]).reshape(rank_rows.shape[0], -1)


def attend(queries, key_rows, value_rows, segment, sink_logits):
    row_count = queries.shape[0]
    block_rows = min(512, row_count)
    key_pad = jnp.pad(key_rows, ((WINDOW, 0), (0, 0), (0, 0)))
    value_pad = jnp.pad(value_rows, ((WINDOW, 0), (0, 0), (0, 0)))
    segment_pad = jnp.pad(segment, (WINDOW, 0), constant_values=-1)
    sink_weight = jnp.exp(sink_logits)[:, None]
    score_scale = queries.shape[-1] ** (-0.5)

    def one_block(block_start):
        row_pos = jnp.arange(block_rows, dtype=jnp.int32)[:, None] + WINDOW
        col_pos = jnp.arange(block_rows + WINDOW, dtype=jnp.int32)[None, :]
        allowed = (
            (segment[:, None] == segment_pad[None, :])
            & (col_pos <= row_pos)
            & (row_pos - col_pos < WINDOW)
        )
        scores = (
            jnp.einsum("qhd,khd->hqk", queries, key_pad, preferred_element_type=jnp.float32)
            * score_scale
        )
        weights = jnp.where(allowed[None], jnp.exp(scores), 0.0)
        denominator = sink_weight + jnp.sum(weights, axis=-1)
        weights_bf = (weights / denominator[..., None]).astype(jnp.bfloat16)
        mixed_block = jnp.einsum(
            "hqk,khd->qhd", weights_bf, value_pad, preferred_element_type=jnp.float32
        )
        return mixed_block.astype(jnp.bfloat16).reshape(block_rows, -1)

    block_starts = jnp.arange(row_count // block_rows, dtype=jnp.int32) * block_rows
    return lax.map(one_block, block_starts).reshape(row_count, -1)


def swap_owner(outgoing):
    return lax.all_to_all(outgoing, "adapter", split_axis=0, concat_axis=0, tiled=True)


def gather_tokens(row_block):
    return lax.all_gather(row_block, "tensor", axis=0, tiled=True)


def tensor_total(partial_value):
    return lax.psum(partial_value.astype(jnp.bfloat16), "tensor").astype(jnp.float32)


def partial_sum(term_maker, own_rows):
    return lax.psum_scatter(
        term_maker(jnp.int32(0), lax.axis_size("tensor") * own_rows).astype(jnp.bfloat16),
        "tensor",
        scatter_dimension=0,
        tiled=True,
    ).astype(jnp.float32)


def ask_owners(normed_own, bank, lengths, prompt_adapter, adapter_slot):
    own_rows = normed_own.shape[0]
    owner_count = lax.axis_size("adapter")
    owner_here = lax.axis_index("adapter")
    first_row = lax.axis_index("tensor") * own_rows
    stored, rank_width, width_d = bank.shape
    adapter_count = adapter_slot.shape[0]
    adapter_ids = jnp.arange(adapter_count, dtype=jnp.int32)

    def slots_of(length_row, adapter_row):
        adapter = token_tables(length_row, adapter_row, first_row, own_rows)[2]
        return jnp.sum(
            jnp.where(adapter[:, None] == adapter_ids[None, :], adapter_slot[None, :], 0), axis=1
        )

    all_slots = jax.vmap(slots_of)(lengths, prompt_adapter)
    own_slots = lax.dynamic_index_in_dim(all_slots, owner_here, 0, keepdims=False)
    route_mask = (own_slots // stored)[None, :] == jnp.arange(owner_count, dtype=jnp.int32)[:, None]
    outgoing = jnp.where(
        route_mask[:, :, None], normed_own[None, :, :], jnp.zeros((), jnp.bfloat16)
    )
    incoming = swap_owner(outgoing)
    local_slot = all_slots - owner_here * stored
    pick_hot = (
        local_slot[:, :, None] == jnp.arange(stored, dtype=jnp.int32)[None, None, :]
    ).astype(jnp.float32)
    flat_rows = incoming.reshape(owner_count * own_rows, width_d)
    projected = lax.dot_general(
        flat_rows,
        bank.reshape(stored * rank_width, width_d),
        (((1,), (1,)), ((), ())),
        preferred_element_type=jnp.float32,
    )
    projected = projected.reshape(owner_count, own_rows, stored, rank_width)
    answer = jnp.sum(projected * pick_hot[..., None], axis=2).astype(jnp.bfloat16)
    returned = swap_owner(answer.reshape(owner_count, own_rows * rank_width))
    return jnp.sum(
        returned.reshape(owner_count, own_rows, rank_width).astype(jnp.float32), axis=0
    ).astype(jnp.bfloat16)


def per_device(
    tokens,
    gain_attention,
    query_weight,
    keyval_weight,
    output_weight,
    sink_logits,
    heads_down,
    query_up,
    keyval_up,
    output_down,
    output_up,
    gain_mixture,
    gate_up_weight,
    down_weight,
    mixture_down,
    mixture_up,
    lengths,
    prompt_adapter,
    adapter_slot,
    expert_ids,
    expert_weights,
):
    own_rows = tokens.shape[0]
    tensor_here = lax.axis_index("tensor")
    group_here = lax.axis_index("adapter")
    group_rows = own_rows * lax.axis_size("tensor")
    adapter_count = adapter_slot.shape[0]
    query_cols = query_weight.shape[1]
    local_count = output_up.shape[0]
    slice_width = down_weight.shape[0]
    first_own = tensor_here * own_rows
    entries_here = keyval_weight.shape[2]
    length_row = lax.dynamic_index_in_dim(lengths, group_here, 0, keepdims=False)
    adapter_row = lax.dynamic_index_in_dim(prompt_adapter, group_here, 0, keepdims=False)
    segment, position, adapter = token_tables(length_row, adapter_row, jnp.int32(0), group_rows)
    adapter_hit = adapter[:, None] == jnp.arange(adapter_count, dtype=jnp.int32)[None, :]
    onehot = adapter_hit.astype(jnp.bfloat16)
    local_ids = tensor_here * local_count + jnp.arange(local_count, dtype=jnp.int32)
    local_hot = (adapter[:, None] == local_ids[None, :]).astype(jnp.bfloat16)
    normed_own = rms_scale(tokens, gain_attention)
    tokens_all = gather_tokens(tokens)
    normed = rms_scale(tokens_all, gain_attention)
    rank_own = ask_owners(normed_own, heads_down, lengths, prompt_adapter, adapter_slot)
    rank_qkv = gather_tokens(rank_own)
    queries = jnp.dot(normed, query_weight, preferred_element_type=jnp.float32)
    queries = queries + jnp.dot(
        spread_rank(onehot, rank_qkv[:, :R]),
        query_up.reshape(adapter_count * R, query_cols),
        preferred_element_type=jnp.float32,
    )
    queries = rotate(queries.reshape(group_rows, query_cols // HD, HD), position).astype(
        jnp.bfloat16
    )
    key_weight = keyval_weight[:, 0].reshape(keyval_weight.shape[0], entries_here * KVH)
    value_weight = keyval_weight[:, 1].reshape(keyval_weight.shape[0], entries_here * KVH)
    key_part = jnp.dot(normed, key_weight, preferred_element_type=jnp.float32)
    key_part = key_part + jnp.dot(
        spread_rank(onehot, rank_qkv[:, R : 2 * R]),
        keyval_up[:, 0].reshape(adapter_count * R, -1),
        preferred_element_type=jnp.float32,
    )
    value_part = jnp.dot(normed, value_weight, preferred_element_type=jnp.float32)
    value_part = value_part + jnp.dot(
        spread_rank(onehot, rank_qkv[:, 2 * R : 3 * R]),
        keyval_up[:, 1].reshape(adapter_count * R, -1),
        preferred_element_type=jnp.float32,
    )
    keyval_part = (
        jnp.stack([key_part, value_part], axis=1)
        .astype(jnp.bfloat16)
        .reshape(group_rows, 2, entries_here, KVH)
    )
    keyval_all = lax.all_gather(keyval_part, "tensor", axis=2, tiled=True)
    key_rows = rotate(
        jnp.transpose(keyval_all[:, 0].astype(jnp.float32), (0, 2, 1)), position
    ).astype(jnp.bfloat16)
    value_rows = jnp.transpose(keyval_all[:, 1], (0, 2, 1))
    heads_here = query_cols // HD
    head_map = (tensor_here * heads_here + jnp.arange(heads_here, dtype=jnp.int32)) // (QH // KVH)
    mixed_rows = attend(
        queries,
        jnp.take(key_rows, head_map, axis=1),
        jnp.take(value_rows, head_map, axis=1),
        segment,
        sink_logits,
    )
    rank_table = output_down.reshape(adapter_count * R, query_cols)
    rank_terms = lax.dot_general(
        mixed_rows, rank_table, (((1,), (1,)), ((), ())), preferred_element_type=jnp.float32
    )
    rank_terms = jnp.sum(
        rank_terms.reshape(group_rows, adapter_count, R) * onehot[:, :, None], axis=1
    )
    rank_out = tensor_total(settle(rank_terms)).astype(jnp.bfloat16)
    spread_out = spread_rank(local_hot, rank_out)
    up_out = output_up.reshape(local_count * R, -1)
    term = jnp.dot(mixed_rows, output_weight, preferred_element_type=jnp.float32)
    attn_all = tensor_total(
        settle(term + jnp.dot(spread_out, up_out, preferred_element_type=jnp.float32))
    )
    hidden_all = tokens_all.astype(jnp.float32) + attn_all
    normed_two = rms_scale(hidden_all, gain_mixture)
    hidden_own = lax.dynamic_slice_in_dim(hidden_all, first_own, own_rows, 0)
    normed_two_own = lax.dynamic_slice_in_dim(normed_two, first_own, own_rows, 0)
    rank_moe_own = ask_owners(normed_two_own, mixture_down, lengths, prompt_adapter, adapter_slot)
    rank_moe = gather_tokens(rank_moe_own)
    expert_here = tensor_here * slice_width // FF
    named = expert_ids == expert_here
    route_weight = jnp.sum(jnp.where(named, expert_weights, 0.0), axis=1)
    picked = jnp.any(named, axis=1)
    capacity = group_rows * TOP // ROUTED * 2
    order = jnp.cumsum(picked.astype(jnp.int32)) - 1
    target = jnp.where(picked, order, capacity)
    source = (
        jnp.zeros((capacity,), jnp.int32)
        .at[target]
        .set(jnp.arange(group_rows, dtype=jnp.int32), mode="drop")
    )
    slot_used = jnp.arange(capacity, dtype=jnp.int32) < jnp.sum(picked.astype(jnp.int32))
    compact_in = jnp.take(normed_two, source, axis=0)
    compact_route = jnp.where(slot_used, jnp.take(route_weight, source, axis=0), 0.0)
    gate_val = jnp.dot(compact_in, gate_up_weight[:, 0], preferred_element_type=jnp.float32)
    lift_val = jnp.dot(compact_in, gate_up_weight[:, 1], preferred_element_type=jnp.float32)
    active = (
        (lift_val + 1.0)
        * gate_val
        * jax.nn.sigmoid(SWIGLU_ALPHA * gate_val)
        * compact_route[:, None]
    ).astype(jnp.bfloat16)
    compact_terms = jnp.dot(active, down_weight, preferred_element_type=jnp.float32)
    spread_moe = spread_rank(local_hot, rank_moe)
    up_moe = mixture_up.reshape(local_count * R, -1)

    def moe_term(row_start, row_count):
        expert_rows = jnp.take(compact_terms, jnp.clip(order, 0, capacity - 1), axis=0)
        expert_rows = jnp.where(picked[:, None], expert_rows, 0.0)
        return settle(expert_rows + jnp.dot(spread_moe, up_moe, preferred_element_type=jnp.float32))

    moe_own = partial_sum(moe_term, own_rows)
    return (hidden_own + moe_own).astype(jnp.bfloat16)


def solution(mesh):
    in_specs = (
        P(("adapter", "tensor"), None),
        P(),
        P(None, "tensor"),
        P(None, None, "tensor", None),
        P("tensor", None),
        P("tensor"),
        P("adapter", None, None),
        P(None, None, "tensor"),
        P(None, None, None, "tensor", None),
        P(None, None, "tensor"),
        P("tensor", None, None),
        P(),
        P(None, None, "tensor"),
        P("tensor", None),
        P("adapter", None, None),
        P("tensor", None, None),
        P(),
        P(),
        P(),
        P("adapter", None),
        P("adapter", None),
    )
    out_specs = P(("adapter", "tensor"), None)
    return jax.shard_map(
        per_device, mesh=mesh, in_specs=in_specs, out_specs=out_specs, check_vma=False
    )
```

profile of v0, /device:TPU:8, one launch (start us, length us, event | category | flops | bytes accessed | tf_op | source)
XLA Modules:
  0.0 790.1 jit_solution(13386743152633411253)
XLA Ops:
  9.6 0.9 select_reduce_fusion
  10.6 1.0 fusion.54
  11.6 1.0 fusion.56
  12.6 1.0 broadcast_select_fusion.2
  13.6 5.6 all-to-all-start
  21.0 0.9 fusion.106
  21.9 8.7 %all-to-all-done = bf16[8,16,2880]{2,1,0:T(8,128)(2,1)S(1)} async-done(((bf16[8,16,2880]{2,1,0:T(8,128)(2,1)}), bf16[8,16,2880]{2,1,0:T(8,128)(2,1)S(1)}, u32[]{:S(2)}, u32[]{:S(2)}) %all-to-all-start) | async-done | bytes 737312 | tf_op jit(solution)/shard_map/all_to_all | solution.py:102
  30.6 1.5 fusion.20
  34.0 4.7 all-to-all-start.1
  39.8 2.8 all-to-all-done.1
  42.8 45.8 %all_gather.13 = bf16[512,48]{1,0:T(8,128)(2,1)S(1)} all-gather(bf16[16,48]{1,0:T(8,128)(2,1)S(1)} %reduce_sum.170), channel_id=1, replica_groups=mesh['tensor'=32,'adapter'=8] {'tensor'}, dimensions={0}, use_global_device_ids=true | all-gather | bytes 50688 | tf_op jit(solution)/shard_map/all_gather | solution.py:106
  88.9 1.5 broadcast_multiply_fusion.1
  90.4 1.8 all-gather.3.cloned.1.call-done
  92.2 2.7 fusion
  94.9 1.0 fusion.2
  95.9 0.9 fusion.69
  96.8 0.9 fusion.71
  99.8 1.2 fusion.15
  101.0 1.3 convolution_bitcast_fusion
  102.3 2.2 convolution_add_fusion
  104.6 68.5 %all-gather.5.cloned.1.call-done = bf16[512,2,64,8]{0,3,1,2:T(8,128)(2,1)} async-done(((bf16[512,2,2,8]{0,3,1,2:T(8,128)(2,1)}), bf16[512,2,64,8]{0,3,1,2:T(8,128)(2,1)}) %all-gather.5.cloned.1.call-update) | async-done | bytes 1048592 | tf_op jit(solution)/shard_map/all_gather | solution.py:236
  173.1 1.3 fusion.104
  176.2 1.0 fusion.7
  177.3 0.9 fusion.24
  178.7 140.5 %psum.14 = bf16[512,16]{0,1:T(8,128)(2,1)S(1)} all-reduce(bf16[512,16]{0,1:T(8,128)(2,1)S(1)} %multiply_reduce_fusion.1), channel_id=1, replica_groups=mesh['tensor'=32,'adapter'=8] {'tensor'}, use_global_device_ids=true, to_apply=%region_13.15 | all-reduce | flops 8192 | bytes 32768 | tf_op jit(solution)/shard_map/psum | solution.py:110
  319.1 1.0 fusion.79
  320.2 2.6 fusion.3
  324.3 2.4 scatter_custom_fusion
  326.8 151.8 %all-reduce.5.cloned.1.call-done = bf16[512,2880]{1,0:T(8,128)(2,1)} async-done(((bf16[512,2880]{1,0:T(8,128)(2,1)}), bf16[512,2880]{1,0:T(8,128)(2,1)}) %all-reduce.5.cloned.1.call-update) | async-done | bytes 2949136 | tf_op jit(solution)/shard_map/psum | solution.py:110
  478.6 5.6 convert_add_fusion
  484.2 3.1 multiply_convert_fusion
  487.3 0.9 constant_dynamic-slice_fusion.1
  488.2 1.1 broadcast_select_fusion.1
  489.3 4.8 all-to-all-start.2
  494.7 1.3 gather_fusion.1
  496.7 4.1 gather_fusion
  500.7 2.4 fusion.8
  503.1 2.3 all-to-all-done.2
  505.4 2.2 fusion.23
  509.0 4.7 all-to-all-start.3
  513.6 3.6 fusion.41
  517.3 4.5 gather_fusion.2
  521.8 6.4 copy.120
  528.4 41.5 %all_gather.15 = bf16[512,16]{1,0:T(8,128)(2,1)S(1)} all-gather(bf16[16,16]{1,0:T(8,128)(2,1)S(1)} %reduce_sum.180), channel_id=1, replica_groups=mesh['tensor'=32,'adapter'=8] {'tensor'}, dimensions={0}, use_global_device_ids=true | all-gather | bytes 16896 | tf_op jit(solution)/shard_map/all_gather | solution.py:106
  569.9 5.3 fusion.4
  575.1 4.8 copy.132
  580.0 202.0 %reduce-scatter.4.cloned.1.call-done = bf16[16,2880]{1,0:T(8,128)(2,1)} async-done(((bf16[512,2880]{1,0:T(8,128)(2,1)}), bf16[16,2880]{1,0:T(8,128)(2,1)}) %reduce-scatter.4.cloned.1.call-update) | async-done | bytes 92176 | tf_op jit(solution)/shard_map/reduce_scatter | solution.py:114
  782.0 1.6 add_convert_fusion.1
  (122 shorter events, 17.1 us)
Async XLA Ops:
  6.5 24.0 %copy-start = (bf16[8,48,2880]{2,1,0:T(8,128)(2,1)S(1)}, bf16[8,48,2880]{2,1,0:T(8,128)(2,1)}, u32[]{:S(2)}) copy-start(bf16[8,48,2880]{2,1,0:T(8,128)(2,1)} %param.29) | copy-start | bytes 6635524
  6.5 85.6 %all-gather.3.cloned.1.call-start = ((), (), s32[]{:S(2)}) async-start(), calls=%async_computation.5 | async-start | bytes 3108864 | tf_op jit(solution)/shard_map/all_gather | solution.py:106
  13.6 17.0 %all-to-all-start = ((bf16[8,16,2880]{2,1,0:T(8,128)(2,1)}), bf16[8,16,2880]{2,1,0:T(8,128)(2,1)S(1)}, u32[]{:S(2)}, u32[]{:S(2)}) async-start(bf16[8,16,2880]{2,1,0:T(8,128)(2,1)} %broadcast_select_fusion.2), calls=%async_computation | async-start | bytes 1507328 | tf_op jit(solution)/shard_map/all_to_all | solution.py:102
  21.0 17.8 %copy-start.17 = (f32[2]{0:T(128)S(1)}, f32[2]{0:T(128)}, u32[]{:S(2)}) copy-start(f32[2]{0:T(128)} %param.28) | copy-start | bytes 28
  34.0 8.6 %all-to-all-start.1 = ((bf16[8,2,384]{2,1,0:T(2,128)(2,1)}), bf16[8,2,384]{2,1,0:T(2,128)(2,1)S(1)}, u32[]{:S(2)}, u32[]{:S(2)}) async-start(bf16[8,2,384]{2,1,0:T(2,128)(2,1)} %reshape.584), calls=%async_computation.1 | async-start | bytes 24576 | tf_op jit(solution)/shard_map/all_to_all | solution.py:102
  38.7 134.4 %all-gather.5.cloned.1.call-start = ((), (), s32[]{:S(2)}) async-start(), calls=%async_computation.6 | async-start | bytes 1081344 | tf_op jit(solution)/shard_map/all_gather | solution.py:236
  88.6 6.3 copy-start.12
  92.2 2.8 copy-start.2
  94.9 1.0 copy-start.10
  96.8 1.2 copy-start.6
  96.8 1.6 copy-start.5
  99.3 379.3 %all-reduce.5.cloned.1.call-start = ((), (), s32[]{:S(2)}) async-start(), calls=%async_computation.7 | async-start | bytes 6029312 | tf_op jit(solution)/shard_map/psum | solution.py:110
  174.6 1.6 copy-start.8
  177.3 1.0 copy-start.16
  177.3 141.8 %copy-start.9 = (bf16[2,16,2880]{2,1,0:T(8,128)(2,1)S(1)}, bf16[2,16,2880]{2,1,0:T(8,128)(2,1)}, u32[]{:S(2)}) copy-start(bf16[2,16,2880]{2,1,0:T(8,128)(2,1)} %param.33) | copy-start | bytes 552964
  319.1 1.1 copy-start.7
  322.9 0.7 copy-start.14
  322.9 0.7 copy-start.15
  322.9 155.7 %copy-start.3 = (bf16[512,2880]{1,0:T(8,128)(2,1)S(1)}, bf16[512,2880]{1,0:T(8,128)(2,1)}, u32[]{:S(2)}) copy-start(bf16[512,2880]{1,0:T(8,128)(2,1)} %all-gather.3.cloned.1.call-done) | copy-start | bytes 8847364
  326.7 157.5 %copy-start.13 = (f32[2880]{0:T(1024)S(1)}, f32[2880]{0:T(1024)}, u32[]{:S(2)}) copy-start(f32[2880]{0:T(1024)} %param.34) | copy-start | bytes 34564
  478.6 5.6 copy-start.4
  489.3 16.1 %all-to-all-start.2 = ((bf16[8,16,2880]{2,1,0:T(8,128)(2,1)}), bf16[8,16,2880]{2,1,0:T(8,128)(2,1)S(1)}, u32[]{:S(2)}, u32[]{:S(2)}) async-start(bf16[8,16,2880]{2,1,0:T(8,128)(2,1)} %broadcast_select_fusion.1), calls=%async_computation.2 | async-start | bytes 1507328 | tf_op jit(solution)/shard_map/all_to_all | solution.py:102
  509.0 19.3 %all-to-all-start.3 = ((bf16[8,2,128]{2,1,0:T(2,128)(2,1)}), bf16[8,2,128]{2,1,0:T(2,128)(2,1)S(1)}, u32[]{:S(2)}, u32[]{:S(2)}) async-start(bf16[8,2,128]{2,1,0:T(2,128)(2,1)} %reshape.586), calls=%async_computation.3 | async-start | bytes 8192 | tf_op jit(solution)/shard_map/all_to_all | solution.py:102
  513.6 268.3 %reduce-scatter.4.cloned.1.call-start = ((), (), s32[]{:S(2)}) async-start(), calls=%async_computation.8 | async-start | bytes 3108864 | tf_op jit(solution)/shard_map/reduce_scatter | solution.py:114
  521.8 48.1 %copy-start.11 = (bf16[2,16,2880]{2,1,0:T(8,128)(2,1)S(1)}, bf16[2,16,2880]{2,1,0:T(8,128)(2,1)}, u32[]{:S(2)}) copy-start(bf16[2,16,2880]{2,1,0:T(8,128)(2,1)} %param.38) | copy-start | bytes 552964
  575.1 208.4 %copy-start.1 = (bf16[8,48,2880]{2,1,0:T(8,128)(2,1)S(1)}, bf16[8,48,2880]{2,1,0:T(8,128)(2,1)}, u32[]{:S(2)}) copy-start(bf16[8,48,2880]{2,1,0:T(8,128)(2,1)} %param.29) | copy-start | bytes 6635524
Sparse Core Ops, SparseCore 0:
  9.9 82.1 all-gather.2
  99.4 73.7 all-gather.4
  323.0 155.5 all-reduce.4
  580.1 201.8 reduce-scatter.3
where the time goes:
time: 791 us; the launch traced here: 790 us
  waiting for transfers between devices  439 us (55%)
  blocking collectives  228 us (29%)
  local copies, waits for them, and re-layouts  33.7 us (4%)
  other arithmetic  29.9 us (4%)
  matrix products  26.7 us (3%)
  starting transfers between devices  19.9 us (3%)
  between operations  13.6 us (2%)
    reduce_scatter x1, waiting for transfers between devices, partial_sum(): lax.psum_scatter(term_maker(jnp.int32(0), lax.axis_size('tensor') * own_r...  202 us
    psum x1, waiting for transfers between devices, tensor_total(): lax.psum(partial_value.astype(jnp.bfloat16), 'tensor').astype(jnp.float32)  152 us
    psum x1, blocking collectives, tensor_total(): lax.psum(partial_value.astype(jnp.bfloat16), 'tensor').astype(jnp.float32)  140 us
    all_gather x2, blocking collectives, gather_tokens(): return lax.all_gather(row_block, 'tensor', axis=0, tiled=True)  87.3 us
    all_gather x1, waiting for transfers between devices, per_device(): keyval_all = lax.all_gather(keyval_part, 'tensor', axis=2, tiled=True)  68.5 us
    all_to_all x4, starting transfers between devices, swap_owner(): lax.all_to_all(outgoing, 'adapter', split_axis=0, concat_axis=0, tiled=True)  19.8 us
  transfers between devices with their start and end apart: 8, of which 7 were waited for; matrix products, arithmetic and copies ran while one was open for 6% of the time, Pallas kernels for 0%

commit v1 on v0

--- a/solution.py
+++ b/solution.py
@@ -3,7 +3,7 @@
 import jax
 import jax.numpy as jnp
 from jax import lax
-from jax.sharding import PartitionSpec as P
+from jax.sharding import Mesh, PartitionSpec as P
 
 QH = 64
 KVH = 8
@@ -13,6 +13,7 @@
 TOP = 4
 ROUTED = 32
 R = 16
+TENSOR = ("tz", "tx")
 
 
 NORM_EPS = 1e-05
@@ -98,24 +99,44 @@
     return lax.map(one_block, block_starts).reshape(row_count, -1)
 
 
+def tensor_index():
+    return lax.axis_index("tz") * lax.axis_size("tx") + lax.axis_index("tx")
+
+
+def tensor_size():
+    return lax.axis_size("tz") * lax.axis_size("tx")
+
+
+def gather_tensor(block, axis=0):
+    inner = lax.all_gather(block, "tx", axis=axis, tiled=True)
+    return lax.all_gather(inner, "tz", axis=axis, tiled=True)
+
+
+def scatter_tensor(block):
+    inner = lax.psum_scatter(block, "tz", scatter_dimension=0, tiled=True)
+    return lax.psum_scatter(inner, "tx", scatter_dimension=0, tiled=True)
+
+
 def swap_owner(outgoing):
     return lax.all_to_all(outgoing, "adapter", split_axis=0, concat_axis=0, tiled=True)
 
 
 def gather_tokens(row_block):
-    return lax.all_gather(row_block, "tensor", axis=0, tiled=True)
+    return gather_tensor(row_block)
 
 
 def tensor_total(partial_value):
-    return lax.psum(partial_value.astype(jnp.bfloat16), "tensor").astype(jnp.float32)
+    return gather_tensor(scatter_tensor(partial_value.astype(jnp.bfloat16))).astype(jnp.float32)
+
+
+def small_total(partial_value):
+    inner = lax.psum(partial_value.astype(jnp.bfloat16), "tx")
+    return lax.psum(inner, "tz").astype(jnp.float32)
 
 
 def partial_sum(term_maker, own_rows):
-    return lax.psum_scatter(
-        term_maker(jnp.int32(0), lax.axis_size("tensor") * own_rows).astype(jnp.bfloat16),
-        "tensor",
-        scatter_dimension=0,
-        tiled=True,
+    return scatter_tensor(
+        term_maker(jnp.int32(0), tensor_size() * own_rows).astype(jnp.bfloat16)
     ).astype(jnp.float32)
 
 
@@ -123,7 +144,7 @@
     own_rows = normed_own.shape[0]
     owner_count = lax.axis_size("adapter")
     owner_here = lax.axis_index("adapter")
-    first_row = lax.axis_index("tensor") * own_rows
+    first_row = tensor_index() * own_rows
     stored, rank_width, width_d = bank.shape
     adapter_count = adapter_slot.shape[0]
     adapter_ids = jnp.arange(adapter_count, dtype=jnp.int32)
@@ -184,9 +205,9 @@
     expert_weights,
 ):
     own_rows = tokens.shape[0]
-    tensor_here = lax.axis_index("tensor")
+    tensor_here = tensor_index()
     group_here = lax.axis_index("adapter")
-    group_rows = own_rows * lax.axis_size("tensor")
+    group_rows = own_rows * tensor_size()
     adapter_count = adapter_slot.shape[0]
     query_cols = query_weight.shape[1]
     local_count = output_up.shape[0]
@@ -233,7 +254,7 @@
         .astype(jnp.bfloat16)
         .reshape(group_rows, 2, entries_here, KVH)
     )
-    keyval_all = lax.all_gather(keyval_part, "tensor", axis=2, tiled=True)
+    keyval_all = gather_tensor(keyval_part, axis=2)
     key_rows = rotate(
         jnp.transpose(keyval_all[:, 0].astype(jnp.float32), (0, 2, 1)), position
     ).astype(jnp.bfloat16)
@@ -254,7 +275,7 @@
     rank_terms = jnp.sum(
         rank_terms.reshape(group_rows, adapter_count, R) * onehot[:, :, None], axis=1
     )
-    rank_out = tensor_total(settle(rank_terms)).astype(jnp.bfloat16)
+    rank_out = small_total(settle(rank_terms)).astype(jnp.bfloat16)
     spread_out = spread_rank(local_hot, rank_out)
     up_out = output_up.reshape(local_count * R, -1)
     term = jnp.dot(mixed_rows, output_weight, preferred_element_type=jnp.float32)
@@ -303,31 +324,40 @@
     return (hidden_own + moe_own).astype(jnp.bfloat16)
 
 
+def split_mesh(mesh):
+    grid = mesh.devices
+    tensor_count, adapter_count = grid.shape
+    x_coords = {getattr(d, "coords", (i,))[0] for i, d in enumerate(grid[:, 0])}
+    x_count = len(x_coords) if tensor_count % len(x_coords) == 0 else 1
+    return Mesh(grid.reshape(tensor_count // x_count, x_count, adapter_count), ("tz", "tx", "adapter"))
+
+
 def solution(mesh):
+    mesh = split_mesh(mesh)
     in_specs = (
-        P(("adapter", "tensor"), None),
-        P(),
-        P(None, "tensor"),
-        P(None, None, "tensor", None),
-        P("tensor", None),
-        P("tensor"),
+        P(("adapter", "tz", "tx"), None),
+        P(),
+        P(None, TENSOR),
+        P(None, None, TENSOR, None),
+        P(TENSOR, None),
+        P(TENSOR),
         P("adapter", None, None),
-        P(None, None, "tensor"),
-        P(None, None, None, "tensor", None),
-        P(None, None, "tensor"),
-        P("tensor", None, None),
-        P(),
-        P(None, None, "tensor"),
-        P("tensor", None),
+        P(None, None, TENSOR),
+        P(None, None, None, TENSOR, None),
+        P(None, None, TENSOR),
+        P(TENSOR, None, None),
+        P(),
+        P(None, None, TENSOR),
+        P(TENSOR, None),
         P("adapter", None, None),
-        P("tensor", None, None),
+        P(TENSOR, None, None),
         P(),
         P(),
         P(),
         P("adapter", None),
         P("adapter", None),
     )
-    out_specs = P(("adapter", "tensor"), None)
+    out_specs = P(("adapter", "tz", "tx"), None)
     return jax.shard_map(
         per_device, mesh=mesh, in_specs=in_specs, out_specs=out_specs, check_vma=False
     )

time: 791 us -> 513 us (0.65)
  waiting for transfers between devices: 439 us -> 223 us
  blocking collectives: 228 us -> 163 us
    psum x1 -> x0, waiting for transfers between devices: 152 us -> none  [tensor_total(): lax.psum(partial_value.astype(jnp.bfloat16), 'tensor').astype(jnp.float32)]
    reduce_scatter x1 -> x2, waiting for transfers between devices: 202 us -> 50.8 us  [scatter_tensor(): return lax.psum_scatter(inner, 'tx', scatter_dimension=0, tiled=True)]
    psum x1 -> x2, blocking collectives: 140 us -> 45.3 us  [the longest x1 28.4 us: small_total(): return lax.psum(inner, 'tz').astype(jnp.float32)]
    unnamed x4 -> x9, waiting for transfers between devices: 0.76 us -> 88.2 us
    all_gather x2 -> x7, blocking collectives: 87.3 us -> 117 us  [the longest x5 64.4 us: gather_tensor(): inner = lax.all_gather(block, 'tx', axis=axis, tiled=True)]
    all_gather x2 -> x3, waiting for transfers between devices: 70.3 us -> 71.3 us  [gather_tensor(): return lax.all_gather(inner, 'tz', axis=axis, tiled=True)]
  transfers between devices with their start and end apart: 8 -> 11, of which waited for: 7 -> 9; matrix products, arithmetic and copies ran while one was open for 6% -> 9% of each run, Pallas kernels for 0% -> 0%
where the time goes in v1:
time: 513 us; the launch traced here: 511 us
  waiting for transfers between devices  223 us (43%)
  blocking collectives  163 us (32%)
  local copies, waits for them, and re-layouts  35.9 us (7%)
  other arithmetic  31.5 us (6%)
  matrix products  25 us (5%)
  starting transfers between devices  19.3 us (4%)
  between operations  14 us (3%)
    unnamed x9, waiting for transfers between devices  88.2 us
    all_gather x3, waiting for transfers between devices, gather_tensor(): return lax.all_gather(inner, 'tz', axis=axis, tiled=True)  71.3 us
    all_gather x5, blocking collectives, gather_tensor(): inner = lax.all_gather(block, 'tx', axis=axis, tiled=True)  64.4 us
    all_gather x2, blocking collectives, gather_tensor(): return lax.all_gather(inner, 'tz', axis=axis, tiled=True)  52.9 us
    reduce_scatter x2, waiting for transfers between devices, scatter_tensor(): return lax.psum_scatter(inner, 'tx', scatter_dimension=0, tiled=True)  50.8 us
    psum x1, blocking collectives, small_total(): return lax.psum(inner, 'tz').astype(jnp.float32)  28.4 us
    all_to_all x4, starting transfers between devices, swap_owner(): lax.all_to_all(outgoing, 'adapter', split_axis=0, concat_axis=0, tiled=True)  19.1 us
    psum x1, blocking collectives, small_total(): inner = lax.psum(partial_value.astype(jnp.bfloat16), 'tx')  16.8 us
  transfers between devices with their start and end apart: 11, of which 9 were waited for; matrix products, arithmetic and copies ran while one was open for 9% of the time, Pallas kernels for 0%

profile of v1, /device:TPU:8, one launch (start us, length us, event | category | flops | bytes accessed | tf_op | source)
XLA Modules:
  0.0 511.3 jit_solution(16262713971922473817)
XLA Ops:
  6.5 14.6 %all_gather.30 = bf16[64,2880]{1,0:T(8,128)(2,1)} all-gather(bf16[16,2880]{1,0:T(8,128)(2,1)} %param.23), channel_id=1, replica_groups=mesh['tz'=8,'tx'=4,'adapter'=8] {'tx'}, dimensions={0}, use_global_device_ids=true | all-gather | bytes 460800 | tf_op jit(solution)/shard_map/all_gather | solution.py:111
  24.5 1.0 fusion.54
  25.5 1.0 fusion.56
  26.5 1.0 broadcast_select_fusion.2
  27.6 4.9 all-to-all-start
  35.5 8.3 %all-to-all-done = bf16[8,16,2880]{2,1,0:T(8,128)(2,1)S(1)} async-done(((bf16[8,16,2880]{2,1,0:T(8,128)(2,1)}), bf16[8,16,2880]{2,1,0:T(8,128)(2,1)S(1)}, u32[]{:S(2)}, u32[]{:S(2)}) %all-to-all-start) | async-done | bytes 737312 | tf_op jit(solution)/shard_map/all_to_all | solution.py:121
  43.8 1.5 fusion.20
  47.2 4.7 all-to-all-start.1
  53.5 2.3 all-to-all-done.1
  56.0 12.0 %all_gather.32 = bf16[64,48]{1,0:T(8,128)(2,1)S(1)} all-gather(bf16[16,48]{1,0:T(8,128)(2,1)S(1)} %reduce_sum.170), channel_id=1, replica_groups=mesh['tz'=8,'tx'=4,'adapter'=8] {'tx'}, dimensions={0}, use_global_device_ids=true | all-gather | bytes 7680 | tf_op jit(solution)/shard_map/all_gather | solution.py:111
  68.0 28.2 %all-gather = bf16[8,64,48]{1,2,0:T(8,128)(2,1)S(1)} all-gather(bf16[1,64,48]{1,2,0:T(8,128)(2,1)S(1)} %bitcast.146), channel_id=1, replica_groups=mesh['tz'=8,'tx'=4,'adapter'=8] {'tz'}, dimensions={0}, use_global_device_ids=true | all-gather | bytes 55296 | tf_op jit(solution)/shard_map/all_gather | solution.py:112
  97.1 1.5 broadcast_multiply_fusion.1
  98.6 2.7 fusion
  101.3 1.0 fusion.2
  105.0 12.0 %all_gather.34 = bf16[512,2,8,8]{0,3,1,2:T(8,128)(2,1)S(1)} all-gather(bf16[512,2,2,8]{0,3,1,2:T(8,128)(2,1)S(1)} %pad_maximum_fusion.1), channel_id=1, replica_groups=mesh['tz'=8,'tx'=4,'adapter'=8] {'tx'}, dimensions={2}, use_global_device_ids=true | all-gather | bytes 163840 | tf_op jit(solution)/shard_map/all_gather | solution.py:111
  119.3 1.3 convolution_bitcast_fusion
  120.6 2.2 convolution_add_fusion
  122.9 30.3 %all-gather.8.cloned.1.call-done = bf16[512,2,64,8]{0,2,3,1:T(8,128)(2,1)} async-done(((bf16[512,2,8,8]{0,2,3,1:T(8,128)(2,1)}), bf16[512,2,64,8]{0,2,3,1:T(8,128)(2,1)}) %all-gather.8.cloned.1.call-update) | async-done | bytes 1048592 | tf_op jit(solution)/shard_map/all_gather | solution.py:112
  153.3 1.4 slice_bitcast_fusion.1
  156.3 1.0 fusion.7
  158.8 16.8 %psum.14 = bf16[512,16]{0,1:T(8,128)(2,1)S(1)} all-reduce(bf16[512,16]{0,1:T(8,128)(2,1)S(1)} %multiply_reduce_fusion.1), channel_id=1, replica_groups=mesh['tz'=8,'tx'=4,'adapter'=8] {'tx'}, use_global_device_ids=true, to_apply=%region_13.15 | all-reduce | flops 8192 | bytes 32768 | tf_op jit(solution)/shard_map/psum | solution.py:133
  175.7 28.4 %psum.15 = bf16[512,16]{0,1:T(8,128)(2,1)S(1)} all-reduce(bf16[512,16]{0,1:T(8,128)(2,1)S(1)} %psum.14), channel_id=1, replica_groups=mesh['tz'=8,'tx'=4,'adapter'=8] {'tz'}, use_global_device_ids=true, to_apply=%region_14.16 | all-reduce | flops 8192 | bytes 32768 | tf_op jit(solution)/shard_map/psum | solution.py:134
  206.1 3.0 copy.115
  209.2 43.9 %reduce-scatter.13.cloned.1.call-done = bf16[64,2880]{1,0:T(8,128)(2,1)} async-done(((bf16[512,2880]{1,0:T(8,128)(2,1)}), bf16[64,2880]{1,0:T(8,128)(2,1)}) %reduce-scatter.13.cloned.1.call-update) | async-done | bytes 368656
  253.1 25.2 %reduce-scatter.15.cloned.1.call-done = bf16[16,2880]{1,0:T(8,128)(2,1)} async-done(((bf16[64,2880]{1,0:T(8,128)(2,1)}), bf16[16,2880]{1,0:T(8,128)(2,1)}) %reduce-scatter.15.cloned.1.call-update) | async-done | bytes 92176 | tf_op jit(solution)/shard_map/reduce_scatter | solution.py:117
  278.4 13.4 %all_gather.36 = bf16[64,2880]{1,0:T(8,128)(2,1)} all-gather(bf16[16,2880]{1,0:T(8,128)(2,1)} %reduce-scatter.15.cloned.1.call-done), channel_id=1, replica_groups=mesh['tz'=8,'tx'=4,'adapter'=8] {'tx'}, dimensions={0}, use_global_device_ids=true | all-gather | bytes 460800 | tf_op jit(solution)/shard_map/all_gather | solution.py:111
  292.6 2.4 scatter_custom_fusion
  295.1 40.9 %all-gather.10.cloned.1.call-done = bf16[512,2880]{1,0:T(8,128)(2,1)} async-done(((bf16[64,2880]{1,0:T(8,128)(2,1)}), bf16[512,2880]{1,0:T(8,128)(2,1)}) %all-gather.10.cloned.1.call-update) | async-done | bytes 2949136 | tf_op jit(solution)/shard_map/all_gather | solution.py:112
  336.0 5.6 %convert_add_fusion = (f32[512,2880]{1,0:T(8,128)}, f32[512]{0:T(512)S(1)}) fusion(bf16[512,2880]{1,0:T(8,128)(2,1)S(1)} %copy-done.3, bf16[512,2880]{1,0:T(8,128)(2,1)} %all-gather.10.cloned.1.call-done), kind=kLoop, calls=%fused_computation.6 | loop fusion | flops 7372288 | bytes 11798528 | tf_op jit(solution)/shard_map/add | solution.py:285
  341.6 3.1 multiply_convert_fusion
  345.6 1.1 broadcast_select_fusion.1
  346.7 4.8 all-to-all-start.2
  352.1 1.3 gather_fusion.1
  354.1 4.1 gather_fusion
  358.1 2.4 fusion.8
  360.6 2.3 all-to-all-done.2
  362.8 2.2 fusion.23
  366.4 4.7 all-to-all-start.3
  371.1 3.6 fusion.41
  374.7 4.5 gather_fusion.2
  379.2 6.4 %copy.105 = f32[512,2880]{0,1:T(8,128)} copy(f32[512,2880]{1,0:T(8,128)} %gather_fusion.2) | data formatting | bytes 11796480 | tf_op jit(solution)/shard_map/jit(_take)/gather | solution.py:319
  385.8 12.3 %all_gather.38 = bf16[64,16]{1,0:T(8,128)(2,1)S(1)} all-gather(bf16[16,16]{1,0:T(8,128)(2,1)S(1)} %reduce_sum.180), channel_id=1, replica_groups=mesh['tz'=8,'tx'=4,'adapter'=8] {'tx'}, dimensions={0}, use_global_device_ids=true | all-gather | bytes 2560 | tf_op jit(solution)/shard_map/all_gather | solution.py:111
  398.2 24.7 %all-gather.1 = bf16[8,64,16]{1,2,0:T(8,128)(2,1)S(1)} all-gather(bf16[1,64,16]{1,2,0:T(8,128)(2,1)S(1)} %bitcast.147), channel_id=1, replica_groups=mesh['tz'=8,'tx'=4,'adapter'=8] {'tz'}, dimensions={0}, use_global_device_ids=true | all-gather | bytes 18432 | tf_op jit(solution)/shard_map/all_gather | solution.py:112
  422.9 5.2 %fusion.3 = bf16[512,2880]{0,1:T(8,128)(2,1)} fusion(f32[512,2880]{0,1:T(8,128)} %copy.105, bf16[2,16,2880]{2,1,0:T(8,128)(2,1)S(1)} %copy-done.10, pred[512]{0:T(512)(128)(4,1)S(1)} %get-tuple-element.23, pred[512]{0:T(512)(128)(4,1)S(1)} %reduce_or.11, bf16[512,16]{0,1:T(8,128)(2,1)S(1)} %reshape.570, bf16[512,2]{0,1:T(2,128)(2,1)S(1)} %compare_convert_fusion), kind=kOutput, calls=%fused_computation.15 | convolution fusion | flops 100286464 | bytes 9051136 | tf_op jit(solution)/shard_map/dot_general | solution.py:321
  428.2 4.8 copy.119
  433.1 44.2 %reduce-scatter.17.cloned.1.call-done = bf16[64,2880]{1,0:T(8,128)(2,1)} async-done(((bf16[512,2880]{1,0:T(8,128)(2,1)}), bf16[64,2880]{1,0:T(8,128)(2,1)}) %reduce-scatter.17.cloned.1.call-update) | async-done | bytes 368656
  477.3 25.5 %reduce-scatter.19.cloned.1.call-done = bf16[16,2880]{1,0:T(8,128)(2,1)} async-done(((bf16[64,2880]{1,0:T(8,128)(2,1)}), bf16[16,2880]{1,0:T(8,128)(2,1)}) %reduce-scatter.19.cloned.1.call-update) | async-done | bytes 92176 | tf_op jit(solution)/shard_map/reduce_scatter | solution.py:117
  502.9 1.6 add_convert_fusion.1
  (153 shorter events, 25.7 us)
Async XLA Ops:
  6.5 37.3 %copy-start = (bf16[8,48,2880]{2,1,0:T(8,128)(2,1)S(1)}, bf16[8,48,2880]{2,1,0:T(8,128)(2,1)}, u32[]{:S(2)}) copy-start(bf16[8,48,2880]{2,1,0:T(8,128)(2,1)} %param.29) | copy-start | bytes 6635524
  6.5 28.2 %copy-start.12 = (bf16[64,2,16,2,8]{0,4,3,2,1:T(8,128)(2,1)S(1)}, bf16[64,2,16,2,8]{0,4,3,2,1:T(8,128)(2,1)}, u32[]{:S(2)}) copy-start(bf16[64,2,16,2,8]{0,4,3,2,1:T(8,128)(2,1)} %param.31) | copy-start | bytes 196612
  6.5 92.0 %all-gather.6.cloned.1.call-start = ((), (), s32[]{:S(2)}) async-start(), calls=%async_computation.8 | async-start | bytes 3391488 | tf_op jit(solution)/shard_map/all_gather | solution.py:112
  25.5 2.0 copy-start.19
  27.6 16.2 %all-to-all-start = ((bf16[8,16,2880]{2,1,0:T(8,128)(2,1)}), bf16[8,16,2880]{2,1,0:T(8,128)(2,1)S(1)}, u32[]{:S(2)}, u32[]{:S(2)}) async-start(bf16[8,16,2880]{2,1,0:T(8,128)(2,1)} %broadcast_select_fusion.2), calls=%async_computation | async-start | bytes 1507328 | tf_op jit(solution)/shard_map/all_to_all | solution.py:121
  34.8 12.5 %copy-start.14 = (f32[8,16,8]{1,2,0:T(8,128)}, f32[8,16,8]{1,2,0:T(8,128)S(1)}, u32[]{:S(2)}) copy-start(f32[8,16,8]{1,2,0:T(8,128)S(1)} %fusion.81) | copy-start | bytes 12292
  34.8 17.2 %copy-start.24 = (f32[2]{0:T(128)S(1)}, f32[2]{0:T(128)}, u32[]{:S(2)}) copy-start(f32[2]{0:T(128)} %param.28) | copy-start | bytes 28
  47.2 8.6 %all-to-all-start.1 = ((bf16[8,2,384]{2,1,0:T(2,128)(2,1)}), bf16[8,2,384]{2,1,0:T(2,128)(2,1)S(1)}, u32[]{:S(2)}, u32[]{:S(2)}) async-start(bf16[8,2,384]{2,1,0:T(2,128)(2,1)} %reshape.594), calls=%async_computation.1 | async-start | bytes 24576 | tf_op jit(solution)/shard_map/all_to_all | solution.py:121
  51.9 101.3 %all-gather.8.cloned.1.call-start = ((), (), s32[]{:S(2)}) async-start(), calls=%async_computation.9 | async-start | bytes 1179648 | tf_op jit(solution)/shard_map/all_gather | solution.py:112
  53.4 47.8 %copy-start.13 = (f32[2880]{0:T(1024)S(1)}, f32[2880]{0:T(1024)}, u32[]{:S(2)}) copy-start(f32[2880]{0:T(1024)} %param.24) | copy-start | bytes 34564
  98.6 2.8 copy-start.2
  101.3 1.0 copy-start.9
  103.2 1.2 copy-start.6
  103.2 1.6 copy-start.5
  117.8 135.3 %reduce-scatter.13.cloned.1.call-start = ((), (), s32[]{:S(2)}) async-start(), calls=%async_computation.11 | async-start | bytes 3391488
  122.9 33.3 %copy-start.21 = (pred[2]{0:T(512)(128)(4,1)S(1)}, pred[2]{0:T(512)(128)(4,1)}, u32[]{:S(2)}) copy-start(pred[2]{0:T(512)(128)(4,1)} %compare_and_fusion) | copy-start | bytes 10
  155.5 1.8 copy-start.22
  157.4 0.9 copy-start.11
  157.4 1.0 copy-start.23
  157.4 46.7 %copy-start.8 = (bf16[2,16,2880]{2,1,0:T(8,128)(2,1)S(1)}, bf16[2,16,2880]{2,1,0:T(8,128)(2,1)}, u32[]{:S(2)}) copy-start(bf16[2,16,2880]{2,1,0:T(8,128)(2,1)} %param.33) | copy-start | bytes 552964
  204.1 1.1 copy-start.7
  209.1 82.7 %copy-start.17 = (f32[512,4]{0,1:T(4,128)S(1)}, f32[512,4]{0,1:T(4,128)}, u32[]{:S(2)}) copy-start(f32[512,4]{0,1:T(4,128)} %param.43) | copy-start | bytes 24580
  209.1 82.7 %copy-start.18 = (s32[512,4]{0,1:T(4,128)S(1)}, s32[512,4]{0,1:T(4,128)}, u32[]{:S(2)}) copy-start(s32[512,4]{0,1:T(4,128)} %param.42) | copy-start | bytes 24580
  209.1 126.9 %copy-start.3 = (bf16[512,2880]{1,0:T(8,128)(2,1)S(1)}, bf16[512,2880]{1,0:T(8,128)(2,1)}, u32[]{:S(2)}) copy-start(bf16[512,2880]{1,0:T(8,128)(2,1)} %all-gather.6.cloned.1.call-done) | copy-start | bytes 8847364
  209.2 69.2 %reduce-scatter.15.cloned.1.call-start = ((), (), s32[]{:S(2)}) async-start(), calls=%async_computation.12 | async-start | bytes 471040 | tf_op jit(solution)/shard_map/reduce_scatter | solution.py:117
  253.1 82.9 %all-gather.10.cloned.1.call-start = ((), (), s32[]{:S(2)}) async-start(), calls=%async_computation.10 | async-start | bytes 3391488 | tf_op jit(solution)/shard_map/all_gather | solution.py:112
  295.0 46.6 %copy-start.16 = (f32[2880]{0:T(1024)S(1)}, f32[2880]{0:T(1024)}, u32[]{:S(2)}) copy-start(f32[2880]{0:T(1024)} %param.34) | copy-start | bytes 34564
  336.0 5.6 %copy-start.4 = (bf16[512,2880]{1,0:T(8,128)(2,1)S(1)}, bf16[512,2880]{1,0:T(8,128)(2,1)}, u32[]{:S(2)}) copy-start(bf16[512,2880]{1,0:T(8,128)(2,1)} %all-gather.10.cloned.1.call-done) | copy-start | bytes 8847364
  341.6 4.0 copy-start.20
  346.7 16.1 %all-to-all-start.2 = ((bf16[8,16,2880]{2,1,0:T(8,128)(2,1)}), bf16[8,16,2880]{2,1,0:T(8,128)(2,1)S(1)}, u32[]{:S(2)}, u32[]{:S(2)}) async-start(bf16[8,16,2880]{2,1,0:T(8,128)(2,1)} %broadcast_select_fusion.1), calls=%async_computation.2 | async-start | bytes 1507328 | tf_op jit(solution)/shard_map/all_to_all | solution.py:121
  358.1 4.7 copy-start.15
  366.4 19.3 %all-to-all-start.3 = ((bf16[8,2,128]{2,1,0:T(2,128)(2,1)}), bf16[8,2,128]{2,1,0:T(2,128)(2,1)S(1)}, u32[]{:S(2)}, u32[]{:S(2)}) async-start(bf16[8,2,128]{2,1,0:T(2,128)(2,1)} %reshape.596), calls=%async_computation.3 | async-start | bytes 8192 | tf_op jit(solution)/shard_map/all_to_all | solution.py:121
  371.1 106.2 %reduce-scatter.17.cloned.1.call-start = ((), (), s32[]{:S(2)}) async-start(), calls=%async_computation.13 | async-start | bytes 3391488
  379.2 43.7 %copy-start.10 = (bf16[2,16,2880]{2,1,0:T(8,128)(2,1)S(1)}, bf16[2,16,2880]{2,1,0:T(8,128)(2,1)}, u32[]{:S(2)}) copy-start(bf16[2,16,2880]{2,1,0:T(8,128)(2,1)} %param.38) | copy-start | bytes 552964
  428.2 76.3 %copy-start.1 = (bf16[8,48,2880]{2,1,0:T(8,128)(2,1)S(1)}, bf16[8,48,2880]{2,1,0:T(8,128)(2,1)}, u32[]{:S(2)}) copy-start(bf16[8,48,2880]{2,1,0:T(8,128)(2,1)} %param.29) | copy-start | bytes 6635524
  433.0 69.8 %reduce-scatter.19.cloned.1.call-start = ((), (), s32[]{:S(2)}) async-start(), calls=%async_computation.14 | async-start | bytes 471040 | tf_op jit(solution)/shard_map/reduce_scatter | solution.py:117
Sparse Core Ops, SparseCore 0:
  21.3 45.7 all-gather.5
  117.9 35.3 all-gather.7
  209.3 43.7 reduce-scatter.12
  255.5 22.8 reduce-scatter.14
  291.9 44.0 all-gather.9
  433.1 44.0 reduce-scatter.16
  479.8 22.9 reduce-scatter.18

commit v2 on v1

--- a/solution.py
+++ b/solution.py
@@ -235,36 +235,39 @@
     queries = rotate(queries.reshape(group_rows, query_cols // HD, HD), position).astype(
         jnp.bfloat16
     )
-    key_weight = keyval_weight[:, 0].reshape(keyval_weight.shape[0], entries_here * KVH)
-    value_weight = keyval_weight[:, 1].reshape(keyval_weight.shape[0], entries_here * KVH)
-    key_part = jnp.dot(normed, key_weight, preferred_element_type=jnp.float32)
+    heads_here = query_cols // HD
+    tensor_count = tensor_size()
+    dest_head = (jnp.arange(tensor_count, dtype=jnp.int32) * heads_here) // (QH // KVH)
+    weight_send = jnp.moveaxis(jnp.take(keyval_weight, dest_head, axis=3), 3, 0)
+    weight_recv = lax.all_to_all(weight_send, TENSOR, 0, 0, tiled=True)
+    head_weight = jnp.transpose(weight_recv, (1, 2, 0, 3)).reshape(
+        keyval_weight.shape[0], 2, tensor_count * entries_here
+    )
+    up_send = jnp.moveaxis(jnp.take(keyval_up, dest_head, axis=4), 4, 0)
+    up_recv = lax.all_to_all(up_send, TENSOR, 0, 0, tiled=True)
+    head_up = jnp.transpose(up_recv, (1, 2, 3, 0, 4)).reshape(
+        adapter_count, 2, R, tensor_count * entries_here
+    )
+    key_part = jnp.dot(normed, head_weight[:, 0], preferred_element_type=jnp.float32)
     key_part = key_part + jnp.dot(
         spread_rank(onehot, rank_qkv[:, R : 2 * R]),
-        keyval_up[:, 0].reshape(adapter_count * R, -1),
-        preferred_element_type=jnp.float32,
-    )
-    value_part = jnp.dot(normed, value_weight, preferred_element_type=jnp.float32)
+        head_up[:, 0].reshape(adapter_count * R, -1),
+        preferred_element_type=jnp.float32,
+    )
+    value_part = jnp.dot(normed, head_weight[:, 1], preferred_element_type=jnp.float32)
     value_part = value_part + jnp.dot(
         spread_rank(onehot, rank_qkv[:, 2 * R : 3 * R]),
-        keyval_up[:, 1].reshape(adapter_count * R, -1),
-        preferred_element_type=jnp.float32,
-    )
-    keyval_part = (
-        jnp.stack([key_part, value_part], axis=1)
-        .astype(jnp.bfloat16)
-        .reshape(group_rows, 2, entries_here, KVH)
-    )
-    keyval_all = gather_tensor(keyval_part, axis=2)
+        head_up[:, 1].reshape(adapter_count * R, -1),
+        preferred_element_type=jnp.float32,
+    )
     key_rows = rotate(
-        jnp.transpose(keyval_all[:, 0].astype(jnp.float32), (0, 2, 1)), position
+        key_part.astype(jnp.bfloat16).astype(jnp.float32)[:, None, :], position
     ).astype(jnp.bfloat16)
-    value_rows = jnp.transpose(keyval_all[:, 1], (0, 2, 1))
-    heads_here = query_cols // HD
-    head_map = (tensor_here * heads_here + jnp.arange(heads_here, dtype=jnp.int32)) // (QH // KVH)
+    value_rows = value_part.astype(jnp.bfloat16)[:, None, :]
     mixed_rows = attend(
         queries,
-        jnp.take(key_rows, head_map, axis=1),
-        jnp.take(value_rows, head_map, axis=1),
+        jnp.broadcast_to(key_rows, (group_rows, heads_here, HD)),
+        jnp.broadcast_to(value_rows, (group_rows, heads_here, HD)),
         segment,
         sink_logits,
     )
@@ -286,8 +289,24 @@
     normed_two = rms_scale(hidden_all, gain_mixture)
     hidden_own = lax.dynamic_slice_in_dim(hidden_all, first_own, own_rows, 0)
     normed_two_own = lax.dynamic_slice_in_dim(normed_two, first_own, own_rows, 0)
-    rank_moe_own = ask_owners(normed_two_own, mixture_down, lengths, prompt_adapter, adapter_slot)
-    rank_moe = gather_tokens(rank_moe_own)
+    prompt_count = adapter_row.shape[0]
+    owner_count = lax.axis_size("adapter")
+    bank_send = jnp.broadcast_to(mixture_down[None], (owner_count,) + mixture_down.shape)
+    bank_all = lax.all_to_all(bank_send, "adapter", 0, 0, tiled=True)
+    bank_all = bank_all.reshape(-1, R, mixture_down.shape[-1])
+    bank_group = jnp.take(bank_all, jnp.take(adapter_slot, adapter_row), axis=0)
+    moe_proj = lax.dot_general(
+        normed_two,
+        bank_group.reshape(prompt_count * R, -1),
+        (((1,), (1,)), ((), ())),
+        preferred_element_type=jnp.float32,
+    )
+    segment_hot = (segment[:, None] == jnp.arange(prompt_count, dtype=jnp.int32)[None, :]).astype(
+        jnp.float32
+    )
+    rank_moe = jnp.sum(
+        moe_proj.reshape(group_rows, prompt_count, R) * segment_hot[:, :, None], axis=1
+    ).astype(jnp.bfloat16)
     expert_here = tensor_here * slice_width // FF
     named = expert_ids == expert_here
     route_weight = jnp.sum(jnp.where(named, expert_weights, 0.0), axis=1)

time: 513 us -> 445 us (0.87)
  blocking collectives: 163 us -> 112 us
  waiting for transfers between devices: 223 us -> 178 us
  local copies, waits for them, and re-layouts: 35.9 us -> 53.8 us
  starting transfers between devices: 19.3 us -> 29.7 us
    all_gather x3 -> x2, waiting for transfers between devices: 71.3 us -> 3.55 us  [gather_tensor(): return lax.all_gather(inner, 'tz', axis=axis, tiled=True)]
    all_to_all x0 -> x3, waiting for transfers between devices: none -> 42.1 us  [the longest x1 30.3 us: per_device(): bank_all = lax.all_to_all(bank_send, 'adapter', 0, 0, tiled=True)]
    all_gather x2 -> x1, blocking collectives: 52.9 us -> 25.8 us  [gather_tensor(): return lax.all_gather(inner, 'tz', axis=axis, tiled=True)]
    all_gather x5 -> x3, blocking collectives: 64.4 us -> 41 us  [gather_tensor(): inner = lax.all_gather(block, 'tx', axis=axis, tiled=True)]
    all_to_all x0 -> x3, starting transfers between devices: none -> 19 us  [the longest x1 9.51 us: per_device(): up_recv = lax.all_to_all(up_send, TENSOR, 0, 0, tiled=True)]
    all_to_all x4 -> x2, waiting for transfers between devices: 12.9 us -> 2.35 us  [swap_owner(): lax.all_to_all(outgoing, 'adapter', split_axis=0, concat_axis=0, tiled=True)]
    all_to_all x4 -> x2, starting transfers between devices: 19.1 us -> 10.3 us  [swap_owner(): lax.all_to_all(outgoing, 'adapter', split_axis=0, concat_axis=0, tiled=True)]
    gather x2 -> x4, local copies, waits for them, and re-layouts: 1.35 us -> 9.46 us  [the longest x2 4.06 us: per_device(): bank_group = jnp.take(bank_all, jnp.take(adapter_slot, adapter_row), axis=0)]
  transfers between devices with their start and end apart: 11 -> 11, of which waited for: 9 -> 8; matrix products, arithmetic and copies ran while one was open for 9% -> 11% of each run, Pallas kernels for 0% -> 0%
where the time goes in v2:
time: 445 us; the launch traced here: 443 us
  waiting for transfers between devices  178 us (40%)
  blocking collectives  112 us (25%)
  local copies, waits for them, and re-layouts  53.8 us (12%)
  other arithmetic  30.7 us (7%)
  starting transfers between devices  29.7 us (7%)
  matrix products  25.2 us (6%)
  between operations  14.2 us (3%)
    unnamed x8, waiting for transfers between devices  86.8 us
    reduce_scatter x2, waiting for transfers between devices, scatter_tensor(): return lax.psum_scatter(inner, 'tx', scatter_dimension=0, tiled=True)  42.7 us
    all_gather x3, blocking collectives, gather_tensor(): inner = lax.all_gather(block, 'tx', axis=axis, tiled=True)  41 us
    all_to_all x1, waiting for transfers between devices, per_device(): bank_all = lax.all_to_all(bank_send, 'adapter', 0, 0, tiled=True)  30.3 us
    psum x1, blocking collectives, small_total(): return lax.psum(inner, 'tz').astype(jnp.float32)  28.5 us
    all_gather x1, blocking collectives, gather_tensor(): return lax.all_gather(inner, 'tz', axis=axis, tiled=True)  25.8 us
    psum x1, blocking collectives, small_total(): inner = lax.psum(partial_value.astype(jnp.bfloat16), 'tx')  16.7 us
    unnamed x65, local copies, waits for them, and re-layouts  13.4 us
  transfers between devices with their start and end apart: 11, of which 8 were waited for; matrix products, arithmetic and copies ran while one was open for 11% of the time, Pallas kernels for 0%

profile of v2, /device:TPU:8, one launch (start us, length us, event | category | flops | bytes accessed | tf_op | source)
XLA Modules:
  0.0 443.1 jit_solution(16449099014106447579)
XLA Ops:
  6.5 14.6 %all_gather.18 = bf16[64,2880]{1,0:T(8,128)(2,1)} all-gather(bf16[16,2880]{1,0:T(8,128)(2,1)} %param.21), channel_id=1, replica_groups=mesh['tz'=8,'tx'=4,'adapter'=8] {'tx'}, dimensions={0}, use_global_device_ids=true | all-gather | bytes 460800 | tf_op jit(solution)/shard_map/all_gather | solution.py:111
  27.6 5.5 %all-to-all-start.1 = ((bf16[8,16,2880]{2,1,0:T(8,128)(2,1)}), bf16[8,16,2880]{2,1,0:T(8,128)(2,1)}, u32[]{:S(2)}, u32[]{:S(2)}) async-start(bf16[8,16,2880]{2,1,0:T(8,128)(2,1)} %broadcast_select_fusion.2), calls=%async_computation.1 | async-start | bytes 1507328 | tf_op jit(solution)/shard_map/all_to_all | solution.py:121
  35.4 2.6 gather_fusion.1
  38.7 1.1 reshape.818
  39.8 2.8 gather_fusion
  45.5 9.5 %all-to-all-start.3 = ((bf16[32,2,2048]{2,1,0:T(2,128)(2,1)}), bf16[32,2,2048]{2,1,0:T(2,128)(2,1)S(1)}, u32[]{:S(2)}, u32[]{:S(2)}) async-start(bf16[32,2,2048]{2,1,0:T(2,128)(2,1)} %reshape.818), calls=%async_computation.3 | async-start | bytes 524288 | tf_op jit(solution)/shard_map/all_to_all | solution.py:247
  55.1 2.6 fusion.22
  59.6 11.8 %all-to-all-done.3 = bf16[32,2,2048]{2,1,0:T(2,128)(2,1)S(1)} async-done(((bf16[32,2,2048]{2,1,0:T(2,128)(2,1)}), bf16[32,2,2048]{2,1,0:T(2,128)(2,1)S(1)}, u32[]{:S(2)}, u32[]{:S(2)}) %all-to-all-start.3) | async-done | bytes 262176 | tf_op jit(solution)/shard_map/all_to_all | solution.py:247
  71.5 4.8 %all-to-all-start.2 = ((bf16[8,2,384]{2,1,0:T(2,128)(2,1)}), bf16[8,2,384]{2,1,0:T(2,128)(2,1)S(1)}, u32[]{:S(2)}, u32[]{:S(2)}) async-start(bf16[8,2,384]{2,1,0:T(2,128)(2,1)} %reshape.816), calls=%async_computation.2 | async-start | bytes 24576 | tf_op jit(solution)/shard_map/all_to_all | solution.py:121
  76.4 1.5 copy.82
  77.8 2.4 all-to-all-done.2
  80.2 3.9 all-to-all-start
  84.8 1.2 fusion.17
  86.5 1.1 copy.89
  88.1 12.6 %all_gather.20 = bf16[64,48]{1,0:T(8,128)(2,1)S(1)} all-gather(bf16[16,48]{1,0:T(8,128)(2,1)S(1)} %reduce_sum.148), channel_id=1, replica_groups=mesh['tz'=8,'tx'=4,'adapter'=8] {'tx'}, dimensions={0}, use_global_device_ids=true | all-gather | bytes 7680 | tf_op jit(solution)/shard_map/all_gather | solution.py:111
  100.8 25.8 %all-gather = bf16[8,64,48]{1,2,0:T(8,128)(2,1)S(1)} all-gather(bf16[1,64,48]{1,2,0:T(8,128)(2,1)S(1)} %bitcast.156), channel_id=1, replica_groups=mesh['tz'=8,'tx'=4,'adapter'=8] {'tz'}, dimensions={0}, use_global_device_ids=true | all-gather | bytes 55296 | tf_op jit(solution)/shard_map/all_gather | solution.py:112
  126.8 1.1 convolution_bitcast_fusion
  128.9 1.7 copy.83
  130.6 2.2 fusion.128
  132.8 2.7 fusion
  139.5 1.1 convolution_add_fusion
  143.6 16.7 %psum.14 = bf16[512,16]{0,1:T(8,128)(2,1)S(1)} all-reduce(bf16[512,16]{0,1:T(8,128)(2,1)S(1)} %multiply_reduce_fusion.1), channel_id=1, replica_groups=mesh['tz'=8,'tx'=4,'adapter'=8] {'tx'}, use_global_device_ids=true, to_apply=%region_13.14 | all-reduce | flops 8192 | bytes 32768 | tf_op jit(solution)/shard_map/psum | solution.py:133
  160.3 28.5 %psum.15 = bf16[512,16]{0,1:T(8,128)(2,1)S(1)} all-reduce(bf16[512,16]{0,1:T(8,128)(2,1)S(1)} %psum.14), channel_id=1, replica_groups=mesh['tz'=8,'tx'=4,'adapter'=8] {'tz'}, use_global_device_ids=true, to_apply=%region_14.15 | all-reduce | flops 8192 | bytes 32768 | tf_op jit(solution)/shard_map/psum | solution.py:134
  190.0 2.6 fusion.4
  192.5 4.6 %copy.101 = bf16[512,2880]{1,0:T(8,128)(2,1)} copy(bf16[512,2880]{0,1:T(8,128)(2,1)} %fusion.4) | data formatting | bytes 5898240
  197.2 42.0 %reduce-scatter.13.cloned.1.call-done = bf16[64,2880]{1,0:T(8,128)(2,1)} async-done(((bf16[512,2880]{1,0:T(8,128)(2,1)}), bf16[64,2880]{1,0:T(8,128)(2,1)}) %reduce-scatter.13.cloned.1.call-update) | async-done | bytes 368656
  239.2 3.0 broadcast_in_dim.301
  242.2 5.6 %all-to-all-start.4 = ((bf16[8,8,16,2880]{3,2,1,0:T(8,128)(2,1)}), bf16[8,8,16,2880]{3,2,1,0:T(8,128)(2,1)}, u32[]{:S(2)}, u32[]{:S(2)}) async-start(bf16[8,8,16,2880]{3,2,1,0:T(8,128)(2,1)} %broadcast_in_dim.301), calls=%async_computation.4 | async-start | bytes 12058624 | tf_op jit(solution)/shard_map/all_to_all | solution.py:295
  247.8 17.1 %reduce-scatter.15.cloned.1.call-done = bf16[16,2880]{1,0:T(8,128)(2,1)} async-done(((bf16[64,2880]{1,0:T(8,128)(2,1)}), bf16[16,2880]{1,0:T(8,128)(2,1)}) %reduce-scatter.15.cloned.1.call-update) | async-done | bytes 92176 | tf_op jit(solution)/shard_map/reduce_scatter | solution.py:117
  264.9 13.8 %all_gather.22 = bf16[64,2880]{1,0:T(8,128)(2,1)} all-gather(bf16[16,2880]{1,0:T(8,128)(2,1)} %reduce-scatter.15.cloned.1.call-done), channel_id=1, replica_groups=mesh['tz'=8,'tx'=4,'adapter'=8] {'tx'}, dimensions={0}, use_global_device_ids=true | all-gather | bytes 460800 | tf_op jit(solution)/shard_map/all_gather | solution.py:111
  279.8 2.4 scatter_custom_fusion
  282.2 1.3 gather_fusion.3
  285.5 30.3 %all-to-all-done.4 = bf16[8,8,16,2880]{3,2,1,0:T(8,128)(2,1)} async-done(((bf16[8,8,16,2880]{3,2,1,0:T(8,128)(2,1)}), bf16[8,8,16,2880]{3,2,1,0:T(8,128)(2,1)}, u32[]{:S(2)}, u32[]{:S(2)}) %all-to-all-start.4) | async-done | bytes 5898272 | tf_op jit(solution)/shard_map/all_to_all | solution.py:295
  315.8 3.4 gather_fusion.6
  319.3 3.6 all-gather.6.cloned.1.call-done
  322.8 6.4 %convert_add_fusion = (f32[512,2880]{1,0:T(8,128)}, f32[512]{0:T(512)S(1)}) fusion(bf16[512,2880]{1,0:T(8,128)(2,1)} %all-gather.4.cloned.1.call-done, bf16[512,2880]{1,0:T(8,128)(2,1)} %all-gather.6.cloned.1.call-done), kind=kLoop, calls=%fused_computation.8 | loop fusion | flops 7372288 | bytes 11798528 | tf_op jit(solution)/shard_map/add | solution.py:288
  329.3 3.0 multiply_convert_fusion
  332.3 4.1 gather_fusion.2
  336.3 2.4 fusion.10
  338.7 3.6 fusion.50
  342.4 4.5 %gather_fusion.4 = f32[512,2880]{1,0:T(8,128)} fusion(f32[128,2880]{1,0:T(8,128)S(1)} %fusion.50, s32[1024]{0:T(1024)S(1)} %pad_clamp_fusion.2), kind=kCustom, calls=%fused_computation.4 | custom fusion | bytes 11798528 | tf_op jit(solution)/shard_map/jit(_take)/gather | solution.py:338
  346.9 6.4 %copy.95 = f32[512,2880]{0,1:T(8,128)} copy(f32[512,2880]{1,0:T(8,128)} %gather_fusion.4) | data formatting | bytes 11796480 | tf_op jit(solution)/shard_map/jit(_take)/gather | solution.py:338
  353.3 3.1 fusion.41
  356.9 2.6 fusion.3
  359.4 4.8 %copy.105 = bf16[512,2880]{1,0:T(8,128)(2,1)} copy(bf16[512,2880]{0,1:T(8,128)(2,1)} %fusion.3) | data formatting | bytes 5898240
  364.3 44.7 %reduce-scatter.17.cloned.1.call-done = bf16[64,2880]{1,0:T(8,128)(2,1)} async-done(((bf16[512,2880]{1,0:T(8,128)(2,1)}), bf16[64,2880]{1,0:T(8,128)(2,1)}) %reduce-scatter.17.cloned.1.call-update) | async-done | bytes 368656
  409.1 25.6 %reduce-scatter.19.cloned.1.call-done = bf16[16,2880]{1,0:T(8,128)(2,1)} async-done(((bf16[64,2880]{1,0:T(8,128)(2,1)}), bf16[16,2880]{1,0:T(8,128)(2,1)}) %reduce-scatter.19.cloned.1.call-update) | async-done | bytes 92176 | tf_op jit(solution)/shard_map/reduce_scatter | solution.py:117
  434.6 1.6 add_convert_fusion
  (160 shorter events, 28.7 us)
Async XLA Ops:
  6.5 48.5 %copy-start = (bf16[8,48,2880]{2,1,0:T(8,128)(2,1)S(1)}, bf16[8,48,2880]{2,1,0:T(8,128)(2,1)}, u32[]{:S(2)}) copy-start(bf16[8,48,2880]{2,1,0:T(8,128)(2,1)} %param.27) | copy-start | bytes 6635524
  6.5 28.2 %copy-start.3 = (s32[64]{0:T(128)S(1)}, s32[64]{0:T(128)}, u32[]{:S(2)}) copy-start(s32[64]{0:T(128)} %param.39) | copy-start | bytes 772
  6.5 28.8 %copy-start.4 = (bf16[64,2,16,2,8]{0,4,3,2,1:T(8,128)(2,1)S(1)}, bf16[64,2,16,2,8]{0,4,3,2,1:T(8,128)(2,1)}, u32[]{:S(2)}) copy-start(bf16[64,2,16,2,8]{0,4,3,2,1:T(8,128)(2,1)} %param.29) | copy-start | bytes 196612
  6.5 126.3 %all-gather.4.cloned.1.call-start = ((), (), s32[]{:S(2)}) async-start(), calls=%async_computation.9 | async-start | bytes 3391488 | tf_op jit(solution)/shard_map/all_gather | solution.py:112
  27.6 17.9 %all-to-all-start.1 = ((bf16[8,16,2880]{2,1,0:T(8,128)(2,1)}), bf16[8,16,2880]{2,1,0:T(8,128)(2,1)}, u32[]{:S(2)}, u32[]{:S(2)}) async-start(bf16[8,16,2880]{2,1,0:T(8,128)(2,1)} %broadcast_select_fusion.2), calls=%async_computation.1 | async-start | bytes 1507328 | tf_op jit(solution)/shard_map/all_to_all | solution.py:121
  38.0 1.8 copy-start.2
  45.5 30.8 %copy-start.10 = (bf16[32,2880,2,2]{1,0,3,2:T(8,128)(2,1)S(1)}, bf16[32,2880,2,2]{1,0,3,2:T(8,128)(2,1)}, u32[]{:S(2)}) copy-start(bf16[32,2880,2,2]{1,0,3,2:T(8,128)(2,1)} %broadcast_select_fusion) | copy-start | bytes 2211844
  45.5 26.0 %all-to-all-start.3 = ((bf16[32,2,2048]{2,1,0:T(2,128)(2,1)}), bf16[32,2,2048]{2,1,0:T(2,128)(2,1)S(1)}, u32[]{:S(2)}, u32[]{:S(2)}) async-start(bf16[32,2,2048]{2,1,0:T(2,128)(2,1)} %reshape.818), calls=%async_computation.3 | async-start | bytes 524288 | tf_op jit(solution)/shard_map/all_to_all | solution.py:247
  55.1 29.1 %copy-start.28 = (f32[2]{0:T(128)S(1)}, f32[2]{0:T(128)}, u32[]{:S(2)}) copy-start(f32[2]{0:T(128)} %param.26) | copy-start | bytes 28
  71.5 8.7 %all-to-all-start.2 = ((bf16[8,2,384]{2,1,0:T(2,128)(2,1)}), bf16[8,2,384]{2,1,0:T(2,128)(2,1)S(1)}, u32[]{:S(2)}, u32[]{:S(2)}) async-start(bf16[8,2,384]{2,1,0:T(2,128)(2,1)} %reshape.816), calls=%async_computation.2 | async-start | bytes 24576 | tf_op jit(solution)/shard_map/all_to_all | solution.py:121
  77.8 49.0 %copy-start.26 = (bf16[64,16,128]{2,1,0:T(8,128)(2,1)S(1)}, bf16[64,16,128]{2,1,0:T(8,128)(2,1)}, u32[]{:S(2)}) copy-start(bf16[64,16,128]{2,1,0:T(8,128)(2,1)} %param.28) | copy-start | bytes 786436
  80.2 47.9 %all-to-all-start = ((bf16[32,2880,2,2]{1,3,2,0:T(2,128)(2,1)}), bf16[32,2880,2,2]{1,3,2,0:T(2,128)(2,1)S(1)}, u32[]{:S(2)}, u32[]{:S(2)}) async-start(bf16[32,2880,2,2]{1,3,2,0:T(2,128)(2,1)} %copy.82), calls=%async_computation | async-start | bytes 1507328 | tf_op jit(solution)/shard_map/all_to_all | solution.py:242
  84.1 155.1 %reduce-scatter.13.cloned.1.call-start = ((), (), s32[]{:S(2)}) async-start(), calls=%async_computation.11 | async-start | bytes 3391488
  128.0 0.9 copy-start.9
  130.6 4.9 %copy-start.22 = (f32[2880]{0:T(1024)S(1)}, f32[2880]{0:T(1024)}, u32[]{:S(2)}) copy-start(f32[2880]{0:T(1024)} %param.22) | copy-start | bytes 34564
  132.8 2.8 copy-start.5
  135.6 1.1 copy-start.12
  136.6 1.2 copy-start.11
  137.7 1.7 copy-start.15
  137.8 1.7 copy-start.18
  139.1 1.6 copy-start.17
  140.6 1.2 copy-start.13
  142.2 1.0 copy-start.21
  142.2 1.0 copy-start.27
  142.2 46.7 %copy-start.19 = (bf16[2,16,2880]{2,1,0:T(8,128)(2,1)S(1)}, bf16[2,16,2880]{2,1,0:T(8,128)(2,1)}, u32[]{:S(2)}) copy-start(bf16[2,16,2880]{2,1,0:T(8,128)(2,1)} %param.31) | copy-start | bytes 552964
  188.9 1.1 copy-start.16
  197.1 42.1 %copy-start.14 = (bf16[8,16,2880]{2,1,0:T(8,128)(2,1)S(1)}, bf16[8,16,2880]{2,1,0:T(8,128)(2,1)}, u32[]{:S(2)}) copy-start(bf16[8,16,2880]{2,1,0:T(8,128)(2,1)} %param.35) | copy-start | bytes 2211844
  197.1 67.8 %reduce-scatter.15.cloned.1.call-start = ((), (), s32[]{:S(2)}) async-start(), calls=%async_computation.12 | async-start | bytes 471040 | tf_op jit(solution)/shard_map/reduce_scatter | solution.py:117
  242.2 36.8 %copy-start.24 = (f32[512,4]{0,1:T(4,128)S(1)}, f32[512,4]{0,1:T(4,128)}, u32[]{:S(2)}) copy-start(f32[512,4]{0,1:T(4,128)} %param.41) | copy-start | bytes 24580
  242.2 36.8 %copy-start.25 = (s32[512,4]{0,1:T(4,128)S(1)}, s32[512,4]{0,1:T(4,128)}, u32[]{:S(2)}) copy-start(s32[512,4]{0,1:T(4,128)} %param.40) | copy-start | bytes 24580
  242.2 73.6 %all-to-all-start.4 = ((bf16[8,8,16,2880]{3,2,1,0:T(8,128)(2,1)}), bf16[8,8,16,2880]{3,2,1,0:T(8,128)(2,1)}, u32[]{:S(2)}, u32[]{:S(2)}) async-start(bf16[8,8,16,2880]{3,2,1,0:T(8,128)(2,1)} %broadcast_in_dim.301), calls=%async_computation.4 | async-start | bytes 12058624 | tf_op jit(solution)/shard_map/all_to_all | solution.py:295
  247.8 75.0 %all-gather.6.cloned.1.call-start = ((), (), s32[]{:S(2)}) async-start(), calls=%async_computation.10 | async-start | bytes 3391488 | tf_op jit(solution)/shard_map/all_gather | solution.py:112
  278.7 130.3 %reduce-scatter.17.cloned.1.call-start = ((), (), s32[]{:S(2)}) async-start(), calls=%async_computation.13 | async-start | bytes 3391488
  319.3 10.0 %copy-start.23 = (f32[2880]{0:T(1024)S(1)}, f32[2880]{0:T(1024)}, u32[]{:S(2)}) copy-start(f32[2880]{0:T(1024)} %param.32) | copy-start | bytes 34564
  322.8 6.5 %copy-start.6 = (bf16[512,2880]{1,0:T(8,128)(2,1)S(1)}, bf16[512,2880]{1,0:T(8,128)(2,1)}, u32[]{:S(2)}) copy-start(bf16[512,2880]{1,0:T(8,128)(2,1)} %all-gather.4.cloned.1.call-done) | copy-start | bytes 8847364
  322.8 6.5 %copy-start.8 = (bf16[512,2880]{1,0:T(8,128)(2,1)S(1)}, bf16[512,2880]{1,0:T(8,128)(2,1)}, u32[]{:S(2)}) copy-start(bf16[512,2880]{1,0:T(8,128)(2,1)} %all-gather.6.cloned.1.call-done) | copy-start | bytes 8847364
  353.3 3.6 copy-start.7
  353.3 3.6 copy-start.20
  359.4 76.8 %copy-start.1 = (bf16[8,48,2880]{2,1,0:T(8,128)(2,1)S(1)}, bf16[8,48,2880]{2,1,0:T(8,128)(2,1)}, u32[]{:S(2)}) copy-start(bf16[8,48,2880]{2,1,0:T(8,128)(2,1)} %param.27) | copy-start | bytes 6635524
  364.3 70.4 %reduce-scatter.19.cloned.1.call-start = ((), (), s32[]{:S(2)}) async-start(), calls=%async_computation.14 | async-start | bytes 471040 | tf_op jit(solution)/shard_map/reduce_scatter | solution.py:117
Sparse Core Ops, SparseCore 0:
  21.3 51.2 all-gather.3
  197.2 41.8 reduce-scatter.12
  241.7 23.1 reduce-scatter.14
  278.9 43.9 all-gather.5
  364.4 44.6 reduce-scatter.16
  411.4 23.1 reduce-scatter.18

commit v3 on v2

--- a/solution.py
+++ b/solution.py
@@ -271,6 +271,12 @@
         segment,
         sink_logits,
     )
+    prompt_count = adapter_row.shape[0]
+    owner_count = lax.axis_size("adapter")
+    bank_send = jnp.broadcast_to(mixture_down[None], (owner_count,) + mixture_down.shape)
+    bank_all = lax.all_to_all(bank_send, "adapter", 0, 0, tiled=True)
+    bank_all = bank_all.reshape(-1, R, mixture_down.shape[-1])
+    bank_all, mixed_rows = lax.optimization_barrier((bank_all, mixed_rows))
     rank_table = output_down.reshape(adapter_count * R, query_cols)
     rank_terms = lax.dot_general(
         mixed_rows, rank_table, (((1,), (1,)), ((), ())), preferred_element_type=jnp.float32
@@ -289,11 +295,6 @@
     normed_two = rms_scale(hidden_all, gain_mixture)
     hidden_own = lax.dynamic_slice_in_dim(hidden_all, first_own, own_rows, 0)
     normed_two_own = lax.dynamic_slice_in_dim(normed_two, first_own, own_rows, 0)
-    prompt_count = adapter_row.shape[0]
-    owner_count = lax.axis_size("adapter")
-    bank_send = jnp.broadcast_to(mixture_down[None], (owner_count,) + mixture_down.shape)
-    bank_all = lax.all_to_all(bank_send, "adapter", 0, 0, tiled=True)
-    bank_all = bank_all.reshape(-1, R, mixture_down.shape[-1])
     bank_group = jnp.take(bank_all, jnp.take(adapter_slot, adapter_row), axis=0)
     moe_proj = lax.dot_general(
         normed_two,
@@ -311,32 +312,20 @@
     named = expert_ids == expert_here
     route_weight = jnp.sum(jnp.where(named, expert_weights, 0.0), axis=1)
     picked = jnp.any(named, axis=1)
-    capacity = group_rows * TOP // ROUTED * 2
-    order = jnp.cumsum(picked.astype(jnp.int32)) - 1
-    target = jnp.where(picked, order, capacity)
-    source = (
-        jnp.zeros((capacity,), jnp.int32)
-        .at[target]
-        .set(jnp.arange(group_rows, dtype=jnp.int32), mode="drop")
-    )
-    slot_used = jnp.arange(capacity, dtype=jnp.int32) < jnp.sum(picked.astype(jnp.int32))
-    compact_in = jnp.take(normed_two, source, axis=0)
-    compact_route = jnp.where(slot_used, jnp.take(route_weight, source, axis=0), 0.0)
-    gate_val = jnp.dot(compact_in, gate_up_weight[:, 0], preferred_element_type=jnp.float32)
-    lift_val = jnp.dot(compact_in, gate_up_weight[:, 1], preferred_element_type=jnp.float32)
+    gate_val = jnp.dot(normed_two, gate_up_weight[:, 0], preferred_element_type=jnp.float32)
+    lift_val = jnp.dot(normed_two, gate_up_weight[:, 1], preferred_element_type=jnp.float32)
     active = (
         (lift_val + 1.0)
         * gate_val
         * jax.nn.sigmoid(SWIGLU_ALPHA * gate_val)
-        * compact_route[:, None]
+        * route_weight[:, None]
     ).astype(jnp.bfloat16)
-    compact_terms = jnp.dot(active, down_weight, preferred_element_type=jnp.float32)
+    expert_terms = jnp.dot(active, down_weight, preferred_element_type=jnp.float32)
     spread_moe = spread_rank(local_hot, rank_moe)
     up_moe = mixture_up.reshape(local_count * R, -1)
 
     def moe_term(row_start, row_count):
-        expert_rows = jnp.take(compact_terms, jnp.clip(order, 0, capacity - 1), axis=0)
-        expert_rows = jnp.where(picked[:, None], expert_rows, 0.0)
+        expert_rows = jnp.where(picked[:, None], expert_terms, 0.0)
         return settle(expert_rows + jnp.dot(spread_moe, up_moe, preferred_element_type=jnp.float32))
 
     moe_own = partial_sum(moe_term, own_rows)

time: 445 us -> 497 us (1.12)
  waiting for transfers between devices: 178 us -> 246 us
  local copies, waits for them, and re-layouts: 53.8 us -> 34.9 us
  matrix products: 25.2 us -> 31.6 us
    all_gather x2, waiting for transfers between devices: 3.55 us -> 39.7 us  [gather_tensor(): return lax.all_gather(inner, 'tz', axis=axis, tiled=True)]
    all_to_all x1, waiting for transfers between devices: 30.3 us -> 53.8 us  [per_device(): bank_all = lax.all_to_all(bank_send, 'adapter', 0, 0, tiled=True)]
    gather x4 -> x0, local copies, waits for them, and re-layouts: 16.2 us -> none  [the longest x2 10.9 us: moe_term(): jnp.take(compact_terms, jnp.clip(order, 0, capacity - 1), axis=0)]
    reduce_scatter x2, waiting for transfers between devices: 42.7 us -> 51 us  [scatter_tensor(): return lax.psum_scatter(inner, 'tx', scatter_dimension=0, tiled=True)]
    dot_general x1, matrix products: 3.64 us -> 9.44 us  [per_device(): jnp.dot(active, down_weight, preferred_element_type=jnp.float32)]
    unnamed x65 -> x63, local copies, waits for them, and re-layouts: 13.4 us -> 12.1 us
where the time goes in v3:
time: 497 us; the launch traced here: 496 us
  waiting for transfers between devices  246 us (49%)
  blocking collectives  112 us (23%)
  local copies, waits for them, and re-layouts  34.9 us (7%)
  matrix products  31.6 us (6%)
  starting transfers between devices  30.2 us (6%)
  other arithmetic  27.4 us (6%)
  between operations  14.1 us (3%)
    unnamed x8, waiting for transfers between devices  87 us
    all_to_all x1, waiting for transfers between devices, per_device(): bank_all = lax.all_to_all(bank_send, 'adapter', 0, 0, tiled=True)  53.8 us
    reduce_scatter x2, waiting for transfers between devices, scatter_tensor(): return lax.psum_scatter(inner, 'tx', scatter_dimension=0, tiled=True)  51 us
    all_gather x3, blocking collectives, gather_tensor(): inner = lax.all_gather(block, 'tx', axis=axis, tiled=True)  40.6 us
    all_gather x2, waiting for transfers between devices, gather_tensor(): return lax.all_gather(inner, 'tz', axis=axis, tiled=True)  39.7 us
    psum x1, blocking collectives, small_total(): return lax.psum(inner, 'tz').astype(jnp.float32)  28.5 us
    all_gather x1, blocking collectives, gather_tensor(): return lax.all_gather(inner, 'tz', axis=axis, tiled=True)  25.9 us
    psum x1, blocking collectives, small_total(): inner = lax.psum(partial_value.astype(jnp.bfloat16), 'tx')  16.7 us
  transfers between devices with their start and end apart: 11, of which 8 were waited for; matrix products, arithmetic and copies ran while one was open for 11% of the time, Pallas kernels for 0%

profile of v3, /device:TPU:8, one launch (start us, length us, event | category | flops | bytes accessed | tf_op | source)
XLA Modules:
  0.0 495.7 jit_solution(7699175362204760890)
XLA Ops:
  6.5 14.6 %all_gather.18 = bf16[64,2880]{1,0:T(8,128)(2,1)} all-gather(bf16[16,2880]{1,0:T(8,128)(2,1)} %param.21), channel_id=1, replica_groups=mesh['tz'=8,'tx'=4,'adapter'=8] {'tx'}, dimensions={0}, use_global_device_ids=true | all-gather | bytes 460800 | tf_op jit(solution)/shard_map/all_gather | solution.py:111
  21.2 1.0 fusion.70
  26.6 1.0 broadcast_select_fusion.1
  27.6 5.5 %all-to-all-start.2 = ((bf16[8,16,2880]{2,1,0:T(8,128)(2,1)}), bf16[8,16,2880]{2,1,0:T(8,128)(2,1)}, u32[]{:S(2)}, u32[]{:S(2)}) async-start(bf16[8,16,2880]{2,1,0:T(8,128)(2,1)} %broadcast_select_fusion.1), calls=%async_computation.2 | async-start | bytes 1507328 | tf_op jit(solution)/shard_map/all_to_all | solution.py:121
  35.4 2.6 gather_fusion.1
  38.7 1.1 reshape.681
  39.8 2.8 gather_fusion
  44.4 1.0 broadcast_select_fusion
  45.5 9.5 %all-to-all-start.4 = ((bf16[32,2,2048]{2,1,0:T(2,128)(2,1)}), bf16[32,2,2048]{2,1,0:T(2,128)(2,1)S(1)}, u32[]{:S(2)}, u32[]{:S(2)}) async-start(bf16[32,2,2048]{2,1,0:T(2,128)(2,1)} %reshape.681), calls=%async_computation.4 | async-start | bytes 524288 | tf_op jit(solution)/shard_map/all_to_all | solution.py:247
  55.0 2.6 fusion.37
  59.6 11.8 %all-to-all-done.4 = bf16[32,2,2048]{2,1,0:T(2,128)(2,1)S(1)} async-done(((bf16[32,2,2048]{2,1,0:T(2,128)(2,1)}), bf16[32,2,2048]{2,1,0:T(2,128)(2,1)S(1)}, u32[]{:S(2)}, u32[]{:S(2)}) %all-to-all-start.4) | async-done | bytes 262176 | tf_op jit(solution)/shard_map/all_to_all | solution.py:247
  71.4 4.8 all-to-all-start.3
  76.3 1.5 copy.71
  77.8 2.4 all-to-all-done.3
  80.1 3.9 all-to-all-start.1
  84.8 1.2 fusion.17
  86.4 1.1 copy.78
  88.1 12.6 %all_gather.20 = bf16[64,48]{1,0:T(8,128)(2,1)S(1)} all-gather(bf16[16,48]{1,0:T(8,128)(2,1)S(1)} %reduce_sum.139), channel_id=1, replica_groups=mesh['tz'=8,'tx'=4,'adapter'=8] {'tx'}, dimensions={0}, use_global_device_ids=true | all-gather | bytes 7680 | tf_op jit(solution)/shard_map/all_gather | solution.py:111
  100.7 25.9 %all-gather = bf16[8,64,48]{1,2,0:T(8,128)(2,1)S(1)} all-gather(bf16[1,64,48]{1,2,0:T(8,128)(2,1)S(1)} %bitcast.148), channel_id=1, replica_groups=mesh['tz'=8,'tx'=4,'adapter'=8] {'tz'}, dimensions={0}, use_global_device_ids=true | all-gather | bytes 55296 | tf_op jit(solution)/shard_map/all_gather | solution.py:112
  126.8 1.1 convolution_bitcast_fusion
  128.0 4.4 broadcast_in_dim.230
  132.4 6.1 %all-to-all-start = ((bf16[8,8,16,2880]{3,2,1,0:T(8,128)(2,1)}), bf16[8,8,16,2880]{3,2,1,0:T(8,128)(2,1)}, u32[]{:S(2)}, u32[]{:S(2)}) async-start(bf16[8,8,16,2880]{3,2,1,0:T(8,128)(2,1)} %broadcast_in_dim.230), calls=%async_computation | async-start | bytes 12058624 | tf_op jit(solution)/shard_map/all_to_all | solution.py:277
  138.5 1.7 copy.72
  140.2 2.2 fusion.119
  142.4 2.7 fusion
  146.3 1.0 fusion.59
  148.0 1.1 convolution_add_fusion
  150.3 1.0 fusion.62
  152.7 53.8 %all-to-all-done = bf16[8,8,16,2880]{3,2,1,0:T(8,128)(2,1)} async-done(((bf16[8,8,16,2880]{3,2,1,0:T(8,128)(2,1)}), bf16[8,8,16,2880]{3,2,1,0:T(8,128)(2,1)}, u32[]{:S(2)}, u32[]{:S(2)}) %all-to-all-start) | async-done | bytes 5898272 | tf_op jit(solution)/shard_map/all_to_all | solution.py:277
  206.9 16.7 %psum.14 = bf16[512,16]{0,1:T(8,128)(2,1)S(1)} all-reduce(bf16[512,16]{0,1:T(8,128)(2,1)S(1)} %multiply_reduce_fusion.1), channel_id=1, replica_groups=mesh['tz'=8,'tx'=4,'adapter'=8] {'tx'}, use_global_device_ids=true, to_apply=%region_13.14 | all-reduce | flops 8192 | bytes 32768 | tf_op jit(solution)/shard_map/psum | solution.py:133
  223.6 28.5 %psum.15 = bf16[512,16]{0,1:T(8,128)(2,1)S(1)} all-reduce(bf16[512,16]{0,1:T(8,128)(2,1)S(1)} %psum.14), channel_id=1, replica_groups=mesh['tz'=8,'tx'=4,'adapter'=8] {'tz'}, use_global_device_ids=true, to_apply=%region_14.15 | all-reduce | flops 8192 | bytes 32768 | tf_op jit(solution)/shard_map/psum | solution.py:134
  253.2 2.5 fusion.4
  255.7 4.7 copy.90
  260.5 42.1 %reduce-scatter.13.cloned.1.call-done = bf16[64,2880]{1,0:T(8,128)(2,1)} async-done(((bf16[512,2880]{1,0:T(8,128)(2,1)}), bf16[64,2880]{1,0:T(8,128)(2,1)}) %reduce-scatter.13.cloned.1.call-update) | async-done | bytes 368656
  302.6 25.5 %reduce-scatter.15.cloned.1.call-done = bf16[16,2880]{1,0:T(8,128)(2,1)} async-done(((bf16[64,2880]{1,0:T(8,128)(2,1)}), bf16[16,2880]{1,0:T(8,128)(2,1)}) %reduce-scatter.15.cloned.1.call-update) | async-done | bytes 92176 | tf_op jit(solution)/shard_map/reduce_scatter | solution.py:117
  328.2 13.4 %all_gather.22 = bf16[64,2880]{1,0:T(8,128)(2,1)} all-gather(bf16[16,2880]{1,0:T(8,128)(2,1)} %reduce-scatter.15.cloned.1.call-done), channel_id=1, replica_groups=mesh['tz'=8,'tx'=4,'adapter'=8] {'tx'}, dimensions={0}, use_global_device_ids=true | all-gather | bytes 460800 | tf_op jit(solution)/shard_map/all_gather | solution.py:111
  342.7 3.4 gather_fusion.3
  346.1 39.7 %all-gather.6.cloned.1.call-done = bf16[512,2880]{1,0:T(8,128)(2,1)} async-done(((bf16[64,2880]{1,0:T(8,128)(2,1)}), bf16[512,2880]{1,0:T(8,128)(2,1)}) %all-gather.6.cloned.1.call-update) | async-done | bytes 2949136 | tf_op jit(solution)/shard_map/all_gather | solution.py:112
  385.8 6.4 %convert_add_fusion = (f32[512,2880]{1,0:T(8,128)}, f32[512]{0:T(512)S(1)}) fusion(bf16[512,2880]{1,0:T(8,128)(2,1)} %all-gather.4.cloned.1.call-done, bf16[512,2880]{1,0:T(8,128)(2,1)} %all-gather.6.cloned.1.call-done), kind=kLoop, calls=%fused_computation.4 | loop fusion | flops 7372288 | bytes 11798528 | tf_op jit(solution)/shard_map/add | solution.py:294
  392.3 1.4 multiply_convert_fusion
  393.8 4.0 fusion.10
  397.8 1.1 fusion.44
  399.0 3.5 fusion.89
  402.5 9.4 %fusion.3 = bf16[512,2880]{0,1:T(8,128)(2,1)} fusion(f32[512,2880,1]{0,1,2:T(8,128)} %fusion.89, bf16[360,2880]{1,0:T(8,128)(2,1)} %param.34, pred[512]{0:T(512)(128)(4,1)S(1)} %reduce_or.9, f32[512,360]{0,1:T(8,128)S(1)} %fusion.10, bf16[512,2880]{1,0:T(8,128)(2,1)} %copy-done.10, bf16[2880,2,360]{0,2,1:T(8,128)(2,1)} %param.33, f32[512]{0:T(512)S(1)} %get-tuple-element.36), kind=kOutput, calls=%fused_computation.13 | convolution fusion | flops 2129448960 | bytes 16841216 | tf_op jit(solution)/shard_map/dot_general | solution.py:323
  412.0 4.8 copy.94
  416.8 44.8 %reduce-scatter.17.cloned.1.call-done = bf16[64,2880]{1,0:T(8,128)(2,1)} async-done(((bf16[512,2880]{1,0:T(8,128)(2,1)}), bf16[64,2880]{1,0:T(8,128)(2,1)}) %reduce-scatter.17.cloned.1.call-update) | async-done | bytes 368656
  461.7 25.5 %reduce-scatter.19.cloned.1.call-done = bf16[16,2880]{1,0:T(8,128)(2,1)} async-done(((bf16[64,2880]{1,0:T(8,128)(2,1)}), bf16[16,2880]{1,0:T(8,128)(2,1)}) %reduce-scatter.19.cloned.1.call-update) | async-done | bytes 92176 | tf_op jit(solution)/shard_map/reduce_scatter | solution.py:117
  487.2 1.6 add_convert_fusion
  (140 shorter events, 20.3 us)
Async XLA Ops:
  6.5 48.5 %copy-start = (bf16[8,48,2880]{2,1,0:T(8,128)(2,1)S(1)}, bf16[8,48,2880]{2,1,0:T(8,128)(2,1)}, u32[]{:S(2)}) copy-start(bf16[8,48,2880]{2,1,0:T(8,128)(2,1)} %param.27) | copy-start | bytes 6635524
  6.5 28.2 %copy-start.3 = (s32[64]{0:T(128)S(1)}, s32[64]{0:T(128)}, u32[]{:S(2)}) copy-start(s32[64]{0:T(128)} %param.39) | copy-start | bytes 772
  6.5 28.8 %copy-start.4 = (bf16[64,2,16,2,8]{0,4,3,2,1:T(8,128)(2,1)S(1)}, bf16[64,2,16,2,8]{0,4,3,2,1:T(8,128)(2,1)}, u32[]{:S(2)}) copy-start(bf16[64,2,16,2,8]{0,4,3,2,1:T(8,128)(2,1)} %param.29) | copy-start | bytes 196612
  6.5 135.9 %all-gather.4.cloned.1.call-start = ((), (), s32[]{:S(2)}) async-start(), calls=%async_computation.9 | async-start | bytes 3391488 | tf_op jit(solution)/shard_map/all_gather | solution.py:112
  27.6 17.9 %all-to-all-start.2 = ((bf16[8,16,2880]{2,1,0:T(8,128)(2,1)}), bf16[8,16,2880]{2,1,0:T(8,128)(2,1)}, u32[]{:S(2)}, u32[]{:S(2)}) async-start(bf16[8,16,2880]{2,1,0:T(8,128)(2,1)} %broadcast_select_fusion.1), calls=%async_computation.2 | async-start | bytes 1507328 | tf_op jit(solution)/shard_map/all_to_all | solution.py:121
  38.0 1.8 copy-start.2
  45.5 30.8 %copy-start.9 = (bf16[32,2880,2,2]{1,0,3,2:T(8,128)(2,1)S(1)}, bf16[32,2880,2,2]{1,0,3,2:T(8,128)(2,1)}, u32[]{:S(2)}) copy-start(bf16[32,2880,2,2]{1,0,3,2:T(8,128)(2,1)} %broadcast_select_fusion) | copy-start | bytes 2211844
  45.5 26.0 %all-to-all-start.4 = ((bf16[32,2,2048]{2,1,0:T(2,128)(2,1)}), bf16[32,2,2048]{2,1,0:T(2,128)(2,1)S(1)}, u32[]{:S(2)}, u32[]{:S(2)}) async-start(bf16[32,2,2048]{2,1,0:T(2,128)(2,1)} %reshape.681), calls=%async_computation.4 | async-start | bytes 524288 | tf_op jit(solution)/shard_map/all_to_all | solution.py:247
  55.0 29.0 %copy-start.27 = (f32[2]{0:T(128)S(1)}, f32[2]{0:T(128)}, u32[]{:S(2)}) copy-start(f32[2]{0:T(128)} %param.26) | copy-start | bytes 28
  71.4 8.7 %all-to-all-start.3 = ((bf16[8,2,384]{2,1,0:T(2,128)(2,1)}), bf16[8,2,384]{2,1,0:T(2,128)(2,1)S(1)}, u32[]{:S(2)}, u32[]{:S(2)}) async-start(bf16[8,2,384]{2,1,0:T(2,128)(2,1)} %reshape.679), calls=%async_computation.3 | async-start | bytes 24576 | tf_op jit(solution)/shard_map/all_to_all | solution.py:121
  77.8 49.0 %copy-start.25 = (bf16[64,16,128]{2,1,0:T(8,128)(2,1)S(1)}, bf16[64,16,128]{2,1,0:T(8,128)(2,1)}, u32[]{:S(2)}) copy-start(bf16[64,16,128]{2,1,0:T(8,128)(2,1)} %param.28) | copy-start | bytes 786436
  80.1 47.9 %all-to-all-start.1 = ((bf16[32,2880,2,2]{1,3,2,0:T(2,128)(2,1)}), bf16[32,2880,2,2]{1,3,2,0:T(2,128)(2,1)S(1)}, u32[]{:S(2)}, u32[]{:S(2)}) async-start(bf16[32,2880,2,2]{1,3,2,0:T(2,128)(2,1)} %copy.71), calls=%async_computation.1 | async-start | bytes 1507328 | tf_op jit(solution)/shard_map/all_to_all | solution.py:242
  128.0 4.4 copy-start.8
  132.4 74.0 %all-to-all-start = ((bf16[8,8,16,2880]{3,2,1,0:T(8,128)(2,1)}), bf16[8,8,16,2880]{3,2,1,0:T(8,128)(2,1)}, u32[]{:S(2)}, u32[]{:S(2)}) async-start(bf16[8,8,16,2880]{3,2,1,0:T(8,128)(2,1)} %broadcast_in_dim.230), calls=%async_computation | async-start | bytes 12058624 | tf_op jit(solution)/shard_map/all_to_all | solution.py:277
  138.5 164.1 %reduce-scatter.13.cloned.1.call-start = ((), (), s32[]{:S(2)}) async-start(), calls=%async_computation.11 | async-start | bytes 3391488
  140.2 4.9 copy-start.21
  142.4 2.8 copy-start.5
  145.2 1.1 copy-start.12
  146.3 1.7 copy-start.14
  146.3 1.7 copy-start.17
  147.7 1.6 copy-start.16
  149.2 1.1 copy-start.11
  150.3 1.1 copy-start.13
  151.7 54.7 %copy-start.20 = (f32[512,64]{0,1:T(8,128)S(1)}, f32[512,64]{0,1:T(8,128)}, u32[]{:S(2)}) copy-start(f32[512,64]{0,1:T(8,128)} %get-tuple-element.58) | copy-start | bytes 393220
  151.7 54.7 %copy-start.26 = (bf16[64,16,128]{2,1,0:T(8,128)(2,1)S(1)}, bf16[64,16,128]{2,1,0:T(8,128)(2,1)}, u32[]{:S(2)}) copy-start(bf16[64,16,128]{2,1,0:T(8,128)(2,1)} %param.30) | copy-start | bytes 786436
  151.8 100.3 %copy-start.18 = (bf16[2,16,2880]{2,1,0:T(8,128)(2,1)S(1)}, bf16[2,16,2880]{2,1,0:T(8,128)(2,1)}, u32[]{:S(2)}) copy-start(bf16[2,16,2880]{2,1,0:T(8,128)(2,1)} %param.31) | copy-start | bytes 552964
  252.1 1.1 copy-start.15
  260.4 81.5 %copy-start.23 = (f32[512,4]{0,1:T(4,128)S(1)}, f32[512,4]{0,1:T(4,128)}, u32[]{:S(2)}) copy-start(f32[512,4]{0,1:T(4,128)} %param.41) | copy-start | bytes 24580
  260.4 81.5 %copy-start.24 = (s32[512,4]{0,1:T(4,128)S(1)}, s32[512,4]{0,1:T(4,128)}, u32[]{:S(2)}) copy-start(s32[512,4]{0,1:T(4,128)} %param.40) | copy-start | bytes 24580
  260.4 67.7 %reduce-scatter.15.cloned.1.call-start = ((), (), s32[]{:S(2)}) async-start(), calls=%async_computation.12 | async-start | bytes 471040 | tf_op jit(solution)/shard_map/reduce_scatter | solution.py:117
  302.6 83.2 %all-gather.6.cloned.1.call-start = ((), (), s32[]{:S(2)}) async-start(), calls=%async_computation.10 | async-start | bytes 3391488 | tf_op jit(solution)/shard_map/all_gather | solution.py:112
  341.6 120.1 %reduce-scatter.17.cloned.1.call-start = ((), (), s32[]{:S(2)}) async-start(), calls=%async_computation.13 | async-start | bytes 3391488
  346.1 46.2 %copy-start.22 = (f32[2880]{0:T(1024)S(1)}, f32[2880]{0:T(1024)}, u32[]{:S(2)}) copy-start(f32[2880]{0:T(1024)} %param.32) | copy-start | bytes 34564
  385.8 6.5 %copy-start.6 = (bf16[512,2880]{1,0:T(8,128)(2,1)S(1)}, bf16[512,2880]{1,0:T(8,128)(2,1)}, u32[]{:S(2)}) copy-start(bf16[512,2880]{1,0:T(8,128)(2,1)} %all-gather.4.cloned.1.call-done) | copy-start | bytes 8847364
  385.8 6.5 %copy-start.7 = (bf16[512,2880]{1,0:T(8,128)(2,1)S(1)}, bf16[512,2880]{1,0:T(8,128)(2,1)}, u32[]{:S(2)}) copy-start(bf16[512,2880]{1,0:T(8,128)(2,1)} %all-gather.6.cloned.1.call-done) | copy-start | bytes 8847364
  393.7 4.1 copy-start.10
  397.8 1.1 copy-start.19
  412.0 76.9 %copy-start.1 = (bf16[8,48,2880]{2,1,0:T(8,128)(2,1)S(1)}, bf16[8,48,2880]{2,1,0:T(8,128)(2,1)}, u32[]{:S(2)}) copy-start(bf16[8,48,2880]{2,1,0:T(8,128)(2,1)} %param.27) | copy-start | bytes 6635524
  416.8 70.4 %reduce-scatter.19.cloned.1.call-start = ((), (), s32[]{:S(2)}) async-start(), calls=%async_computation.14 | async-start | bytes 471040 | tf_op jit(solution)/shard_map/reduce_scatter | solution.py:117
Sparse Core Ops, SparseCore 0:
  21.3 51.1 all-gather.3
  260.5 41.9 reduce-scatter.12
  305.1 23.0 reduce-scatter.14
  341.7 44.0 all-gather.5
  416.9 44.7 reduce-scatter.16
  464.1 23.1 reduce-scatter.18

commit v4 on v3

--- a/solution.py
+++ b/solution.py
@@ -4,14 +4,13 @@
 import jax.numpy as jnp
 from jax import lax
 from jax.sharding import Mesh, PartitionSpec as P
+
 
 QH = 64
 KVH = 8
 HD = 64
 FF = 2880
 WINDOW = 128
-TOP = 4
-ROUTED = 32
 R = 16
 TENSOR = ("tz", "tx")
 
@@ -129,11 +128,6 @@
     return gather_tensor(scatter_tensor(partial_value.astype(jnp.bfloat16))).astype(jnp.float32)
 
 
-def small_total(partial_value):
-    inner = lax.psum(partial_value.astype(jnp.bfloat16), "tx")
-    return lax.psum(inner, "tz").astype(jnp.float32)
-
-
 def partial_sum(term_maker, own_rows):
     return scatter_tensor(
         term_maker(jnp.int32(0), tensor_size() * own_rows).astype(jnp.bfloat16)
@@ -181,7 +175,7 @@
     ).astype(jnp.bfloat16)
 
 
-def per_device(
+def layer(
     tokens,
     gain_attention,
     query_weight,
@@ -223,6 +217,11 @@
     local_hot = (adapter[:, None] == local_ids[None, :]).astype(jnp.bfloat16)
     normed_own = rms_scale(tokens, gain_attention)
     tokens_all = gather_tokens(tokens)
+    prompt_count = adapter_row.shape[0]
+    owned = (adapter_row // local_count) == tensor_here
+    up_pick = jnp.take(output_up, adapter_row % local_count, axis=0)
+    up_pick = jnp.where(owned[:, None, None], up_pick, jnp.zeros((), up_pick.dtype))
+    up_group = tensor_total(up_pick.reshape(prompt_count * R, -1)).astype(jnp.bfloat16)
     normed = rms_scale(tokens_all, gain_attention)
     rank_own = ask_owners(normed_own, heads_down, lengths, prompt_adapter, adapter_slot)
     rank_qkv = gather_tokens(rank_own)
@@ -271,12 +270,10 @@
         segment,
         sink_logits,
     )
-    prompt_count = adapter_row.shape[0]
     owner_count = lax.axis_size("adapter")
     bank_send = jnp.broadcast_to(mixture_down[None], (owner_count,) + mixture_down.shape)
     bank_all = lax.all_to_all(bank_send, "adapter", 0, 0, tiled=True)
     bank_all = bank_all.reshape(-1, R, mixture_down.shape[-1])
-    bank_all, mixed_rows = lax.optimization_barrier((bank_all, mixed_rows))
     rank_table = output_down.reshape(adapter_count * R, query_cols)
     rank_terms = lax.dot_general(
         mixed_rows, rank_table, (((1,), (1,)), ((), ())), preferred_element_type=jnp.float32
@@ -284,12 +281,20 @@
     rank_terms = jnp.sum(
         rank_terms.reshape(group_rows, adapter_count, R) * onehot[:, :, None], axis=1
     )
-    rank_out = small_total(settle(rank_terms)).astype(jnp.bfloat16)
-    spread_out = spread_rank(local_hot, rank_out)
-    up_out = output_up.reshape(local_count * R, -1)
+    prompt_hot = (segment[:, None] == jnp.arange(prompt_count, dtype=jnp.int32)[None, :]).astype(
+        jnp.bfloat16
+    )
+    spread_out = spread_rank(prompt_hot, settle(rank_terms).astype(jnp.bfloat16))
     term = jnp.dot(mixed_rows, output_weight, preferred_element_type=jnp.float32)
     attn_all = tensor_total(
-        settle(term + jnp.dot(spread_out, up_out, preferred_element_type=jnp.float32))
+        settle(
+            term
+            + jnp.dot(
+                spread_out,
+                up_group.reshape(prompt_count * R, -1),
+                preferred_element_type=jnp.float32,
+            )
+        )
     )
     hidden_all = tokens_all.astype(jnp.float32) + attn_all
     normed_two = rms_scale(hidden_all, gain_mixture)
@@ -366,6 +371,4 @@
         P("adapter", None),
     )
     out_specs = P(("adapter", "tz", "tx"), None)
-    return jax.shard_map(
-        per_device, mesh=mesh, in_specs=in_specs, out_specs=out_specs, check_vma=False
-    )
+    return jax.shard_map(layer, mesh=mesh, in_specs=in_specs, out_specs=out_specs, check_vma=False)

time: 497 us -> 457 us (0.920)
  waiting for transfers between devices: 246 us -> 215 us
  blocking collectives: 112 us -> 104 us
    psum x2 -> x0, blocking collectives: 45.2 us -> none  [the longest x1 28.5 us: small_total(): return lax.psum(inner, 'tz').astype(jnp.float32)]
    all_gather x2, waiting for transfers between devices: 39.7 us -> 3.51 us  [gather_tensor(): return lax.all_gather(inner, 'tz', axis=axis, tiled=True)]
    reduce_scatter x0 -> x1, waiting for transfers between devices: none -> 33.1 us  [scatter_tensor(): inner = lax.psum_scatter(block, 'tz', scatter_dimension=0, tiled=True)]
    all_gather x1 -> x2, blocking collectives: 25.9 us -> 52.4 us  [gather_tensor(): return lax.all_gather(inner, 'tz', axis=axis, tiled=True)]
    all_to_all x3, waiting for transfers between devices: 65.6 us -> 43.4 us  [the longest x1 36.5 us: layer(): bank_all = lax.all_to_all(bank_send, 'adapter', 0, 0, tiled=True)]
    all_gather x3 -> x4, blocking collectives: 40.6 us -> 51.9 us  [gather_tensor(): inner = lax.all_gather(block, 'tx', axis=axis, tiled=True)]
    reduce_scatter x2, waiting for transfers between devices: 51 us -> 42.8 us  [scatter_tensor(): return lax.psum_scatter(inner, 'tx', scatter_dimension=0, tiled=True)]
    unnamed x8 -> x11, waiting for transfers between devices: 87 us -> 89.9 us
  transfers between devices with their start and end apart: 11 -> 13, of which waited for: 8 -> 9; matrix products, arithmetic and copies ran while one was open for 11% -> 8% of each run, Pallas kernels for 0% -> 0%
where the time goes in v4:
time: 457 us; the launch traced here: 455 us
  waiting for transfers between devices  215 us (47%)
  blocking collectives  104 us (23%)
  local copies, waits for them, and re-layouts  38.3 us (8%)
  matrix products  31.6 us (7%)
  starting transfers between devices  27.9 us (6%)
  other arithmetic  23.3 us (5%)
  between operations  14.9 us (3%)
    unnamed x11, waiting for transfers between devices  89.9 us
    all_gather x2, blocking collectives, gather_tensor(): return lax.all_gather(inner, 'tz', axis=axis, tiled=True)  52.4 us
    all_gather x4, blocking collectives, gather_tensor(): inner = lax.all_gather(block, 'tx', axis=axis, tiled=True)  51.9 us
    reduce_scatter x2, waiting for transfers between devices, scatter_tensor(): return lax.psum_scatter(inner, 'tx', scatter_dimension=0, tiled=True)  42.8 us
    all_to_all x1, waiting for transfers between devices, layer(): bank_all = lax.all_to_all(bank_send, 'adapter', 0, 0, tiled=True)  36.5 us
    reduce_scatter x1, waiting for transfers between devices, scatter_tensor(): inner = lax.psum_scatter(block, 'tz', scatter_dimension=0, tiled=True)  33.1 us
    unnamed x84, local copies, waits for them, and re-layouts  14.5 us
    all_to_all x2, starting transfers between devices, swap_owner(): lax.all_to_all(outgoing, 'adapter', split_axis=0, concat_axis=0, tiled=True)  11.1 us
  transfers between devices with their start and end apart: 13, of which 9 were waited for; matrix products, arithmetic and copies ran while one was open for 8% of the time, Pallas kernels for 0%

profile of v4, /device:TPU:8, one launch (start us, length us, event | category | flops | bytes accessed | tf_op | source)
XLA Modules:
  0.0 455.4 jit_solution(6250854706287598537)
XLA Ops:
  7.5 1.3 gather_fusion.3
  10.2 1.6 gather_fusion.2
  11.8 1.1 fusion.52
  13.8 1.0 broadcast_select_fusion.1
  14.9 6.3 %all-to-all-start.1 = ((bf16[8,16,2880]{2,1,0:T(8,128)(2,1)}), bf16[8,16,2880]{2,1,0:T(8,128)(2,1)}, u32[]{:S(2)}, u32[]{:S(2)}) async-start(bf16[8,16,2880]{2,1,0:T(8,128)(2,1)} %broadcast_select_fusion.1), calls=%async_computation.1 | async-start | bytes 1507328 | tf_op jit(solution)/shard_map/all_to_all | solution.py:120
  21.1 33.1 %reduce-scatter.14.cloned.1.call-done = bf16[16,2880]{1,0:T(8,128)(2,1)} async-done(((bf16[128,2880]{1,0:T(8,128)(2,1)}), bf16[16,2880]{1,0:T(8,128)(2,1)}) %reduce-scatter.14.cloned.1.call-update) | async-done | bytes 92176 | tf_op jit(solution)/shard_map/reduce_scatter | solution.py:115
  54.3 13.5 %all_gather.24 = bf16[64,2880]{1,0:T(8,128)(2,1)} all-gather(bf16[16,2880]{1,0:T(8,128)(2,1)S(1)} %copy-done.14), channel_id=1, replica_groups=mesh['tz'=8,'tx'=4,'adapter'=8] {'tx'}, dimensions={0}, use_global_device_ids=true | all-gather | bytes 460800 | tf_op jit(solution)/shard_map/all_gather | solution.py:110
  68.2 2.6 gather_fusion.1
  71.5 1.1 reshape.807
  72.6 2.8 gather_fusion
  76.9 7.0 %all-to-all-start.3 = ((bf16[32,2,2048]{2,1,0:T(2,128)(2,1)}), bf16[32,2,2048]{2,1,0:T(2,128)(2,1)S(1)}, u32[]{:S(2)}, u32[]{:S(2)}) async-start(bf16[32,2,2048]{2,1,0:T(2,128)(2,1)} %reshape.807), calls=%async_computation.3 | async-start | bytes 524288 | tf_op jit(solution)/shard_map/all_to_all | solution.py:246
  83.9 2.6 fusion.36
  88.5 6.9 %all-to-all-done.3 = bf16[32,2,2048]{2,1,0:T(2,128)(2,1)S(1)} async-done(((bf16[32,2,2048]{2,1,0:T(2,128)(2,1)}), bf16[32,2,2048]{2,1,0:T(2,128)(2,1)S(1)}, u32[]{:S(2)}, u32[]{:S(2)}) %all-to-all-start.3) | async-done | bytes 262176 | tf_op jit(solution)/shard_map/all_to_all | solution.py:246
  95.4 4.8 %all-to-all-start.2 = ((bf16[8,2,384]{2,1,0:T(2,128)(2,1)}), bf16[8,2,384]{2,1,0:T(2,128)(2,1)S(1)}, u32[]{:S(2)}, u32[]{:S(2)}) async-start(bf16[8,2,384]{2,1,0:T(2,128)(2,1)} %reshape.805), calls=%async_computation.2 | async-start | bytes 24576 | tf_op jit(solution)/shard_map/all_to_all | solution.py:120
  100.3 1.5 copy.74
  101.7 2.4 all-to-all-done.2
  104.1 3.9 all-to-all-start
  110.5 1.2 fusion.16
  112.1 1.1 copy.81
  113.8 12.6 %all_gather.26 = bf16[64,48]{1,0:T(8,128)(2,1)S(1)} all-gather(bf16[16,48]{1,0:T(8,128)(2,1)S(1)} %reduce_sum.139), channel_id=1, replica_groups=mesh['tz'=8,'tx'=4,'adapter'=8] {'tx'}, dimensions={0}, use_global_device_ids=true | all-gather | bytes 7680 | tf_op jit(solution)/shard_map/all_gather | solution.py:110
  126.4 26.4 %all-gather = bf16[8,64,48]{1,2,0:T(8,128)(2,1)S(1)} all-gather(bf16[1,64,48]{1,2,0:T(8,128)(2,1)S(1)} %bitcast.162), channel_id=1, replica_groups=mesh['tz'=8,'tx'=4,'adapter'=8] {'tz'}, dimensions={0}, use_global_device_ids=true | all-gather | bytes 55296 | tf_op jit(solution)/shard_map/all_gather | solution.py:111
  153.0 1.1 convolution_bitcast_fusion
  155.1 1.7 copy.75
  156.8 2.2 fusion.116
  159.8 11.9 %all-gather.1 = bf16[4,4,2880]{2,1,0:T(4,128)(2,1)S(1)} all-gather(bf16[1,4,2880]{2,1,0:T(4,128)(2,1)S(1)} %dynamic-slice_bitcast_fusion), channel_id=1, replica_groups=mesh['tz'=8,'tx'=4,'adapter'=8] {'tx'}, dimensions={0}, use_global_device_ids=true | all-gather | bytes 115200 | tf_op jit(solution)/shard_map/all_gather | solution.py:110
  171.8 26.0 %all_gather.29 = bf16[128,2880]{1,0:T(8,128)(2,1)S(1)} all-gather(bf16[16,2880]{1,0:T(8,128)(2,1)S(1)} %reshape.789), channel_id=1, replica_groups=mesh['tz'=8,'tx'=4,'adapter'=8] {'tz'}, dimensions={0}, use_global_device_ids=true | all-gather | bytes 829440 | tf_op jit(solution)/shard_map/all_gather | solution.py:111
  197.8 2.7 fusion
  204.5 1.1 convolution_add_fusion
  209.8 2.5 add_convert_fusion
  212.3 4.6 %copy.93 = bf16[512,2880]{1,0:T(8,128)(2,1)} copy(bf16[512,2880]{0,1:T(8,128)(2,1)} %add_convert_fusion) | data formatting | bytes 5898240
  217.0 44.9 %reduce-scatter.16.cloned.1.call-done = bf16[64,2880]{1,0:T(8,128)(2,1)} async-done(((bf16[512,2880]{1,0:T(8,128)(2,1)}), bf16[64,2880]{1,0:T(8,128)(2,1)}) %reduce-scatter.16.cloned.1.call-update) | async-done | bytes 368656
  261.9 3.0 broadcast_in_dim.297
  264.9 5.5 %all-to-all-start.4 = ((bf16[8,8,16,2880]{3,2,1,0:T(8,128)(2,1)}), bf16[8,8,16,2880]{3,2,1,0:T(8,128)(2,1)}, u32[]{:S(2)}, u32[]{:S(2)}) async-start(bf16[8,8,16,2880]{3,2,1,0:T(8,128)(2,1)} %broadcast_in_dim.297), calls=%async_computation.5 | async-start | bytes 12058624 | tf_op jit(solution)/shard_map/all_to_all | solution.py:275
  270.4 17.1 %reduce-scatter.18.cloned.1.call-done = bf16[16,2880]{1,0:T(8,128)(2,1)} async-done(((bf16[64,2880]{1,0:T(8,128)(2,1)}), bf16[16,2880]{1,0:T(8,128)(2,1)}) %reduce-scatter.18.cloned.1.call-update) | async-done | bytes 92176 | tf_op jit(solution)/shard_map/reduce_scatter | solution.py:116
  287.5 13.9 %all_gather.30 = bf16[64,2880]{1,0:T(8,128)(2,1)} all-gather(bf16[16,2880]{1,0:T(8,128)(2,1)} %reduce-scatter.18.cloned.1.call-done), channel_id=1, replica_groups=mesh['tz'=8,'tx'=4,'adapter'=8] {'tx'}, dimensions={0}, use_global_device_ids=true | all-gather | bytes 460800 | tf_op jit(solution)/shard_map/all_gather | solution.py:110
  301.8 36.5 %all-to-all-done.4 = bf16[8,8,16,2880]{3,2,1,0:T(8,128)(2,1)} async-done(((bf16[8,8,16,2880]{3,2,1,0:T(8,128)(2,1)}), bf16[8,8,16,2880]{3,2,1,0:T(8,128)(2,1)}, u32[]{:S(2)}, u32[]{:S(2)}) %all-to-all-start.4) | async-done | bytes 5898272 | tf_op jit(solution)/shard_map/all_to_all | solution.py:275
  338.4 3.4 gather_fusion.4
  341.8 3.5 all-gather.7.cloned.1.call-done
  345.3 6.5 %convert_add_fusion = (f32[512,2880]{1,0:T(8,128)}, f32[512]{0:T(512)S(1)}) fusion(bf16[512,2880]{1,0:T(8,128)(2,1)} %all-gather.5.cloned.1.call-done, bf16[512,2880]{1,0:T(8,128)(2,1)} %all-gather.7.cloned.1.call-done), kind=kLoop, calls=%fused_computation.5 | loop fusion | flops 7372288 | bytes 11798528 | tf_op jit(solution)/shard_map/add | solution.py:299
  351.8 1.4 multiply_convert_fusion
  353.3 4.0 fusion.9
  357.4 1.1 fusion.43
  358.5 3.5 fusion.88
  362.0 9.4 %fusion.3 = bf16[512,2880]{0,1:T(8,128)(2,1)} fusion(f32[512,2880,1]{0,1,2:T(8,128)} %fusion.88, bf16[360,2880]{1,0:T(8,128)(2,1)} %param.34, pred[512]{0:T(512)(128)(4,1)S(1)} %reduce_or.9, f32[512,360]{0,1:T(8,128)S(1)} %fusion.9, bf16[512,2880]{1,0:T(8,128)(2,1)} %copy-done.10, bf16[2880,2,360]{0,2,1:T(8,128)(2,1)} %param.33, f32[512]{0:T(512)S(1)} %get-tuple-element.22), kind=kOutput, calls=%fused_computation.14 | convolution fusion | flops 2129448960 | bytes 16841216 | tf_op jit(solution)/shard_map/dot_general | solution.py:328
  371.5 4.8 %copy.97 = bf16[512,2880]{1,0:T(8,128)(2,1)} copy(bf16[512,2880]{0,1:T(8,128)(2,1)} %fusion.3) | data formatting | bytes 5898240
  376.3 44.9 %reduce-scatter.20.cloned.1.call-done = bf16[64,2880]{1,0:T(8,128)(2,1)} async-done(((bf16[512,2880]{1,0:T(8,128)(2,1)}), bf16[64,2880]{1,0:T(8,128)(2,1)}) %reduce-scatter.20.cloned.1.call-update) | async-done | bytes 368656
  421.2 25.7 %reduce-scatter.22.cloned.1.call-done = bf16[16,2880]{1,0:T(8,128)(2,1)} async-done(((bf16[64,2880]{1,0:T(8,128)(2,1)}), bf16[16,2880]{1,0:T(8,128)(2,1)}) %reduce-scatter.22.cloned.1.call-update) | async-done | bytes 92176 | tf_op jit(solution)/shard_map/reduce_scatter | solution.py:116
  447.0 1.6 add_convert_fusion.1
  (175 shorter events, 21.1 us)
Async XLA Ops:
  6.5 77.3 %copy-start = (bf16[8,48,2880]{2,1,0:T(8,128)(2,1)S(1)}, bf16[8,48,2880]{2,1,0:T(8,128)(2,1)}, u32[]{:S(2)}) copy-start(bf16[8,48,2880]{2,1,0:T(8,128)(2,1)} %param.27) | copy-start | bytes 6635524
  6.5 6.7 %copy-start.27 = (s32[8,8]{1,0:T(8,128)S(1)}, s32[8,8]{1,0:T(8,128)}, u32[]{:S(2)}) copy-start(s32[8,8]{1,0:T(8,128)} %param.38) | copy-start | bytes 772
  6.5 6.8 %copy-start.3 = (s32[64]{0:T(128)S(1)}, s32[64]{0:T(128)}, u32[]{:S(2)}) copy-start(s32[64]{0:T(128)} %param.39) | copy-start | bytes 772
  6.5 6.4 %copy-start.14 = (bf16[16,2880]{1,0:T(8,128)(2,1)S(1)}, bf16[16,2880]{1,0:T(8,128)(2,1)}, u32[]{:S(2)}) copy-start(bf16[16,2880]{1,0:T(8,128)(2,1)} %param.21) | copy-start | bytes 276484
  6.5 6.5 %copy-start.23 = (s32[8,8]{1,0:T(8,128)S(1)}, s32[8,8]{1,0:T(8,128)}, u32[]{:S(2)}) copy-start(s32[8,8]{1,0:T(8,128)} %param.37) | copy-start | bytes 772
  6.5 7.2 %copy-start.22 = (f32[2880]{0:T(1024)S(1)}, f32[2880]{0:T(1024)}, u32[]{:S(2)}) copy-start(f32[2880]{0:T(1024)} %param.22) | copy-start | bytes 34564
  6.6 47.7 %reduce-scatter.14.cloned.1.call-start = ((), (), s32[]{:S(2)}) async-start(), calls=%async_computation.11 | async-start | bytes 847872 | tf_op jit(solution)/shard_map/reduce_scatter | solution.py:115
  11.8 56.4 %copy-start.4 = (bf16[64,2,16,2,8]{0,4,3,2,1:T(8,128)(2,1)S(1)}, bf16[64,2,16,2,8]{0,4,3,2,1:T(8,128)(2,1)}, u32[]{:S(2)}) copy-start(bf16[64,2,16,2,8]{0,4,3,2,1:T(8,128)(2,1)} %param.29) | copy-start | bytes 196612
  14.9 62.0 %all-to-all-start.1 = ((bf16[8,16,2880]{2,1,0:T(8,128)(2,1)}), bf16[8,16,2880]{2,1,0:T(8,128)(2,1)}, u32[]{:S(2)}, u32[]{:S(2)}) async-start(bf16[8,16,2880]{2,1,0:T(8,128)(2,1)} %broadcast_select_fusion.1), calls=%async_computation.1 | async-start | bytes 1507328 | tf_op jit(solution)/shard_map/all_to_all | solution.py:120
  21.1 137.9 %all-reduce.6.cloned.1.call-start = ((), (), s32[]{:S(2)}) async-start(), calls=%async_computation.17 | async-start | bytes 188416
  54.3 143.6 %all-gather.5.cloned.1.call-start = ((), (), s32[]{:S(2)}) async-start(), calls=%async_computation.10 | async-start | bytes 3391488 | tf_op jit(solution)/shard_map/all_gather | solution.py:111
  70.8 1.8 copy-start.2
  75.5 11.0 %copy-start.28 = (f32[32]{0:T(128)}, f32[32]{0:T(128)S(1)}, u32[]{:S(2)}) copy-start(f32[32]{0:T(128)S(1)} %multiply_exponential_fusion) | copy-start | bytes 388
  76.9 23.4 %copy-start.9 = (bf16[32,2880,2,2]{1,0,3,2:T(8,128)(2,1)S(1)}, bf16[32,2880,2,2]{1,0,3,2:T(8,128)(2,1)}, u32[]{:S(2)}) copy-start(bf16[32,2880,2,2]{1,0,3,2:T(8,128)(2,1)} %broadcast_select_fusion) | copy-start | bytes 2211844
  76.9 18.5 %all-to-all-start.3 = ((bf16[32,2,2048]{2,1,0:T(2,128)(2,1)}), bf16[32,2,2048]{2,1,0:T(2,128)(2,1)S(1)}, u32[]{:S(2)}, u32[]{:S(2)}) async-start(bf16[32,2,2048]{2,1,0:T(2,128)(2,1)} %reshape.807), calls=%async_computation.3 | async-start | bytes 524288 | tf_op jit(solution)/shard_map/all_to_all | solution.py:246
  83.9 24.2 %copy-start.35 = (f32[2]{0:T(128)S(1)}, f32[2]{0:T(128)}, u32[]{:S(2)}) copy-start(f32[2]{0:T(128)} %param.26) | copy-start | bytes 28
  86.5 22.1 %copy-start.36 = (u32[256]{0:T(256)S(1)}, u32[256]{0:T(256)}, u32[]{:S(2)}) copy-start(u32[256]{0:T(256)} %constant.220) | copy-start | bytes 3076
  95.4 8.7 %all-to-all-start.2 = ((bf16[8,2,384]{2,1,0:T(2,128)(2,1)}), bf16[8,2,384]{2,1,0:T(2,128)(2,1)S(1)}, u32[]{:S(2)}, u32[]{:S(2)}) async-start(bf16[8,2,384]{2,1,0:T(2,128)(2,1)} %reshape.805), calls=%async_computation.2 | async-start | bytes 24576 | tf_op jit(solution)/shard_map/all_to_all | solution.py:120
  101.7 51.3 %copy-start.33 = (bf16[64,16,128]{2,1,0:T(8,128)(2,1)S(1)}, bf16[64,16,128]{2,1,0:T(8,128)(2,1)}, u32[]{:S(2)}) copy-start(bf16[64,16,128]{2,1,0:T(8,128)(2,1)} %param.28) | copy-start | bytes 786436
  104.1 50.1 %all-to-all-start = ((bf16[32,2880,2,2]{1,3,2,0:T(2,128)(2,1)}), bf16[32,2880,2,2]{1,3,2,0:T(2,128)(2,1)S(1)}, u32[]{:S(2)}, u32[]{:S(2)}) async-start(bf16[32,2880,2,2]{1,3,2,0:T(2,128)(2,1)} %copy.74), calls=%async_computation | async-start | bytes 1507328 | tf_op jit(solution)/shard_map/all_to_all | solution.py:241
  108.0 153.9 %reduce-scatter.16.cloned.1.call-start = ((), (), s32[]{:S(2)}) async-start(), calls=%async_computation.13 | async-start | bytes 3391488
  197.8 2.8 copy-start.5
  200.6 1.1 copy-start.12
  201.6 1.2 copy-start.11
  202.8 1.4 copy-start.29
  202.8 1.7 copy-start.16
  202.8 1.7 copy-start.19
  204.2 1.6 copy-start.18
  205.7 1.1 copy-start.31
  205.7 1.2 copy-start.13
  207.2 1.0 copy-start.34
  208.7 1.1 copy-start.17
  216.9 45.0 %copy-start.15 = (bf16[8,16,2880]{2,1,0:T(8,128)(2,1)S(1)}, bf16[8,16,2880]{2,1,0:T(8,128)(2,1)}, u32[]{:S(2)}) copy-start(bf16[8,16,2880]{2,1,0:T(8,128)(2,1)} %param.35) | copy-start | bytes 2211844
  217.0 70.5 %reduce-scatter.18.cloned.1.call-start = ((), (), s32[]{:S(2)}) async-start(), calls=%async_computation.14 | async-start | bytes 471040 | tf_op jit(solution)/shard_map/reduce_scatter | solution.py:116
  264.9 36.7 %copy-start.25 = (f32[512,4]{0,1:T(4,128)S(1)}, f32[512,4]{0,1:T(4,128)}, u32[]{:S(2)}) copy-start(f32[512,4]{0,1:T(4,128)} %param.41) | copy-start | bytes 24580
  264.9 36.7 %copy-start.26 = (s32[512,4]{0,1:T(4,128)S(1)}, s32[512,4]{0,1:T(4,128)}, u32[]{:S(2)}) copy-start(s32[512,4]{0,1:T(4,128)} %param.40) | copy-start | bytes 24580
  264.9 36.8 %copy-start.30 = (s32[8]{0:T(128)S(1)}, s32[8]{0:T(128)}, u32[]{:S(2)}) copy-start(s32[8]{0:T(128)} %get-tuple-element.60) | copy-start | bytes 100
  264.9 73.4 %all-to-all-start.4 = ((bf16[8,8,16,2880]{3,2,1,0:T(8,128)(2,1)}), bf16[8,8,16,2880]{3,2,1,0:T(8,128)(2,1)}, u32[]{:S(2)}, u32[]{:S(2)}) async-start(bf16[8,8,16,2880]{3,2,1,0:T(8,128)(2,1)} %broadcast_in_dim.297), calls=%async_computation.5 | async-start | bytes 12058624 | tf_op jit(solution)/shard_map/all_to_all | solution.py:275
  270.4 74.9 %all-gather.7.cloned.1.call-start = ((), (), s32[]{:S(2)}) async-start(), calls=%async_computation.12 | async-start | bytes 3391488 | tf_op jit(solution)/shard_map/all_gather | solution.py:111
  301.4 119.8 %reduce-scatter.20.cloned.1.call-start = ((), (), s32[]{:S(2)}) async-start(), calls=%async_computation.15 | async-start | bytes 3391488
  341.8 10.0 %copy-start.24 = (f32[2880]{0:T(1024)S(1)}, f32[2880]{0:T(1024)}, u32[]{:S(2)}) copy-start(f32[2880]{0:T(1024)} %param.32) | copy-start | bytes 34564
  345.3 6.5 %copy-start.6 = (bf16[512,2880]{1,0:T(8,128)(2,1)S(1)}, bf16[512,2880]{1,0:T(8,128)(2,1)}, u32[]{:S(2)}) copy-start(bf16[512,2880]{1,0:T(8,128)(2,1)} %all-gather.5.cloned.1.call-done) | copy-start | bytes 8847364
  345.3 6.5 %copy-start.7 = (bf16[512,2880]{1,0:T(8,128)(2,1)S(1)}, bf16[512,2880]{1,0:T(8,128)(2,1)}, u32[]{:S(2)}) copy-start(bf16[512,2880]{1,0:T(8,128)(2,1)} %all-gather.7.cloned.1.call-done) | copy-start | bytes 8847364
  353.3 4.1 copy-start.10
  353.3 4.1 copy-start.32
  357.4 1.1 copy-start.20
  371.5 77.1 %copy-start.1 = (bf16[8,48,2880]{2,1,0:T(8,128)(2,1)S(1)}, bf16[8,48,2880]{2,1,0:T(8,128)(2,1)}, u32[]{:S(2)}) copy-start(bf16[8,48,2880]{2,1,0:T(8,128)(2,1)} %param.27) | copy-start | bytes 6635524
  376.3 70.7 %reduce-scatter.22.cloned.1.call-start = ((), (), s32[]{:S(2)}) async-start(), calls=%async_computation.16 | async-start | bytes 471040 | tf_op jit(solution)/shard_map/reduce_scatter | solution.py:116
  (2 other events, 1.8 us)
Sparse Core Ops, SparseCore 0:
  13.1 41.1 reduce-scatter.13
  56.6 45.0 all-reduce.5
  103.4 54.1 all-gather.4
  217.1 44.7 reduce-scatter.15
  264.3 23.1 reduce-scatter.17
  301.5 43.7 all-gather.6
  376.4 44.7 reduce-scatter.19
  423.8 23.1 reduce-scatter.21

commit v5 on v3

--- a/solution.py
+++ b/solution.py
@@ -10,8 +10,6 @@
 HD = 64
 FF = 2880
 WINDOW = 128
-TOP = 4
-ROUTED = 32
 R = 16
 TENSOR = ("tz", "tx")
 
@@ -181,7 +179,7 @@
     ).astype(jnp.bfloat16)
 
 
-def per_device(
+def layer(
     tokens,
     gain_attention,
     query_weight,
@@ -276,7 +274,6 @@
     bank_send = jnp.broadcast_to(mixture_down[None], (owner_count,) + mixture_down.shape)
     bank_all = lax.all_to_all(bank_send, "adapter", 0, 0, tiled=True)
     bank_all = bank_all.reshape(-1, R, mixture_down.shape[-1])
-    bank_all, mixed_rows = lax.optimization_barrier((bank_all, mixed_rows))
     rank_table = output_down.reshape(adapter_count * R, query_cols)
     rank_terms = lax.dot_general(
         mixed_rows, rank_table, (((1,), (1,)), ((), ())), preferred_element_type=jnp.float32
@@ -366,6 +363,4 @@
         P("adapter", None),
     )
     out_specs = P(("adapter", "tz", "tx"), None)
-    return jax.shard_map(
-        per_device, mesh=mesh, in_specs=in_specs, out_specs=out_specs, check_vma=False
-    )
+    return jax.shard_map(layer, mesh=mesh, in_specs=in_specs, out_specs=out_specs, check_vma=False)

time: 497 us -> 434 us (0.87)
  waiting for transfers between devices: 246 us -> 184 us
    all_gather x2, waiting for transfers between devices: 39.7 us -> 3.86 us  [gather_tensor(): return lax.all_gather(inner, 'tz', axis=axis, tiled=True)]
    all_to_all x3, waiting for transfers between devices: 65.6 us -> 47.5 us  [the longest x1 35.7 us: layer(): bank_all = lax.all_to_all(bank_send, 'adapter', 0, 0, tiled=True)]
    reduce_scatter x2, waiting for transfers between devices: 51 us -> 43.2 us  [scatter_tensor(): return lax.psum_scatter(inner, 'tx', scatter_dimension=0, tiled=True)]
    unnamed x63 -> x65, local copies, waits for them, and re-layouts: 12.1 us -> 12.9 us
  transfers between devices with their start and end apart: 11 -> 11, of which waited for: 8 -> 8; matrix products, arithmetic and copies ran while one was open for 11% -> 10% of each run, Pallas kernels for 0% -> 0%
where the time goes in v5:
time: 434 us; the launch traced here: 433 us
  waiting for transfers between devices  184 us (42%)
  blocking collectives  112 us (26%)
  local copies, waits for them, and re-layouts  34.5 us (8%)
  matrix products  31.6 us (7%)
  starting transfers between devices  29.3 us (7%)
  other arithmetic  27.4 us (6%)
  between operations  14.1 us (3%)
    unnamed x8, waiting for transfers between devices  87 us
    reduce_scatter x2, waiting for transfers between devices, scatter_tensor(): return lax.psum_scatter(inner, 'tx', scatter_dimension=0, tiled=True)  43.2 us
    all_gather x3, blocking collectives, gather_tensor(): inner = lax.all_gather(block, 'tx', axis=axis, tiled=True)  40.9 us
    all_to_all x1, waiting for transfers between devices, layer(): bank_all = lax.all_to_all(bank_send, 'adapter', 0, 0, tiled=True)  35.7 us
    psum x1, blocking collectives, small_total(): return lax.psum(inner, 'tz').astype(jnp.float32)  28.5 us
    all_gather x1, blocking collectives, gather_tensor(): return lax.all_gather(inner, 'tz', axis=axis, tiled=True)  25.8 us
    psum x1, blocking collectives, small_total(): inner = lax.psum(partial_value.astype(jnp.bfloat16), 'tx')  16.7 us
    unnamed x65, local copies, waits for them, and re-layouts  12.9 us
  transfers between devices with their start and end apart: 11, of which 8 were waited for; matrix products, arithmetic and copies ran while one was open for 10% of the time, Pallas kernels for 0%

profile of v5, /device:TPU:8, one launch (start us, length us, event | category | flops | bytes accessed | tf_op | source)
XLA Modules:
  0.0 432.8 jit_solution(6728106027886407060)
XLA Ops:
  6.5 14.6 %all_gather.18 = bf16[64,2880]{1,0:T(8,128)(2,1)} all-gather(bf16[16,2880]{1,0:T(8,128)(2,1)} %param.21), channel_id=1, replica_groups=mesh['tz'=8,'tx'=4,'adapter'=8] {'tx'}, dimensions={0}, use_global_device_ids=true | all-gather | bytes 460800 | tf_op jit(solution)/shard_map/all_gather | solution.py:109
  21.2 1.0 fusion.70
  26.6 1.0 broadcast_select_fusion.1
  27.6 5.5 %all-to-all-start.1 = ((bf16[8,16,2880]{2,1,0:T(8,128)(2,1)}), bf16[8,16,2880]{2,1,0:T(8,128)(2,1)}, u32[]{:S(2)}, u32[]{:S(2)}) async-start(bf16[8,16,2880]{2,1,0:T(8,128)(2,1)} %broadcast_select_fusion.1), calls=%async_computation.1 | async-start | bytes 1507328 | tf_op jit(solution)/shard_map/all_to_all | solution.py:119
  35.4 2.6 gather_fusion.1
  38.7 1.1 reshape.681
  39.8 2.8 gather_fusion
  44.5 1.0 broadcast_select_fusion
  45.5 9.5 %all-to-all-start.3 = ((bf16[32,2,2048]{2,1,0:T(2,128)(2,1)}), bf16[32,2,2048]{2,1,0:T(2,128)(2,1)S(1)}, u32[]{:S(2)}, u32[]{:S(2)}) async-start(bf16[32,2,2048]{2,1,0:T(2,128)(2,1)} %reshape.681), calls=%async_computation.3 | async-start | bytes 524288 | tf_op jit(solution)/shard_map/all_to_all | solution.py:245
  55.1 2.6 fusion.37
  59.6 11.8 %all-to-all-done.3 = bf16[32,2,2048]{2,1,0:T(2,128)(2,1)S(1)} async-done(((bf16[32,2,2048]{2,1,0:T(2,128)(2,1)}), bf16[32,2,2048]{2,1,0:T(2,128)(2,1)S(1)}, u32[]{:S(2)}, u32[]{:S(2)}) %all-to-all-start.3) | async-done | bytes 262176 | tf_op jit(solution)/shard_map/all_to_all | solution.py:245
  71.5 4.8 %all-to-all-start.2 = ((bf16[8,2,384]{2,1,0:T(2,128)(2,1)}), bf16[8,2,384]{2,1,0:T(2,128)(2,1)S(1)}, u32[]{:S(2)}, u32[]{:S(2)}) async-start(bf16[8,2,384]{2,1,0:T(2,128)(2,1)} %reshape.679), calls=%async_computation.2 | async-start | bytes 24576 | tf_op jit(solution)/shard_map/all_to_all | solution.py:119
  76.4 1.5 copy.71
  77.8 2.4 all-to-all-done.2
  80.2 3.9 all-to-all-start
  84.9 1.2 fusion.17
  86.5 1.1 copy.78
  88.2 12.6 %all_gather.20 = bf16[64,48]{1,0:T(8,128)(2,1)S(1)} all-gather(bf16[16,48]{1,0:T(8,128)(2,1)S(1)} %reduce_sum.139), channel_id=1, replica_groups=mesh['tz'=8,'tx'=4,'adapter'=8] {'tx'}, dimensions={0}, use_global_device_ids=true | all-gather | bytes 7680 | tf_op jit(solution)/shard_map/all_gather | solution.py:109
  100.8 25.8 %all-gather = bf16[8,64,48]{1,2,0:T(8,128)(2,1)S(1)} all-gather(bf16[1,64,48]{1,2,0:T(8,128)(2,1)S(1)} %bitcast.148), channel_id=1, replica_groups=mesh['tz'=8,'tx'=4,'adapter'=8] {'tz'}, dimensions={0}, use_global_device_ids=true | all-gather | bytes 55296 | tf_op jit(solution)/shard_map/all_gather | solution.py:110
  126.8 1.1 convolution_bitcast_fusion
  128.9 1.7 copy.72
  130.6 2.2 fusion.118
  132.8 2.7 fusion
  136.7 1.0 fusion.59
  137.8 1.0 fusion.62
  139.5 1.2 convolution_add_fusion
  143.7 16.7 %psum.14 = bf16[512,16]{0,1:T(8,128)(2,1)S(1)} all-reduce(bf16[512,16]{0,1:T(8,128)(2,1)S(1)} %multiply_reduce_fusion.1), channel_id=1, replica_groups=mesh['tz'=8,'tx'=4,'adapter'=8] {'tx'}, use_global_device_ids=true, to_apply=%region_13.14 | all-reduce | flops 8192 | bytes 32768 | tf_op jit(solution)/shard_map/psum | solution.py:131
  160.3 28.5 %psum.15 = bf16[512,16]{0,1:T(8,128)(2,1)S(1)} all-reduce(bf16[512,16]{0,1:T(8,128)(2,1)S(1)} %psum.14), channel_id=1, replica_groups=mesh['tz'=8,'tx'=4,'adapter'=8] {'tz'}, use_global_device_ids=true, to_apply=%region_14.15 | all-reduce | flops 8192 | bytes 32768 | tf_op jit(solution)/shard_map/psum | solution.py:132
  190.0 2.6 fusion.4
  192.5 4.6 %copy.90 = bf16[512,2880]{1,0:T(8,128)(2,1)} copy(bf16[512,2880]{0,1:T(8,128)(2,1)} %fusion.4) | data formatting | bytes 5898240
  197.2 42.1 %reduce-scatter.13.cloned.1.call-done = bf16[64,2880]{1,0:T(8,128)(2,1)} async-done(((bf16[512,2880]{1,0:T(8,128)(2,1)}), bf16[64,2880]{1,0:T(8,128)(2,1)}) %reduce-scatter.13.cloned.1.call-update) | async-done | bytes 368656
  239.4 3.0 broadcast_in_dim.255
  242.4 5.1 %all-to-all-start.4 = ((bf16[8,8,16,2880]{3,2,1,0:T(8,128)(2,1)}), bf16[8,8,16,2880]{3,2,1,0:T(8,128)(2,1)}, u32[]{:S(2)}, u32[]{:S(2)}) async-start(bf16[8,8,16,2880]{3,2,1,0:T(8,128)(2,1)} %broadcast_in_dim.255), calls=%async_computation.4 | async-start | bytes 12058624 | tf_op jit(solution)/shard_map/all_to_all | solution.py:275
  247.5 17.4 %reduce-scatter.15.cloned.1.call-done = bf16[16,2880]{1,0:T(8,128)(2,1)} async-done(((bf16[64,2880]{1,0:T(8,128)(2,1)}), bf16[16,2880]{1,0:T(8,128)(2,1)}) %reduce-scatter.15.cloned.1.call-update) | async-done | bytes 92176 | tf_op jit(solution)/shard_map/reduce_scatter | solution.py:115
  265.0 13.7 %all_gather.22 = bf16[64,2880]{1,0:T(8,128)(2,1)} all-gather(bf16[16,2880]{1,0:T(8,128)(2,1)} %reduce-scatter.15.cloned.1.call-done), channel_id=1, replica_groups=mesh['tz'=8,'tx'=4,'adapter'=8] {'tx'}, dimensions={0}, use_global_device_ids=true | all-gather | bytes 460800 | tf_op jit(solution)/shard_map/all_gather | solution.py:109
  279.8 35.7 %all-to-all-done.4 = bf16[8,8,16,2880]{3,2,1,0:T(8,128)(2,1)} async-done(((bf16[8,8,16,2880]{3,2,1,0:T(8,128)(2,1)}), bf16[8,8,16,2880]{3,2,1,0:T(8,128)(2,1)}, u32[]{:S(2)}, u32[]{:S(2)}) %all-to-all-start.4) | async-done | bytes 5898272 | tf_op jit(solution)/shard_map/all_to_all | solution.py:275
  315.5 3.4 gather_fusion.3
  318.9 3.9 all-gather.6.cloned.1.call-done
  322.8 6.4 %convert_add_fusion = (f32[512,2880]{1,0:T(8,128)}, f32[512]{0:T(512)S(1)}) fusion(bf16[512,2880]{1,0:T(8,128)(2,1)} %all-gather.4.cloned.1.call-done, bf16[512,2880]{1,0:T(8,128)(2,1)} %all-gather.6.cloned.1.call-done), kind=kLoop, calls=%fused_computation.4 | loop fusion | flops 7372288 | bytes 11798528 | tf_op jit(solution)/shard_map/add | solution.py:291
  329.3 1.4 multiply_convert_fusion
  330.7 4.0 fusion.10
  334.8 1.1 fusion.44
  336.0 3.5 fusion.88
  339.5 9.4 %fusion.3 = bf16[512,2880]{0,1:T(8,128)(2,1)} fusion(f32[512,2880,1]{0,1,2:T(8,128)} %fusion.88, bf16[360,2880]{1,0:T(8,128)(2,1)} %param.34, pred[512]{0:T(512)(128)(4,1)S(1)} %reduce_or.9, f32[512,360]{0,1:T(8,128)S(1)} %fusion.10, bf16[512,2880]{1,0:T(8,128)(2,1)} %copy-done.10, bf16[2880,2,360]{0,2,1:T(8,128)(2,1)} %param.33, f32[512]{0:T(512)S(1)} %get-tuple-element.22), kind=kOutput, calls=%fused_computation.13 | convolution fusion | flops 2129448960 | bytes 16841216 | tf_op jit(solution)/shard_map/dot_general | solution.py:320
  348.9 4.8 %copy.94 = bf16[512,2880]{1,0:T(8,128)(2,1)} copy(bf16[512,2880]{0,1:T(8,128)(2,1)} %fusion.3) | data formatting | bytes 5898240
  353.8 44.7 %reduce-scatter.17.cloned.1.call-done = bf16[64,2880]{1,0:T(8,128)(2,1)} async-done(((bf16[512,2880]{1,0:T(8,128)(2,1)}), bf16[64,2880]{1,0:T(8,128)(2,1)}) %reduce-scatter.17.cloned.1.call-update) | async-done | bytes 368656
  398.6 25.7 %reduce-scatter.19.cloned.1.call-done = bf16[16,2880]{1,0:T(8,128)(2,1)} async-done(((bf16[64,2880]{1,0:T(8,128)(2,1)}), bf16[16,2880]{1,0:T(8,128)(2,1)}) %reduce-scatter.19.cloned.1.call-update) | async-done | bytes 92176 | tf_op jit(solution)/shard_map/reduce_scatter | solution.py:115
  424.3 1.6 add_convert_fusion
  (142 shorter events, 21.2 us)
Async XLA Ops:
  6.5 48.5 %copy-start = (bf16[8,48,2880]{2,1,0:T(8,128)(2,1)S(1)}, bf16[8,48,2880]{2,1,0:T(8,128)(2,1)}, u32[]{:S(2)}) copy-start(bf16[8,48,2880]{2,1,0:T(8,128)(2,1)} %param.27) | copy-start | bytes 6635524
  6.5 28.2 %copy-start.3 = (s32[64]{0:T(128)S(1)}, s32[64]{0:T(128)}, u32[]{:S(2)}) copy-start(s32[64]{0:T(128)} %param.39) | copy-start | bytes 772
  6.5 28.8 %copy-start.4 = (bf16[64,2,16,2,8]{0,4,3,2,1:T(8,128)(2,1)S(1)}, bf16[64,2,16,2,8]{0,4,3,2,1:T(8,128)(2,1)}, u32[]{:S(2)}) copy-start(bf16[64,2,16,2,8]{0,4,3,2,1:T(8,128)(2,1)} %param.29) | copy-start | bytes 196612
  6.5 126.3 %all-gather.4.cloned.1.call-start = ((), (), s32[]{:S(2)}) async-start(), calls=%async_computation.9 | async-start | bytes 3391488 | tf_op jit(solution)/shard_map/all_gather | solution.py:110
  27.6 17.9 %all-to-all-start.1 = ((bf16[8,16,2880]{2,1,0:T(8,128)(2,1)}), bf16[8,16,2880]{2,1,0:T(8,128)(2,1)}, u32[]{:S(2)}, u32[]{:S(2)}) async-start(bf16[8,16,2880]{2,1,0:T(8,128)(2,1)} %broadcast_select_fusion.1), calls=%async_computation.1 | async-start | bytes 1507328 | tf_op jit(solution)/shard_map/all_to_all | solution.py:119
  38.0 1.8 copy-start.2
  45.5 30.9 %copy-start.9 = (bf16[32,2880,2,2]{1,0,3,2:T(8,128)(2,1)S(1)}, bf16[32,2880,2,2]{1,0,3,2:T(8,128)(2,1)}, u32[]{:S(2)}) copy-start(bf16[32,2880,2,2]{1,0,3,2:T(8,128)(2,1)} %broadcast_select_fusion) | copy-start | bytes 2211844
  45.5 26.0 %all-to-all-start.3 = ((bf16[32,2,2048]{2,1,0:T(2,128)(2,1)}), bf16[32,2,2048]{2,1,0:T(2,128)(2,1)S(1)}, u32[]{:S(2)}, u32[]{:S(2)}) async-start(bf16[32,2,2048]{2,1,0:T(2,128)(2,1)} %reshape.681), calls=%async_computation.3 | async-start | bytes 524288 | tf_op jit(solution)/shard_map/all_to_all | solution.py:245
  55.0 29.1 %copy-start.28 = (f32[2]{0:T(128)S(1)}, f32[2]{0:T(128)}, u32[]{:S(2)}) copy-start(f32[2]{0:T(128)} %param.26) | copy-start | bytes 28
  71.5 8.7 %all-to-all-start.2 = ((bf16[8,2,384]{2,1,0:T(2,128)(2,1)}), bf16[8,2,384]{2,1,0:T(2,128)(2,1)S(1)}, u32[]{:S(2)}, u32[]{:S(2)}) async-start(bf16[8,2,384]{2,1,0:T(2,128)(2,1)} %reshape.679), calls=%async_computation.2 | async-start | bytes 24576 | tf_op jit(solution)/shard_map/all_to_all | solution.py:119
  77.8 49.0 %copy-start.26 = (bf16[64,16,128]{2,1,0:T(8,128)(2,1)S(1)}, bf16[64,16,128]{2,1,0:T(8,128)(2,1)}, u32[]{:S(2)}) copy-start(bf16[64,16,128]{2,1,0:T(8,128)(2,1)} %param.28) | copy-start | bytes 786436
  80.2 47.9 %all-to-all-start = ((bf16[32,2880,2,2]{1,3,2,0:T(2,128)(2,1)}), bf16[32,2880,2,2]{1,3,2,0:T(2,128)(2,1)S(1)}, u32[]{:S(2)}, u32[]{:S(2)}) async-start(bf16[32,2880,2,2]{1,3,2,0:T(2,128)(2,1)} %copy.71), calls=%async_computation | async-start | bytes 1507328 | tf_op jit(solution)/shard_map/all_to_all | solution.py:240
  84.1 155.2 %reduce-scatter.13.cloned.1.call-start = ((), (), s32[]{:S(2)}) async-start(), calls=%async_computation.11 | async-start | bytes 3391488
  128.0 0.9 copy-start.8
  130.6 4.9 %copy-start.22 = (f32[2880]{0:T(1024)S(1)}, f32[2880]{0:T(1024)}, u32[]{:S(2)}) copy-start(f32[2880]{0:T(1024)} %param.22) | copy-start | bytes 34564
  132.8 2.8 copy-start.5
  135.6 1.1 copy-start.12
  136.6 1.2 copy-start.11
  137.8 1.7 copy-start.15
  137.8 1.7 copy-start.18
  139.2 1.6 copy-start.17
  140.7 1.2 copy-start.13
  142.2 1.0 copy-start.21
  142.2 1.0 copy-start.27
  142.2 46.7 %copy-start.19 = (bf16[2,16,2880]{2,1,0:T(8,128)(2,1)S(1)}, bf16[2,16,2880]{2,1,0:T(8,128)(2,1)}, u32[]{:S(2)}) copy-start(bf16[2,16,2880]{2,1,0:T(8,128)(2,1)} %param.31) | copy-start | bytes 552964
  188.9 1.1 copy-start.16
  197.1 42.2 %copy-start.14 = (bf16[8,16,2880]{2,1,0:T(8,128)(2,1)S(1)}, bf16[8,16,2880]{2,1,0:T(8,128)(2,1)}, u32[]{:S(2)}) copy-start(bf16[8,16,2880]{2,1,0:T(8,128)(2,1)} %param.35) | copy-start | bytes 2211844
  197.1 67.9 %reduce-scatter.15.cloned.1.call-start = ((), (), s32[]{:S(2)}) async-start(), calls=%async_computation.12 | async-start | bytes 471040 | tf_op jit(solution)/shard_map/reduce_scatter | solution.py:115
  242.4 36.6 %copy-start.24 = (f32[512,4]{0,1:T(4,128)S(1)}, f32[512,4]{0,1:T(4,128)}, u32[]{:S(2)}) copy-start(f32[512,4]{0,1:T(4,128)} %param.41) | copy-start | bytes 24580
  242.4 36.6 %copy-start.25 = (s32[512,4]{0,1:T(4,128)S(1)}, s32[512,4]{0,1:T(4,128)}, u32[]{:S(2)}) copy-start(s32[512,4]{0,1:T(4,128)} %param.40) | copy-start | bytes 24580
  242.4 73.1 %all-to-all-start.4 = ((bf16[8,8,16,2880]{3,2,1,0:T(8,128)(2,1)}), bf16[8,8,16,2880]{3,2,1,0:T(8,128)(2,1)}, u32[]{:S(2)}, u32[]{:S(2)}) async-start(bf16[8,8,16,2880]{3,2,1,0:T(8,128)(2,1)} %broadcast_in_dim.255), calls=%async_computation.4 | async-start | bytes 12058624 | tf_op jit(solution)/shard_map/all_to_all | solution.py:275
  247.5 75.3 %all-gather.6.cloned.1.call-start = ((), (), s32[]{:S(2)}) async-start(), calls=%async_computation.10 | async-start | bytes 3391488 | tf_op jit(solution)/shard_map/all_gather | solution.py:110
  278.7 119.8 %reduce-scatter.17.cloned.1.call-start = ((), (), s32[]{:S(2)}) async-start(), calls=%async_computation.13 | async-start | bytes 3391488
  318.9 10.3 %copy-start.23 = (f32[2880]{0:T(1024)S(1)}, f32[2880]{0:T(1024)}, u32[]{:S(2)}) copy-start(f32[2880]{0:T(1024)} %param.32) | copy-start | bytes 34564
  322.8 6.5 %copy-start.6 = (bf16[512,2880]{1,0:T(8,128)(2,1)S(1)}, bf16[512,2880]{1,0:T(8,128)(2,1)}, u32[]{:S(2)}) copy-start(bf16[512,2880]{1,0:T(8,128)(2,1)} %all-gather.4.cloned.1.call-done) | copy-start | bytes 8847364
  322.8 6.5 %copy-start.7 = (bf16[512,2880]{1,0:T(8,128)(2,1)S(1)}, bf16[512,2880]{1,0:T(8,128)(2,1)}, u32[]{:S(2)}) copy-start(bf16[512,2880]{1,0:T(8,128)(2,1)} %all-gather.6.cloned.1.call-done) | copy-start | bytes 8847364
  330.7 4.1 copy-start.10
  334.8 1.1 copy-start.20
  348.9 77.0 %copy-start.1 = (bf16[8,48,2880]{2,1,0:T(8,128)(2,1)S(1)}, bf16[8,48,2880]{2,1,0:T(8,128)(2,1)}, u32[]{:S(2)}) copy-start(bf16[8,48,2880]{2,1,0:T(8,128)(2,1)} %param.27) | copy-start | bytes 6635524
  353.8 70.5 %reduce-scatter.19.cloned.1.call-start = ((), (), s32[]{:S(2)}) async-start(), calls=%async_computation.14 | async-start | bytes 471040 | tf_op jit(solution)/shard_map/reduce_scatter | solution.py:115
Sparse Core Ops, SparseCore 0:
  21.3 51.2 all-gather.3
  197.3 42.0 reduce-scatter.12
  241.9 23.0 reduce-scatter.14
  278.8 43.9 all-gather.5
  353.9 44.6 reduce-scatter.16
  400.9 23.3 reduce-scatter.18

commit v6 on v5

--- a/solution.py
+++ b/solution.py
@@ -31,10 +31,6 @@
     prompt_begin = jnp.sum(jnp.where(member, prompt_starts[None, :], 0), axis=1)
     adapter = jnp.sum(jnp.where(member, adapter_row[None, :], 0), axis=1)
     return (segment, token_index - prompt_begin, adapter)
-
-
-def settle(values):
-    return lax.optimization_barrier(values.astype(jnp.bfloat16)).astype(jnp.float32)
 
 
 def rms_scale(row_block, gain):
@@ -124,7 +120,9 @@
 
 
 def tensor_total(partial_value):
-    return gather_tensor(scatter_tensor(partial_value.astype(jnp.bfloat16))).astype(jnp.float32)
+    inner = lax.psum_scatter(partial_value.astype(jnp.bfloat16), "tz", scatter_dimension=0, tiled=True)
+    inner = lax.psum(inner, "tx")
+    return lax.all_gather(inner, "tz", axis=0, tiled=True).astype(jnp.float32)
 
 
 def small_total(partial_value):
@@ -281,12 +279,12 @@
     rank_terms = jnp.sum(
         rank_terms.reshape(group_rows, adapter_count, R) * onehot[:, :, None], axis=1
     )
-    rank_out = small_total(settle(rank_terms)).astype(jnp.bfloat16)
+    rank_out = small_total(rank_terms).astype(jnp.bfloat16)
     spread_out = spread_rank(local_hot, rank_out)
     up_out = output_up.reshape(local_count * R, -1)
     term = jnp.dot(mixed_rows, output_weight, preferred_element_type=jnp.float32)
     attn_all = tensor_total(
-        settle(term + jnp.dot(spread_out, up_out, preferred_element_type=jnp.float32))
+        term + jnp.dot(spread_out, up_out, preferred_element_type=jnp.float32)
     )
     hidden_all = tokens_all.astype(jnp.float32) + attn_all
     normed_two = rms_scale(hidden_all, gain_mixture)
@@ -323,7 +321,7 @@
 
     def moe_term(row_start, row_count):
         expert_rows = jnp.where(picked[:, None], expert_terms, 0.0)
-        return settle(expert_rows + jnp.dot(spread_moe, up_moe, preferred_element_type=jnp.float32))
+        return expert_rows + jnp.dot(spread_moe, up_moe, preferred_element_type=jnp.float32)
 
     moe_own = partial_sum(moe_term, own_rows)
     return (hidden_own + moe_own).astype(jnp.bfloat16)

time: 434 us -> 437 us (level)
  waiting for transfers between devices: 184 us -> 209 us
  blocking collectives: 112 us -> 98.3 us
  local copies, waits for them, and re-layouts: 34.5 us -> 25.1 us
    unnamed x8 -> x6, waiting for transfers between devices: 87 us -> 0.1 us
    reduce_scatter x0 -> x2, waiting for transfers between devices: none -> 86.8 us  [the longest x1 44.7 us: scatter_tensor(): inner = lax.psum_scatter(block, 'tz', scatter_dimension=0, tiled=True)]
    psum x0 -> x1, waiting for transfers between devices: none -> 40.8 us  [tensor_total(): inner = lax.psum(inner, 'tx')]
    reduce_scatter x2 -> x1, waiting for transfers between devices: 43.2 us -> 25.7 us  [scatter_tensor(): return lax.psum_scatter(inner, 'tx', scatter_dimension=0, tiled=True)]
    all_gather x0 -> x1, waiting for transfers between devices: none -> 15.6 us  [tensor_total(): return lax.all_gather(inner, 'tz', axis=0, tiled=True).astype(jnp.float32)]
    all_gather x3 -> x2, blocking collectives: 40.9 us -> 27.2 us  [gather_tensor(): inner = lax.all_gather(block, 'tx', axis=axis, tiled=True)]
    all_to_all x1, waiting for transfers between devices: 35.7 us -> 26.1 us  [layer(): bank_all = lax.all_to_all(bank_send, 'adapter', 0, 0, tiled=True)]
    unnamed x65 -> x63, local copies, waits for them, and re-layouts: 12.9 us -> 3.57 us
  transfers between devices with their start and end apart: 11 -> 11, of which waited for: 8 -> 8; matrix products, arithmetic and copies ran while one was open for 10% -> 9% of each run, Pallas kernels for 0% -> 0%
where the time goes in v6:
time: 437 us; the launch traced here: 436 us
  waiting for transfers between devices  209 us (48%)
  blocking collectives  98.3 us (22%)
  matrix products  32.1 us (7%)
  starting transfers between devices  29.3 us (7%)
  other arithmetic  27.4 us (6%)
  local copies, waits for them, and re-layouts  25.1 us (6%)
  between operations  14.1 us (3%)
    reduce_scatter x1, waiting for transfers between devices, scatter_tensor(): inner = lax.psum_scatter(block, 'tz', scatter_dimension=0, tiled=True)  44.7 us
    reduce_scatter x1, waiting for transfers between devices, tensor_total(): lax.psum_scatter(partial_value.astype(jnp.bfloat16), 'tz', scatter_dimens...  42.1 us
    psum x1, waiting for transfers between devices, tensor_total(): inner = lax.psum(inner, 'tx')  40.8 us
    psum x1, blocking collectives, small_total(): return lax.psum(inner, 'tz').astype(jnp.float32)  28.5 us
    all_gather x2, blocking collectives, gather_tensor(): inner = lax.all_gather(block, 'tx', axis=axis, tiled=True)  27.2 us
    all_to_all x1, waiting for transfers between devices, layer(): bank_all = lax.all_to_all(bank_send, 'adapter', 0, 0, tiled=True)  26.1 us
    all_gather x1, blocking collectives, gather_tensor(): return lax.all_gather(inner, 'tz', axis=axis, tiled=True)  25.8 us
    reduce_scatter x1, waiting for transfers between devices, scatter_tensor(): return lax.psum_scatter(inner, 'tx', scatter_dimension=0, tiled=True)  25.7 us
  transfers between devices with their start and end apart: 11, of which 8 were waited for; matrix products, arithmetic and copies ran while one was open for 9% of the time, Pallas kernels for 0%

profile of v6, /device:TPU:8, one launch (start us, length us, event | category | flops | bytes accessed | tf_op | source)
XLA Modules:
  0.0 435.7 jit_solution(2037794431708827679)
XLA Ops:
  6.5 14.6 %all_gather.15 = bf16[64,2880]{1,0:T(8,128)(2,1)} all-gather(bf16[16,2880]{1,0:T(8,128)(2,1)} %param.21), channel_id=1, replica_groups=mesh['tz'=8,'tx'=4,'adapter'=8] {'tx'}, dimensions={0}, use_global_device_ids=true | all-gather | bytes 460800 | tf_op jit(solution)/shard_map/all_gather | solution.py:105
  21.2 1.0 fusion.70
  25.6 1.0 fusion.72
  26.6 1.0 broadcast_select_fusion.1
  27.6 5.5 %all-to-all-start.1 = ((bf16[8,16,2880]{2,1,0:T(8,128)(2,1)}), bf16[8,16,2880]{2,1,0:T(8,128)(2,1)}, u32[]{:S(2)}, u32[]{:S(2)}) async-start(bf16[8,16,2880]{2,1,0:T(8,128)(2,1)} %broadcast_select_fusion.1), calls=%async_computation.1 | async-start | bytes 1507328 | tf_op jit(solution)/shard_map/all_to_all | solution.py:115
  35.4 2.6 gather_fusion.1
  38.7 1.1 reshape.673
  39.8 2.8 gather_fusion
  44.5 1.0 broadcast_select_fusion
  45.5 9.5 %all-to-all-start.3 = ((bf16[32,2,2048]{2,1,0:T(2,128)(2,1)}), bf16[32,2,2048]{2,1,0:T(2,128)(2,1)S(1)}, u32[]{:S(2)}, u32[]{:S(2)}) async-start(bf16[32,2,2048]{2,1,0:T(2,128)(2,1)} %reshape.673), calls=%async_computation.3 | async-start | bytes 524288 | tf_op jit(solution)/shard_map/all_to_all | solution.py:243
  55.1 2.6 fusion.37
  59.6 11.8 %all-to-all-done.3 = bf16[32,2,2048]{2,1,0:T(2,128)(2,1)S(1)} async-done(((bf16[32,2,2048]{2,1,0:T(2,128)(2,1)}), bf16[32,2,2048]{2,1,0:T(2,128)(2,1)S(1)}, u32[]{:S(2)}, u32[]{:S(2)}) %all-to-all-start.3) | async-done | bytes 262176 | tf_op jit(solution)/shard_map/all_to_all | solution.py:243
  71.5 4.8 %all-to-all-start.2 = ((bf16[8,2,384]{2,1,0:T(2,128)(2,1)}), bf16[8,2,384]{2,1,0:T(2,128)(2,1)S(1)}, u32[]{:S(2)}, u32[]{:S(2)}) async-start(bf16[8,2,384]{2,1,0:T(2,128)(2,1)} %reshape.671), calls=%async_computation.2 | async-start | bytes 24576 | tf_op jit(solution)/shard_map/all_to_all | solution.py:115
  76.4 1.5 copy.62
  77.8 2.4 all-to-all-done.2
  80.2 3.9 all-to-all-start
  84.9 1.2 fusion.17
  86.5 1.1 copy.69
  88.2 12.6 %all_gather.17 = bf16[64,48]{1,0:T(8,128)(2,1)S(1)} all-gather(bf16[16,48]{1,0:T(8,128)(2,1)S(1)} %reduce_sum.139), channel_id=1, replica_groups=mesh['tz'=8,'tx'=4,'adapter'=8] {'tx'}, dimensions={0}, use_global_device_ids=true | all-gather | bytes 7680 | tf_op jit(solution)/shard_map/all_gather | solution.py:105
  100.8 25.8 %all-gather = bf16[8,64,48]{1,2,0:T(8,128)(2,1)S(1)} all-gather(bf16[1,64,48]{1,2,0:T(8,128)(2,1)S(1)} %bitcast.144), channel_id=1, replica_groups=mesh['tz'=8,'tx'=4,'adapter'=8] {'tz'}, dimensions={0}, use_global_device_ids=true | all-gather | bytes 55296 | tf_op jit(solution)/shard_map/all_gather | solution.py:106
  126.8 1.1 convolution_bitcast_fusion
  128.9 1.7 copy.63
  130.6 2.2 fusion.118
  132.8 2.7 fusion
  135.6 1.0 fusion.2
  136.7 1.0 fusion.59
  137.8 1.0 fusion.62
  139.5 1.2 convolution_add_fusion
  140.8 1.0 fusion.9
  143.7 16.7 %psum.21 = bf16[512,16]{0,1:T(8,128)(2,1)S(1)} all-reduce(bf16[512,16]{0,1:T(8,128)(2,1)S(1)} %multiply_reduce_fusion.1), channel_id=1, replica_groups=mesh['tz'=8,'tx'=4,'adapter'=8] {'tx'}, use_global_device_ids=true, to_apply=%region_13.14 | all-reduce | flops 8192 | bytes 32768 | tf_op jit(solution)/shard_map/psum | solution.py:129
  160.3 28.5 %psum.22 = bf16[512,16]{0,1:T(8,128)(2,1)S(1)} all-reduce(bf16[512,16]{0,1:T(8,128)(2,1)S(1)} %psum.21), channel_id=1, replica_groups=mesh['tz'=8,'tx'=4,'adapter'=8] {'tz'}, use_global_device_ids=true, to_apply=%region_14.15 | all-reduce | flops 8192 | bytes 32768 | tf_op jit(solution)/shard_map/psum | solution.py:130
  190.0 2.6 fusion.4
  192.7 42.1 %reduce-scatter.4.cloned.1.call-done = bf16[64,2880]{1,0:T(8,128)(2,1)} async-done(((bf16[512,2880]{1,0:T(8,128)(2,1)}), bf16[64,2880]{1,0:T(8,128)(2,1)}) %reduce-scatter.4.cloned.1.call-update) | async-done | bytes 368656 | tf_op jit(solution)/shard_map/reduce_scatter | solution.py:123
  234.8 3.0 broadcast_in_dim.255
  237.8 5.2 %all-to-all-start.4 = ((bf16[8,8,16,2880]{3,2,1,0:T(8,128)(2,1)}), bf16[8,8,16,2880]{3,2,1,0:T(8,128)(2,1)}, u32[]{:S(2)}, u32[]{:S(2)}) async-start(bf16[8,8,16,2880]{3,2,1,0:T(8,128)(2,1)} %broadcast_in_dim.255), calls=%async_computation.5 | async-start | bytes 12058624 | tf_op jit(solution)/shard_map/all_to_all | solution.py:273
  243.0 40.8 %all-reduce.5.cloned.1.call-done = bf16[64,2880]{1,0:T(8,128)(2,1)} async-done(((bf16[64,2880]{1,0:T(8,128)(2,1)}), bf16[64,2880]{1,0:T(8,128)(2,1)}) %all-reduce.5.cloned.1.call-update) | async-done | bytes 368656 | tf_op jit(solution)/shard_map/psum | solution.py:124
  284.9 26.1 %all-to-all-done.4 = bf16[8,8,16,2880]{3,2,1,0:T(8,128)(2,1)} async-done(((bf16[8,8,16,2880]{3,2,1,0:T(8,128)(2,1)}), bf16[8,8,16,2880]{3,2,1,0:T(8,128)(2,1)}, u32[]{:S(2)}, u32[]{:S(2)}) %all-to-all-start.4) | async-done | bytes 5898272 | tf_op jit(solution)/shard_map/all_to_all | solution.py:273
  311.0 3.4 gather_fusion.3
  314.4 15.6 %all-gather.6.cloned.1.call-done = bf16[512,2880]{1,0:T(8,128)(2,1)} async-done(((bf16[64,2880]{1,0:T(8,128)(2,1)}), bf16[512,2880]{1,0:T(8,128)(2,1)}) %all-gather.6.cloned.1.call-update) | async-done | bytes 2949136 | tf_op jit(solution)/shard_map/all_gather | solution.py:125
  330.0 6.4 %convert_add_fusion = (f32[512,2880]{1,0:T(8,128)}, f32[512]{0:T(512)S(1)}) fusion(bf16[512,2880]{1,0:T(8,128)(2,1)} %all-gather.4.cloned.1.call-done, bf16[512,2880]{1,0:T(8,128)(2,1)} %all-gather.6.cloned.1.call-done), kind=kLoop, calls=%fused_computation.4 | loop fusion | flops 7372288 | bytes 11798528 | tf_op jit(solution)/shard_map/add | solution.py:289
  336.5 1.4 multiply_convert_fusion
  337.9 4.0 fusion.10
  342.0 1.1 fusion.44
  343.2 3.6 fusion.88
  346.8 9.9 %fusion.3 = bf16[512,2880]{1,0:T(8,128)(2,1)} fusion(f32[512,2880,1]{1,0,2:T(8,128)} %fusion.88, bf16[360,2880]{1,0:T(8,128)(2,1)} %param.34, pred[512]{0:T(512)(128)(4,1)S(1)} %reduce_or.9, f32[512,360]{0,1:T(8,128)S(1)} %fusion.10, bf16[512,2880]{1,0:T(8,128)(2,1)} %copy-done.10, bf16[2880,2,360]{0,2,1:T(8,128)(2,1)} %param.33, f32[512]{0:T(512)S(1)} %get-tuple-element.22), kind=kOutput, calls=%fused_computation.11 | convolution fusion | flops 2129448960 | bytes 16972288 | tf_op jit(solution)/shard_map/dot_general | solution.py:318
  356.7 44.7 %reduce-scatter.6.cloned.1.call-done = bf16[64,2880]{1,0:T(8,128)(2,1)} async-done(((bf16[512,2880]{1,0:T(8,128)(2,1)}), bf16[64,2880]{1,0:T(8,128)(2,1)}) %reduce-scatter.6.cloned.1.call-update) | async-done | bytes 368656 | tf_op jit(solution)/shard_map/reduce_scatter | solution.py:110
  401.5 25.7 %reduce-scatter.8.cloned.1.call-done = bf16[16,2880]{1,0:T(8,128)(2,1)} async-done(((bf16[64,2880]{1,0:T(8,128)(2,1)}), bf16[16,2880]{1,0:T(8,128)(2,1)}) %reduce-scatter.8.cloned.1.call-update) | async-done | bytes 92176 | tf_op jit(solution)/shard_map/reduce_scatter | solution.py:111
  427.2 1.6 add_convert_fusion
  (139 shorter events, 18.2 us)
Async XLA Ops:
  6.5 48.5 %copy-start = (bf16[8,48,2880]{2,1,0:T(8,128)(2,1)S(1)}, bf16[8,48,2880]{2,1,0:T(8,128)(2,1)}, u32[]{:S(2)}) copy-start(bf16[8,48,2880]{2,1,0:T(8,128)(2,1)} %param.27) | copy-start | bytes 6635524
  6.5 28.2 %copy-start.3 = (s32[64]{0:T(128)S(1)}, s32[64]{0:T(128)}, u32[]{:S(2)}) copy-start(s32[64]{0:T(128)} %param.39) | copy-start | bytes 772
  6.5 28.8 %copy-start.4 = (bf16[64,2,16,2,8]{0,4,3,2,1:T(8,128)(2,1)S(1)}, bf16[64,2,16,2,8]{0,4,3,2,1:T(8,128)(2,1)}, u32[]{:S(2)}) copy-start(bf16[64,2,16,2,8]{0,4,3,2,1:T(8,128)(2,1)} %param.29) | copy-start | bytes 196612
  6.5 126.3 %all-gather.4.cloned.1.call-start = ((), (), s32[]{:S(2)}) async-start(), calls=%async_computation.8 | async-start | bytes 3391488 | tf_op jit(solution)/shard_map/all_gather | solution.py:106
  27.6 17.9 %all-to-all-start.1 = ((bf16[8,16,2880]{2,1,0:T(8,128)(2,1)}), bf16[8,16,2880]{2,1,0:T(8,128)(2,1)}, u32[]{:S(2)}, u32[]{:S(2)}) async-start(bf16[8,16,2880]{2,1,0:T(8,128)(2,1)} %broadcast_select_fusion.1), calls=%async_computation.1 | async-start | bytes 1507328 | tf_op jit(solution)/shard_map/all_to_all | solution.py:115
  38.0 1.8 copy-start.2
  45.5 30.9 %copy-start.9 = (bf16[32,2880,2,2]{1,0,3,2:T(8,128)(2,1)S(1)}, bf16[32,2880,2,2]{1,0,3,2:T(8,128)(2,1)}, u32[]{:S(2)}) copy-start(bf16[32,2880,2,2]{1,0,3,2:T(8,128)(2,1)} %broadcast_select_fusion) | copy-start | bytes 2211844
  45.5 26.0 %all-to-all-start.3 = ((bf16[32,2,2048]{2,1,0:T(2,128)(2,1)}), bf16[32,2,2048]{2,1,0:T(2,128)(2,1)S(1)}, u32[]{:S(2)}, u32[]{:S(2)}) async-start(bf16[32,2,2048]{2,1,0:T(2,128)(2,1)} %reshape.673), calls=%async_computation.3 | async-start | bytes 524288 | tf_op jit(solution)/shard_map/all_to_all | solution.py:243
  55.0 29.1 %copy-start.28 = (f32[2]{0:T(128)S(1)}, f32[2]{0:T(128)}, u32[]{:S(2)}) copy-start(f32[2]{0:T(128)} %param.26) | copy-start | bytes 28
  71.5 8.7 %all-to-all-start.2 = ((bf16[8,2,384]{2,1,0:T(2,128)(2,1)}), bf16[8,2,384]{2,1,0:T(2,128)(2,1)S(1)}, u32[]{:S(2)}, u32[]{:S(2)}) async-start(bf16[8,2,384]{2,1,0:T(2,128)(2,1)} %reshape.671), calls=%async_computation.2 | async-start | bytes 24576 | tf_op jit(solution)/shard_map/all_to_all | solution.py:115
  77.8 49.0 %copy-start.26 = (bf16[64,16,128]{2,1,0:T(8,128)(2,1)S(1)}, bf16[64,16,128]{2,1,0:T(8,128)(2,1)}, u32[]{:S(2)}) copy-start(bf16[64,16,128]{2,1,0:T(8,128)(2,1)} %param.28) | copy-start | bytes 786436
  80.2 47.9 %all-to-all-start = ((bf16[32,2880,2,2]{1,3,2,0:T(2,128)(2,1)}), bf16[32,2880,2,2]{1,3,2,0:T(2,128)(2,1)S(1)}, u32[]{:S(2)}, u32[]{:S(2)}) async-start(bf16[32,2880,2,2]{1,3,2,0:T(2,128)(2,1)} %copy.62), calls=%async_computation | async-start | bytes 1507328 | tf_op jit(solution)/shard_map/all_to_all | solution.py:238
  84.1 150.6 %reduce-scatter.4.cloned.1.call-start = ((), (), s32[]{:S(2)}) async-start(), calls=%async_computation.9 | async-start | bytes 3391488 | tf_op jit(solution)/shard_map/reduce_scatter | solution.py:123
  128.0 0.9 copy-start.8
  130.6 4.9 %copy-start.22 = (f32[2880]{0:T(1024)S(1)}, f32[2880]{0:T(1024)}, u32[]{:S(2)}) copy-start(f32[2880]{0:T(1024)} %param.22) | copy-start | bytes 34564
  132.8 2.8 copy-start.5
  135.6 1.1 copy-start.12
  136.6 1.2 copy-start.11
  137.8 1.7 copy-start.15
  137.8 1.7 copy-start.18
  139.2 1.6 copy-start.17
  140.7 1.2 copy-start.13
  142.2 1.0 copy-start.21
  142.2 1.0 copy-start.27
  142.2 46.7 %copy-start.19 = (bf16[2,16,2880]{2,1,0:T(8,128)(2,1)S(1)}, bf16[2,16,2880]{2,1,0:T(8,128)(2,1)}, u32[]{:S(2)}) copy-start(bf16[2,16,2880]{2,1,0:T(8,128)(2,1)} %param.31) | copy-start | bytes 552964
  188.9 1.1 copy-start.16
  192.6 42.2 %copy-start.14 = (bf16[8,16,2880]{2,1,0:T(8,128)(2,1)S(1)}, bf16[8,16,2880]{2,1,0:T(8,128)(2,1)}, u32[]{:S(2)}) copy-start(bf16[8,16,2880]{2,1,0:T(8,128)(2,1)} %param.35) | copy-start | bytes 2211844
  192.6 91.2 %all-reduce.5.cloned.1.call-start = ((), (), s32[]{:S(2)}) async-start(), calls=%async_computation.10 | async-start | bytes 753664 | tf_op jit(solution)/shard_map/psum | solution.py:124
  237.8 46.3 %copy-start.24 = (f32[512,4]{0,1:T(4,128)S(1)}, f32[512,4]{0,1:T(4,128)}, u32[]{:S(2)}) copy-start(f32[512,4]{0,1:T(4,128)} %param.41) | copy-start | bytes 24580
  237.8 46.3 %copy-start.25 = (s32[512,4]{0,1:T(4,128)S(1)}, s32[512,4]{0,1:T(4,128)}, u32[]{:S(2)}) copy-start(s32[512,4]{0,1:T(4,128)} %param.40) | copy-start | bytes 24580
  237.8 73.1 %all-to-all-start.4 = ((bf16[8,8,16,2880]{3,2,1,0:T(8,128)(2,1)}), bf16[8,8,16,2880]{3,2,1,0:T(8,128)(2,1)}, u32[]{:S(2)}, u32[]{:S(2)}) async-start(bf16[8,8,16,2880]{3,2,1,0:T(8,128)(2,1)} %broadcast_in_dim.255), calls=%async_computation.5 | async-start | bytes 12058624 | tf_op jit(solution)/shard_map/all_to_all | solution.py:273
  243.0 87.0 %all-gather.6.cloned.1.call-start = ((), (), s32[]{:S(2)}) async-start(), calls=%async_computation.11 | async-start | bytes 3391488 | tf_op jit(solution)/shard_map/all_gather | solution.py:125
  283.8 117.7 %reduce-scatter.6.cloned.1.call-start = ((), (), s32[]{:S(2)}) async-start(), calls=%async_computation.12 | async-start | bytes 3391488 | tf_op jit(solution)/shard_map/reduce_scatter | solution.py:110
  314.4 22.1 %copy-start.23 = (f32[2880]{0:T(1024)S(1)}, f32[2880]{0:T(1024)}, u32[]{:S(2)}) copy-start(f32[2880]{0:T(1024)} %param.32) | copy-start | bytes 34564
  330.0 6.5 %copy-start.6 = (bf16[512,2880]{1,0:T(8,128)(2,1)S(1)}, bf16[512,2880]{1,0:T(8,128)(2,1)}, u32[]{:S(2)}) copy-start(bf16[512,2880]{1,0:T(8,128)(2,1)} %all-gather.4.cloned.1.call-done) | copy-start | bytes 8847364
  330.0 6.5 %copy-start.7 = (bf16[512,2880]{1,0:T(8,128)(2,1)S(1)}, bf16[512,2880]{1,0:T(8,128)(2,1)}, u32[]{:S(2)}) copy-start(bf16[512,2880]{1,0:T(8,128)(2,1)} %all-gather.6.cloned.1.call-done) | copy-start | bytes 8847364
  337.9 4.1 copy-start.10
  342.0 1.1 copy-start.20
  346.7 82.1 %copy-start.1 = (bf16[8,48,2880]{2,1,0:T(8,128)(2,1)S(1)}, bf16[8,48,2880]{2,1,0:T(8,128)(2,1)}, u32[]{:S(2)}) copy-start(bf16[8,48,2880]{2,1,0:T(8,128)(2,1)} %param.27) | copy-start | bytes 6635524
  356.7 70.5 %reduce-scatter.8.cloned.1.call-start = ((), (), s32[]{:S(2)}) async-start(), calls=%async_computation.13 | async-start | bytes 471040 | tf_op jit(solution)/shard_map/reduce_scatter | solution.py:111
Sparse Core Ops, SparseCore 0:
  21.3 51.2 all-gather.3
  192.7 41.9 reduce-scatter.3
  237.1 46.6 all-reduce.4
  285.4 44.5 all-gather.5
  356.8 44.6 reduce-scatter.5
  403.9 23.2 reduce-scatter.7

commit v7 on v5

--- a/solution.py
+++ b/solution.py
@@ -128,8 +128,8 @@
 
 
 def small_total(partial_value):
-    inner = lax.psum(partial_value.astype(jnp.bfloat16), "tx")
-    return lax.psum(inner, "tz").astype(jnp.float32)
+    inner = lax.psum(partial_value.astype(jnp.bfloat16), "tz")
+    return lax.psum(inner, "tx").astype(jnp.float32)
 
 
 def partial_sum(term_maker, own_rows):
@@ -286,7 +286,7 @@
     up_out = output_up.reshape(local_count * R, -1)
     term = jnp.dot(mixed_rows, output_weight, preferred_element_type=jnp.float32)
     attn_all = tensor_total(
-        settle(term + jnp.dot(spread_out, up_out, preferred_element_type=jnp.float32))
+        term + jnp.dot(spread_out, up_out, preferred_element_type=jnp.float32)
     )
     hidden_all = tokens_all.astype(jnp.float32) + attn_all
     normed_two = rms_scale(hidden_all, gain_mixture)
@@ -323,7 +323,7 @@
 
     def moe_term(row_start, row_count):
         expert_rows = jnp.where(picked[:, None], expert_terms, 0.0)
-        return settle(expert_rows + jnp.dot(spread_moe, up_moe, preferred_element_type=jnp.float32))
+        return expert_rows + jnp.dot(spread_moe, up_moe, preferred_element_type=jnp.float32)
 
     moe_own = partial_sum(moe_term, own_rows)
     return (hidden_own + moe_own).astype(jnp.bfloat16)

time: 434 us -> 425 us (0.979)
  local copies, waits for them, and re-layouts: 34.5 us -> 25.1 us
    reduce_scatter x0 -> x2, waiting for transfers between devices: none -> 87.1 us  [scatter_tensor(): inner = lax.psum_scatter(block, 'tz', scatter_dimension=0, tiled=True)]
    unnamed x8 -> x6, waiting for transfers between devices: 87 us -> 0.1 us
    unnamed x65 -> x63, local copies, waits for them, and re-layouts: 12.9 us -> 3.57 us
where the time goes in v7:
time: 425 us; the launch traced here: 424 us
  waiting for transfers between devices  183 us (43%)
  blocking collectives  112 us (26%)
  matrix products  32.1 us (8%)
  starting transfers between devices  29.4 us (7%)
  other arithmetic  27.4 us (6%)
  local copies, waits for them, and re-layouts  25.1 us (6%)
  between operations  14.1 us (3%)
    reduce_scatter x2, waiting for transfers between devices, scatter_tensor(): inner = lax.psum_scatter(block, 'tz', scatter_dimension=0, tiled=True)  87.1 us
    reduce_scatter x2, waiting for transfers between devices, scatter_tensor(): return lax.psum_scatter(inner, 'tx', scatter_dimension=0, tiled=True)  42.6 us
    all_gather x3, blocking collectives, gather_tensor(): inner = lax.all_gather(block, 'tx', axis=axis, tiled=True)  41 us
    all_to_all x1, waiting for transfers between devices, layer(): bank_all = lax.all_to_all(bank_send, 'adapter', 0, 0, tiled=True)  35.7 us
    psum x1, blocking collectives, small_total(): inner = lax.psum(partial_value.astype(jnp.bfloat16), 'tz')  28.7 us
    all_gather x1, blocking collectives, gather_tensor(): return lax.all_gather(inner, 'tz', axis=axis, tiled=True)  25.8 us
    psum x1, blocking collectives, small_total(): return lax.psum(inner, 'tx').astype(jnp.float32)  16.5 us
    all_to_all x1, waiting for transfers between devices, layer(): up_recv = lax.all_to_all(up_send, TENSOR, 0, 0, tiled=True)  11.8 us
  transfers between devices with their start and end apart: 11, of which 8 were waited for; matrix products, arithmetic and copies ran while one was open for 10% of the time, Pallas kernels for 0%

profile of v7, /device:TPU:8, one launch (start us, length us, event | category | flops | bytes accessed | tf_op | source)
XLA Modules:
  0.0 423.7 jit_solution(13719695042888353253)
XLA Ops:
  6.5 14.6 %all_gather.18 = bf16[64,2880]{1,0:T(8,128)(2,1)} all-gather(bf16[16,2880]{1,0:T(8,128)(2,1)} %param.21), channel_id=1, replica_groups=mesh['tz'=8,'tx'=4,'adapter'=8] {'tx'}, dimensions={0}, use_global_device_ids=true | all-gather | bytes 460800 | tf_op jit(solution)/shard_map/all_gather | solution.py:109
  21.2 1.0 fusion.70
  25.6 1.0 fusion.72
  26.6 1.0 broadcast_select_fusion.1
  27.6 5.5 %all-to-all-start.1 = ((bf16[8,16,2880]{2,1,0:T(8,128)(2,1)}), bf16[8,16,2880]{2,1,0:T(8,128)(2,1)}, u32[]{:S(2)}, u32[]{:S(2)}) async-start(bf16[8,16,2880]{2,1,0:T(8,128)(2,1)} %broadcast_select_fusion.1), calls=%async_computation.1 | async-start | bytes 1507328 | tf_op jit(solution)/shard_map/all_to_all | solution.py:119
  35.4 2.6 gather_fusion.1
  38.7 1.1 reshape.673
  39.8 2.8 gather_fusion
  44.5 1.0 broadcast_select_fusion
  45.5 9.5 %all-to-all-start.3 = ((bf16[32,2,2048]{2,1,0:T(2,128)(2,1)}), bf16[32,2,2048]{2,1,0:T(2,128)(2,1)S(1)}, u32[]{:S(2)}, u32[]{:S(2)}) async-start(bf16[32,2,2048]{2,1,0:T(2,128)(2,1)} %reshape.673), calls=%async_computation.3 | async-start | bytes 524288 | tf_op jit(solution)/shard_map/all_to_all | solution.py:245
  55.1 2.6 fusion.37
  59.6 11.8 %all-to-all-done.3 = bf16[32,2,2048]{2,1,0:T(2,128)(2,1)S(1)} async-done(((bf16[32,2,2048]{2,1,0:T(2,128)(2,1)}), bf16[32,2,2048]{2,1,0:T(2,128)(2,1)S(1)}, u32[]{:S(2)}, u32[]{:S(2)}) %all-to-all-start.3) | async-done | bytes 262176 | tf_op jit(solution)/shard_map/all_to_all | solution.py:245
  71.5 4.8 %all-to-all-start.2 = ((bf16[8,2,384]{2,1,0:T(2,128)(2,1)}), bf16[8,2,384]{2,1,0:T(2,128)(2,1)S(1)}, u32[]{:S(2)}, u32[]{:S(2)}) async-start(bf16[8,2,384]{2,1,0:T(2,128)(2,1)} %reshape.671), calls=%async_computation.2 | async-start | bytes 24576 | tf_op jit(solution)/shard_map/all_to_all | solution.py:119
  76.4 1.5 copy.62
  77.8 2.4 all-to-all-done.2
  80.2 3.9 all-to-all-start
  84.9 1.2 fusion.17
  86.5 1.1 copy.69
  88.2 12.6 %all_gather.20 = bf16[64,48]{1,0:T(8,128)(2,1)S(1)} all-gather(bf16[16,48]{1,0:T(8,128)(2,1)S(1)} %reduce_sum.139), channel_id=1, replica_groups=mesh['tz'=8,'tx'=4,'adapter'=8] {'tx'}, dimensions={0}, use_global_device_ids=true | all-gather | bytes 7680 | tf_op jit(solution)/shard_map/all_gather | solution.py:109
  100.8 25.8 %all-gather = bf16[8,64,48]{1,2,0:T(8,128)(2,1)S(1)} all-gather(bf16[1,64,48]{1,2,0:T(8,128)(2,1)S(1)} %bitcast.144), channel_id=1, replica_groups=mesh['tz'=8,'tx'=4,'adapter'=8] {'tz'}, dimensions={0}, use_global_device_ids=true | all-gather | bytes 55296 | tf_op jit(solution)/shard_map/all_gather | solution.py:110
  126.8 1.1 convolution_bitcast_fusion
  128.9 1.7 copy.63
  130.6 2.2 fusion.118
  132.8 2.7 fusion
  135.6 1.0 fusion.2
  136.7 1.0 fusion.59
  137.8 1.0 fusion.62
  139.5 1.2 convolution_add_fusion
  143.7 28.7 %psum.14 = bf16[512,16]{0,1:T(8,128)(2,1)S(1)} all-reduce(bf16[512,16]{0,1:T(8,128)(2,1)S(1)} %multiply_reduce_fusion.1), channel_id=1, replica_groups=mesh['tz'=8,'tx'=4,'adapter'=8] {'tz'}, use_global_device_ids=true, to_apply=%region_13.14 | all-reduce | flops 8192 | bytes 32768 | tf_op jit(solution)/shard_map/psum | solution.py:131
  172.4 16.5 %psum.15 = bf16[512,16]{0,1:T(8,128)(2,1)S(1)} all-reduce(bf16[512,16]{0,1:T(8,128)(2,1)S(1)} %psum.14), channel_id=1, replica_groups=mesh['tz'=8,'tx'=4,'adapter'=8] {'tx'}, use_global_device_ids=true, to_apply=%region_14.15 | all-reduce | flops 8192 | bytes 32768 | tf_op jit(solution)/shard_map/psum | solution.py:132
  190.0 2.6 fusion.4
  192.7 42.1 %reduce-scatter.5.cloned.1.call-done = bf16[64,2880]{1,0:T(8,128)(2,1)} async-done(((bf16[512,2880]{1,0:T(8,128)(2,1)}), bf16[64,2880]{1,0:T(8,128)(2,1)}) %reduce-scatter.5.cloned.1.call-update) | async-done | bytes 368656 | tf_op jit(solution)/shard_map/reduce_scatter | solution.py:114
  234.8 3.0 broadcast_in_dim.255
  237.8 5.2 %all-to-all-start.4 = ((bf16[8,8,16,2880]{3,2,1,0:T(8,128)(2,1)}), bf16[8,8,16,2880]{3,2,1,0:T(8,128)(2,1)}, u32[]{:S(2)}, u32[]{:S(2)}) async-start(bf16[8,8,16,2880]{3,2,1,0:T(8,128)(2,1)} %broadcast_in_dim.255), calls=%async_computation.6 | async-start | bytes 12058624 | tf_op jit(solution)/shard_map/all_to_all | solution.py:275
  243.1 17.3 %reduce-scatter.7.cloned.1.call-done = bf16[16,2880]{1,0:T(8,128)(2,1)} async-done(((bf16[64,2880]{1,0:T(8,128)(2,1)}), bf16[16,2880]{1,0:T(8,128)(2,1)}) %reduce-scatter.7.cloned.1.call-update) | async-done | bytes 92176 | tf_op jit(solution)/shard_map/reduce_scatter | solution.py:115
  260.4 13.8 %all_gather.22 = bf16[64,2880]{1,0:T(8,128)(2,1)} all-gather(bf16[16,2880]{1,0:T(8,128)(2,1)} %reduce-scatter.7.cloned.1.call-done), channel_id=1, replica_groups=mesh['tz'=8,'tx'=4,'adapter'=8] {'tx'}, dimensions={0}, use_global_device_ids=true | all-gather | bytes 460800 | tf_op jit(solution)/shard_map/all_gather | solution.py:109
  275.3 35.7 %all-to-all-done.4 = bf16[8,8,16,2880]{3,2,1,0:T(8,128)(2,1)} async-done(((bf16[8,8,16,2880]{3,2,1,0:T(8,128)(2,1)}), bf16[8,8,16,2880]{3,2,1,0:T(8,128)(2,1)}, u32[]{:S(2)}, u32[]{:S(2)}) %all-to-all-start.4) | async-done | bytes 5898272 | tf_op jit(solution)/shard_map/all_to_all | solution.py:275
  311.1 3.4 gather_fusion.3
  314.5 3.7 all-gather.6.cloned.1.call-done
  318.2 6.4 %convert_add_fusion = (f32[512,2880]{1,0:T(8,128)}, f32[512]{0:T(512)S(1)}) fusion(bf16[512,2880]{1,0:T(8,128)(2,1)} %all-gather.4.cloned.1.call-done, bf16[512,2880]{1,0:T(8,128)(2,1)} %all-gather.6.cloned.1.call-done), kind=kLoop, calls=%fused_computation.4 | loop fusion | flops 7372288 | bytes 11798528 | tf_op jit(solution)/shard_map/add | solution.py:291
  324.7 1.4 multiply_convert_fusion
  326.2 4.0 fusion.10
  330.2 1.1 fusion.44
  331.4 3.6 fusion.88
  335.0 9.9 %fusion.3 = bf16[512,2880]{1,0:T(8,128)(2,1)} fusion(f32[512,2880,1]{1,0,2:T(8,128)} %fusion.88, bf16[360,2880]{1,0:T(8,128)(2,1)} %param.34, pred[512]{0:T(512)(128)(4,1)S(1)} %reduce_or.9, f32[512,360]{0,1:T(8,128)S(1)} %fusion.10, bf16[512,2880]{1,0:T(8,128)(2,1)} %copy-done.10, bf16[2880,2,360]{0,2,1:T(8,128)(2,1)} %param.33, f32[512]{0:T(512)S(1)} %get-tuple-element.22), kind=kOutput, calls=%fused_computation.11 | convolution fusion | flops 2129448960 | bytes 16972288 | tf_op jit(solution)/shard_map/dot_general | solution.py:320
  344.9 44.9 %reduce-scatter.9.cloned.1.call-done = bf16[64,2880]{1,0:T(8,128)(2,1)} async-done(((bf16[512,2880]{1,0:T(8,128)(2,1)}), bf16[64,2880]{1,0:T(8,128)(2,1)}) %reduce-scatter.9.cloned.1.call-update) | async-done | bytes 368656 | tf_op jit(solution)/shard_map/reduce_scatter | solution.py:114
  389.9 25.3 %reduce-scatter.11.cloned.1.call-done = bf16[16,2880]{1,0:T(8,128)(2,1)} async-done(((bf16[64,2880]{1,0:T(8,128)(2,1)}), bf16[16,2880]{1,0:T(8,128)(2,1)}) %reduce-scatter.11.cloned.1.call-update) | async-done | bytes 92176 | tf_op jit(solution)/shard_map/reduce_scatter | solution.py:115
  415.3 1.6 add_convert_fusion
  (140 shorter events, 19.2 us)
Async XLA Ops:
  6.5 48.5 %copy-start = (bf16[8,48,2880]{2,1,0:T(8,128)(2,1)S(1)}, bf16[8,48,2880]{2,1,0:T(8,128)(2,1)}, u32[]{:S(2)}) copy-start(bf16[8,48,2880]{2,1,0:T(8,128)(2,1)} %param.27) | copy-start | bytes 6635524
  6.5 28.2 %copy-start.3 = (s32[64]{0:T(128)S(1)}, s32[64]{0:T(128)}, u32[]{:S(2)}) copy-start(s32[64]{0:T(128)} %param.39) | copy-start | bytes 772
  6.5 28.8 %copy-start.4 = (bf16[64,2,16,2,8]{0,4,3,2,1:T(8,128)(2,1)S(1)}, bf16[64,2,16,2,8]{0,4,3,2,1:T(8,128)(2,1)}, u32[]{:S(2)}) copy-start(bf16[64,2,16,2,8]{0,4,3,2,1:T(8,128)(2,1)} %param.29) | copy-start | bytes 196612
  6.5 126.3 %all-gather.4.cloned.1.call-start = ((), (), s32[]{:S(2)}) async-start(), calls=%async_computation.9 | async-start | bytes 3391488 | tf_op jit(solution)/shard_map/all_gather | solution.py:110
  27.6 17.9 %all-to-all-start.1 = ((bf16[8,16,2880]{2,1,0:T(8,128)(2,1)}), bf16[8,16,2880]{2,1,0:T(8,128)(2,1)}, u32[]{:S(2)}, u32[]{:S(2)}) async-start(bf16[8,16,2880]{2,1,0:T(8,128)(2,1)} %broadcast_select_fusion.1), calls=%async_computation.1 | async-start | bytes 1507328 | tf_op jit(solution)/shard_map/all_to_all | solution.py:119
  38.0 1.8 copy-start.2
  45.5 30.9 %copy-start.9 = (bf16[32,2880,2,2]{1,0,3,2:T(8,128)(2,1)S(1)}, bf16[32,2880,2,2]{1,0,3,2:T(8,128)(2,1)}, u32[]{:S(2)}) copy-start(bf16[32,2880,2,2]{1,0,3,2:T(8,128)(2,1)} %broadcast_select_fusion) | copy-start | bytes 2211844
  45.5 26.0 %all-to-all-start.3 = ((bf16[32,2,2048]{2,1,0:T(2,128)(2,1)}), bf16[32,2,2048]{2,1,0:T(2,128)(2,1)S(1)}, u32[]{:S(2)}, u32[]{:S(2)}) async-start(bf16[32,2,2048]{2,1,0:T(2,128)(2,1)} %reshape.673), calls=%async_computation.3 | async-start | bytes 524288 | tf_op jit(solution)/shard_map/all_to_all | solution.py:245
  55.0 29.1 %copy-start.28 = (f32[2]{0:T(128)S(1)}, f32[2]{0:T(128)}, u32[]{:S(2)}) copy-start(f32[2]{0:T(128)} %param.26) | copy-start | bytes 28
  71.5 8.7 %all-to-all-start.2 = ((bf16[8,2,384]{2,1,0:T(2,128)(2,1)}), bf16[8,2,384]{2,1,0:T(2,128)(2,1)S(1)}, u32[]{:S(2)}, u32[]{:S(2)}) async-start(bf16[8,2,384]{2,1,0:T(2,128)(2,1)} %reshape.671), calls=%async_computation.2 | async-start | bytes 24576 | tf_op jit(solution)/shard_map/all_to_all | solution.py:119
  77.8 49.0 %copy-start.26 = (bf16[64,16,128]{2,1,0:T(8,128)(2,1)S(1)}, bf16[64,16,128]{2,1,0:T(8,128)(2,1)}, u32[]{:S(2)}) copy-start(bf16[64,16,128]{2,1,0:T(8,128)(2,1)} %param.28) | copy-start | bytes 786436
  80.2 47.9 %all-to-all-start = ((bf16[32,2880,2,2]{1,3,2,0:T(2,128)(2,1)}), bf16[32,2880,2,2]{1,3,2,0:T(2,128)(2,1)S(1)}, u32[]{:S(2)}, u32[]{:S(2)}) async-start(bf16[32,2880,2,2]{1,3,2,0:T(2,128)(2,1)} %copy.62), calls=%async_computation | async-start | bytes 1507328 | tf_op jit(solution)/shard_map/all_to_all | solution.py:240
  84.1 150.7 %reduce-scatter.5.cloned.1.call-start = ((), (), s32[]{:S(2)}) async-start(), calls=%async_computation.10 | async-start | bytes 3391488 | tf_op jit(solution)/shard_map/reduce_scatter | solution.py:114
  128.0 0.9 copy-start.8
  130.6 4.9 %copy-start.22 = (f32[2880]{0:T(1024)S(1)}, f32[2880]{0:T(1024)}, u32[]{:S(2)}) copy-start(f32[2880]{0:T(1024)} %param.22) | copy-start | bytes 34564
  132.8 2.8 copy-start.5
  135.6 1.1 copy-start.12
  136.6 1.2 copy-start.11
  137.8 1.7 copy-start.15
  137.8 1.7 copy-start.18
  139.2 1.6 copy-start.17
  140.7 1.2 copy-start.13
  142.2 1.0 copy-start.21
  142.2 1.0 copy-start.27
  142.2 46.7 %copy-start.19 = (bf16[2,16,2880]{2,1,0:T(8,128)(2,1)S(1)}, bf16[2,16,2880]{2,1,0:T(8,128)(2,1)}, u32[]{:S(2)}) copy-start(bf16[2,16,2880]{2,1,0:T(8,128)(2,1)} %param.31) | copy-start | bytes 552964
  188.9 1.1 copy-start.16
  192.6 42.2 %copy-start.14 = (bf16[8,16,2880]{2,1,0:T(8,128)(2,1)S(1)}, bf16[8,16,2880]{2,1,0:T(8,128)(2,1)}, u32[]{:S(2)}) copy-start(bf16[8,16,2880]{2,1,0:T(8,128)(2,1)} %param.35) | copy-start | bytes 2211844
  192.6 67.8 %reduce-scatter.7.cloned.1.call-start = ((), (), s32[]{:S(2)}) async-start(), calls=%async_computation.11 | async-start | bytes 471040 | tf_op jit(solution)/shard_map/reduce_scatter | solution.py:115
  237.8 36.7 %copy-start.24 = (f32[512,4]{0,1:T(4,128)S(1)}, f32[512,4]{0,1:T(4,128)}, u32[]{:S(2)}) copy-start(f32[512,4]{0,1:T(4,128)} %param.41) | copy-start | bytes 24580
  237.8 36.7 %copy-start.25 = (s32[512,4]{0,1:T(4,128)S(1)}, s32[512,4]{0,1:T(4,128)}, u32[]{:S(2)}) copy-start(s32[512,4]{0,1:T(4,128)} %param.40) | copy-start | bytes 24580
  237.8 73.2 %all-to-all-start.4 = ((bf16[8,8,16,2880]{3,2,1,0:T(8,128)(2,1)}), bf16[8,8,16,2880]{3,2,1,0:T(8,128)(2,1)}, u32[]{:S(2)}, u32[]{:S(2)}) async-start(bf16[8,8,16,2880]{3,2,1,0:T(8,128)(2,1)} %broadcast_in_dim.255), calls=%async_computation.6 | async-start | bytes 12058624 | tf_op jit(solution)/shard_map/all_to_all | solution.py:275
  243.1 75.1 %all-gather.6.cloned.1.call-start = ((), (), s32[]{:S(2)}) async-start(), calls=%async_computation.12 | async-start | bytes 3391488 | tf_op jit(solution)/shard_map/all_gather | solution.py:110
  274.2 115.6 %reduce-scatter.9.cloned.1.call-start = ((), (), s32[]{:S(2)}) async-start(), calls=%async_computation.13 | async-start | bytes 3391488 | tf_op jit(solution)/shard_map/reduce_scatter | solution.py:114
  314.5 10.2 %copy-start.23 = (f32[2880]{0:T(1024)S(1)}, f32[2880]{0:T(1024)}, u32[]{:S(2)}) copy-start(f32[2880]{0:T(1024)} %param.32) | copy-start | bytes 34564
  318.2 6.5 %copy-start.6 = (bf16[512,2880]{1,0:T(8,128)(2,1)S(1)}, bf16[512,2880]{1,0:T(8,128)(2,1)}, u32[]{:S(2)}) copy-start(bf16[512,2880]{1,0:T(8,128)(2,1)} %all-gather.4.cloned.1.call-done) | copy-start | bytes 8847364
  318.2 6.5 %copy-start.7 = (bf16[512,2880]{1,0:T(8,128)(2,1)S(1)}, bf16[512,2880]{1,0:T(8,128)(2,1)}, u32[]{:S(2)}) copy-start(bf16[512,2880]{1,0:T(8,128)(2,1)} %all-gather.6.cloned.1.call-done) | copy-start | bytes 8847364
  326.1 4.1 copy-start.10
  330.2 1.1 copy-start.20
  335.0 81.9 %copy-start.1 = (bf16[8,48,2880]{2,1,0:T(8,128)(2,1)S(1)}, bf16[8,48,2880]{2,1,0:T(8,128)(2,1)}, u32[]{:S(2)}) copy-start(bf16[8,48,2880]{2,1,0:T(8,128)(2,1)} %param.27) | copy-start | bytes 6635524
  344.9 70.4 %reduce-scatter.11.cloned.1.call-start = ((), (), s32[]{:S(2)}) async-start(), calls=%async_computation.14 | async-start | bytes 471040 | tf_op jit(solution)/shard_map/reduce_scatter | solution.py:115
Sparse Core Ops, SparseCore 0:
  21.3 51.2 all-gather.3
  192.7 41.9 reduce-scatter.4
  237.3 23.0 reduce-scatter.6
  274.4 43.8 all-gather.5
  345.0 44.8 reduce-scatter.8
  392.3 22.9 reduce-scatter.10
